TPU v7x, 256 devices: a whole 4x4x8 slice. The times are simulated.
256 devices in a mesh: section: 16 (over x, z_hi), dp: 16 (over z_lo, y, core).
Axes of the slice: x: 4, y: 4, z: 8 (z_hi: 4, z_lo: 2; z = z_hi * 2 + z_lo), core: 2. Of those that a mesh axis runs over, the one named last changes fastest.
Arguments:
- section_inputs: bfloat16 [16, 768, 1152], P('section'), may hold values from -6 to 6
- mirror_held: bfloat16 [16, 768, 1152], P('section'), may hold values from -6 to 6
- section_cotangents: bfloat16 [16, 768, 1152], P('section'), may hold values from -6 to 6
- next_batch: bfloat16 [768, 1152], replicated, may hold values from -6 to 6
- loss_cotangent: bfloat16 [768, 1152], replicated, may hold values from -6 to 6
- join_weights: bfloat16 [16, 1152, 1152], P('section'), may hold values from -0.125 to 0.125
Outputs:
- section_outputs: bfloat16 [256, 2, 768, 1152], P(('dp', 'section')), parts along dimension 0
- section_gradients: bfloat16 [256, 2, 768, 1152], P(('dp', 'section')), parts along dimension 0
- mirror_arrivals: bfloat16 [256, 768, 1152], P(('dp', 'section')), parts along dimension 0
There are 16 independent parts, one for each index of `dp`. A program takes and returns all parts, laid end to end along the dimension named above; an argument that names none is the same for every part. Nothing has to cross between parts.
All inputs are finite; a program needn't handle non-finite values.
Results may differ from a plain program's by a relative error of at most 0.001.
Values may be sent and summed in bfloat16 or wider, within the bound.
No kernel may reach another device: no remote copies, remote signals or barrier semaphores. Data moves between devices by JAX's collectives and lax.ppermute only.
A program may use at most 128 MiB of HBM per device.

v0:
```python
import jax
import jax.numpy as jnp
from jax import lax
from jax.sharding import PartitionSpec as P


def from_partner(value, axis, bit):
    mask = 2**bit
    pairs = [(source, source ^ mask) for source in range(lax.axis_size(axis))]
    return lax.ppermute(value, axis, pairs)


def shifted(shard, axis, by):
    size = lax.axis_size(axis)
    pairs = [(i, i + by) for i in range(size) if 0 <= i + by < size]
    return lax.ppermute(shard, axis, pairs)


def to_mirror(payload):
    return from_partner(payload, "section", 0)


def pass_middle(payload, first_out, first_grad):
    return from_partner((payload, first_out, first_grad), "section", 0)


def local(
    section_inputs, mirror_held, section_cotangents, next_batch, loss_cotangent, join_weights
):
    count = lax.axis_size("section")
    position = lax.axis_index("section")
    is_early = position % 2 == 0
    weights = join_weights[0]

    def forward(arriving, pending):
        product = jnp.dot(arriving, weights, preferred_element_type=jnp.float32)
        joined = (product + pending.astype(jnp.float32)).astype(jnp.bfloat16)
        leaving = jnp.where(is_early, arriving, joined)
        return (leaving, product.astype(jnp.bfloat16))

    def backward(cotangent, returned):
        operand = jnp.where(is_early, returned, cotangent)
        product = lax.dot_general(
            operand, weights, (((1,), (1,)), ((), ())), preferred_element_type=jnp.float32
        )
        return jnp.where(is_early, cotangent.astype(jnp.float32) + product, product).astype(
            jnp.bfloat16
        )

    held = mirror_held[0]
    first_cot = section_cotangents[0]
    first_out, projected_one = forward(section_inputs[0], held)
    skips_one = to_mirror(projected_one)
    first_grad = backward(first_cot, held)
    returns_one, across_out, across_grad = pass_middle(first_cot, first_out, first_grad)
    from_below = shifted((first_out, first_grad), "section", 2)
    from_above = shifted((first_out, first_grad), "section", -2)
    late_in = jnp.where(position == count - 1, across_out, from_above[0])
    second_in = jnp.where(position == 0, next_batch, jnp.where(is_early, from_below[0], late_in))
    second_out, projected_two = forward(second_in, skips_one)
    early_cot = jnp.where(position == count - 2, across_grad, from_above[1])
    second_cot = jnp.where(
        position == 1, loss_cotangent, jnp.where(is_early, early_cot, from_below[1])
    )
    second_grad = backward(second_cot, returns_one)
    skips_two = to_mirror(projected_two)
    returns_two = to_mirror(second_cot)
    arrivals = jnp.where(is_early, returns_two, skips_two)
    section_outputs = jnp.stack([first_out, second_out], axis=0)[None]
    section_gradients = jnp.stack([first_grad, second_grad], axis=0)[None]
    return (section_outputs, section_gradients, arrivals[None])


def solution(mesh):
    in_specs = (
        P("section", None, None),
        P("section", None, None),
        P("section", None, None),
        P(),
        P(),
        P("section", None, None),
    )
    out_specs = (
        P(("dp", "section"), None, None, None),
        P(("dp", "section"), None, None, None),
        P(("dp", "section"), None, None),
    )
    return jax.shard_map(local, mesh=mesh, in_specs=in_specs, out_specs=out_specs, check_vma=False)
```

profile of v0, /device:TPU:11, one launch (start us, length us, event | category | flops | bytes accessed | tf_op | source)
XLA Modules:
  0.0 779.9 jit_solution(4760314473922903541)
XLA Ops:
  0.6 0.0 copy-start
  0.7 1.7 copy-done
  2.4 0.0 copy-start.2
  2.4 0.0 copy-start.3
  2.4 6.2 fusion
  8.6 8.8 %collective-permute-start.6 = (bf16[768,1152]{1,0:T(8,128)(2,1)}, bf16[768,1152]{1,0:T(8,128)(2,1)}, u32[]{:S(2)}, u32[]{:S(2)}) collective-permute-start(bf16[768,1152]{1,0:T(8,128)(2,1)} %fusion), channel_id=1, source_target_pairs={{0,32},{16,48},{32,64},{48,80},{64,96},{80,112},{96,128},{112,144}... | collective-permute-start | bytes 5308424 | tf_op jit(solution)/shard_map/ppermute | solution.py:16
  17.4 1.3 collective-permute-start.4
  18.7 3.1 collective-permute-start.5
  21.8 0.0 copy-done.2
  21.8 0.0 copy-done.3
  21.8 4.2 fusion.20
  26.0 6.1 collective-permute-start
  32.1 1.2 collective-permute-start.1
  33.3 34.3 %collective-permute-done.6 = bf16[768,1152]{1,0:T(8,128)(2,1)} collective-permute-done((bf16[768,1152]{1,0:T(8,128)(2,1)}, bf16[768,1152]{1,0:T(8,128)(2,1)}, u32[]{:S(2)}, u32[]{:S(2)}) %collective-permute-start.6) | collective-permute-done | bytes 1769504 | tf_op jit(solution)/shard_map/ppermute | solution.py:16
  67.6 7.7 collective-permute-start.2
  75.3 362.0 %collective-permute-done.4 = bf16[768,1152]{1,0:T(8,128)(2,1)} collective-permute-done((bf16[768,1152]{1,0:T(8,128)(2,1)}, bf16[768,1152]{1,0:T(8,128)(2,1)}, u32[]{:S(2)}, u32[]{:S(2)}) %collective-permute-start.4) | collective-permute-done | bytes 1769504 | tf_op jit(solution)/shard_map/ppermute | solution.py:10
  437.3 0.0 collective-permute-start.3
  437.3 0.0 collective-permute-done.5
  437.3 0.0 copy-start.1
  437.3 2.4 collective-permute-start.7
  439.7 1.8 select_select_fusion
  441.5 0.0 collective-permute-done
  441.5 0.8 collective-permute-start.8
  442.3 146.7 %collective-permute-done.1 = bf16[768,1152]{1,0:T(8,128)(2,1)} collective-permute-done((bf16[768,1152]{1,0:T(8,128)(2,1)}, bf16[768,1152]{1,0:T(8,128)(2,1)}, u32[]{:S(2)}, u32[]{:S(2)}) %collective-permute-start.1) | collective-permute-done | bytes 1769504 | tf_op jit(solution)/shard_map/ppermute | solution.py:10
  589.0 0.0 collective-permute-done.2
  589.0 0.0 copy-done.1
  589.0 2.3 select_select_fusion.1
  591.3 2.7 fusion.27
  594.0 0.3 collective-permute-start.9
  594.3 70.4 %collective-permute-done.3 = bf16[768,1152]{1,0:T(8,128)(2,1)S(1)} collective-permute-done((bf16[768,1152]{1,0:T(8,128)(2,1)}, bf16[768,1152]{1,0:T(8,128)(2,1)S(1)}, u32[]{:S(2)}, u32[]{:S(2)}) %collective-permute-start.3) | collective-permute-done | bytes 1769504 | tf_op jit(solution)/shard_map/ppermute | solution.py:10
  664.7 0.6 fusion.19
  665.3 3.6 maximum_bitcast_fusion
  668.9 33.7 %collective-permute-done.7 = bf16[768,1152]{1,0:T(8,128)(2,1)S(1)} collective-permute-done((bf16[768,1152]{1,0:T(8,128)(2,1)}, bf16[768,1152]{1,0:T(8,128)(2,1)S(1)}, u32[]{:S(2)}, u32[]{:S(2)}) %collective-permute-start.7) | collective-permute-done | bytes 1769504 | tf_op jit(solution)/shard_map/ppermute | solution.py:10
  702.6 2.8 fusion.15
  705.5 3.6 maximum_bitcast_fusion.1
  709.1 31.4 %collective-permute-done.8 = bf16[768,1152]{1,0:T(8,128)(2,1)S(1)} collective-permute-done((bf16[768,1152]{1,0:T(8,128)(2,1)S(1)}, bf16[768,1152]{1,0:T(8,128)(2,1)S(1)}, u32[]{:S(2)}, u32[]{:S(2)}) %collective-permute-start.8) | collective-permute-done | bytes 1769504 | tf_op jit(solution)/shard_map/ppermute | solution.py:10
  740.5 37.9 %collective-permute-done.9 = bf16[768,1152]{1,0:T(8,128)(2,1)S(1)} collective-permute-done((bf16[768,1152]{1,0:T(8,128)(2,1)S(1)}, bf16[768,1152]{1,0:T(8,128)(2,1)S(1)}, u32[]{:S(2)}, u32[]{:S(2)}) %collective-permute-start.9) | collective-permute-done | bytes 1769504 | tf_op jit(solution)/shard_map/ppermute | solution.py:10
  778.5 1.4 select_bitcast_fusion
Async XLA Ops:
  0.6 1.8 copy-start
  2.4 19.4 %copy-start.2 = (bf16[1,768,1152]{2,1,0:T(8,128)(2,1)S(1)}, bf16[1,768,1152]{2,1,0:T(8,128)(2,1)}, u32[]{:S(2)}) copy-start(bf16[1,768,1152]{2,1,0:T(8,128)(2,1)} %param.7) | copy-start | bytes 5308420
  2.4 19.4 %copy-start.3 = (bf16[1,768,1152]{2,1,0:T(8,128)(2,1)S(1)}, bf16[1,768,1152]{2,1,0:T(8,128)(2,1)}, u32[]{:S(2)}) copy-start(bf16[1,768,1152]{2,1,0:T(8,128)(2,1)} %param.6) | copy-start | bytes 5308420
  8.6 59.0 %collective-permute-start.6 = (bf16[768,1152]{1,0:T(8,128)(2,1)}, bf16[768,1152]{1,0:T(8,128)(2,1)}, u32[]{:S(2)}, u32[]{:S(2)}) collective-permute-start(bf16[768,1152]{1,0:T(8,128)(2,1)} %fusion), channel_id=1, source_target_pairs={{0,32},{16,48},{32,64},{48,80},{64,96},{80,112},{96,128},{112,144}... | collective-permute-start | bytes 5308424 | tf_op jit(solution)/shard_map/ppermute | solution.py:16
  17.4 419.9 %collective-permute-start.4 = (bf16[768,1152]{1,0:T(8,128)(2,1)}, bf16[768,1152]{1,0:T(8,128)(2,1)}, u32[]{:S(2)}, u32[]{:S(2)}) collective-permute-start(bf16[768,1152]{1,0:T(8,128)(2,1)} %fusion), channel_id=1, source_target_pairs={{0,16},{16,0},{32,48},{48,32},{64,80},{80,64},{96,112},{112,96},{1... | collective-permute-start | bytes 5308424 | tf_op jit(solution)/shard_map/ppermute | solution.py:10
  18.7 418.6 %collective-permute-start.5 = (bf16[768,1152]{1,0:T(8,128)(2,1)}, bf16[768,1152]{1,0:T(8,128)(2,1)}, u32[]{:S(2)}, u32[]{:S(2)}) collective-permute-start(bf16[768,1152]{1,0:T(8,128)(2,1)} %fusion), channel_id=1, source_target_pairs={{32,0},{48,16},{64,32},{80,48},{96,64},{112,80},{128,96},{144,112}... | collective-permute-start | bytes 5308424 | tf_op jit(solution)/shard_map/ppermute | solution.py:16
  26.0 415.5 %collective-permute-start = (bf16[768,1152]{1,0:T(8,128)(2,1)}, bf16[768,1152]{1,0:T(8,128)(2,1)}, u32[]{:S(2)}, u32[]{:S(2)}) collective-permute-start(bf16[768,1152]{1,0:T(8,128)(2,1)} %get-tuple-element.3), channel_id=1, source_target_pairs={{0,32},{16,48},{32,64},{48,80},{64,96},{80,112},{96,128},{112,144}... | collective-permute-start | bytes 5308424 | tf_op jit(solution)/shard_map/ppermute | solution.py:16
  32.1 556.9 %collective-permute-start.1 = (bf16[768,1152]{1,0:T(8,128)(2,1)}, bf16[768,1152]{1,0:T(8,128)(2,1)}, u32[]{:S(2)}, u32[]{:S(2)}) collective-permute-start(bf16[768,1152]{1,0:T(8,128)(2,1)} %get-tuple-element.3), channel_id=1, source_target_pairs={{0,16},{16,0},{32,48},{48,32},{64,80},{80,64},{96,112},{112,96},{1... | collective-permute-start | bytes 5308424 | tf_op jit(solution)/shard_map/ppermute | solution.py:10
  67.6 521.4 %collective-permute-start.2 = (bf16[768,1152]{1,0:T(8,128)(2,1)}, bf16[768,1152]{1,0:T(8,128)(2,1)}, u32[]{:S(2)}, u32[]{:S(2)}) collective-permute-start(bf16[768,1152]{1,0:T(8,128)(2,1)} %get-tuple-element.3), channel_id=1, source_target_pairs={{32,0},{48,16},{64,32},{80,48},{96,64},{112,80},{128,96},{144,112}... | collective-permute-start | bytes 5308424 | tf_op jit(solution)/shard_map/ppermute | solution.py:16
  437.3 227.4 %collective-permute-start.3 = (bf16[768,1152]{1,0:T(8,128)(2,1)}, bf16[768,1152]{1,0:T(8,128)(2,1)S(1)}, u32[]{:S(2)}, u32[]{:S(2)}) collective-permute-start(bf16[768,1152]{1,0:T(8,128)(2,1)} %get-tuple-element.4), channel_id=1, source_target_pairs={{0,16},{16,0},{32,48},{48,32},{64,80},{80,64},{96,112},{112,96},{1... | collective-permute-start | bytes 5308424 | tf_op jit(solution)/shard_map/ppermute | solution.py:10
  437.3 151.7 %copy-start.1 = (bf16[768,1152]{1,0:T(8,128)(2,1)S(1)}, bf16[768,1152]{1,0:T(8,128)(2,1)}, u32[]{:S(2)}) copy-start(bf16[768,1152]{1,0:T(8,128)(2,1)} %param.9) | copy-start | bytes 5308420
  437.3 265.3 %collective-permute-start.7 = (bf16[768,1152]{1,0:T(8,128)(2,1)}, bf16[768,1152]{1,0:T(8,128)(2,1)S(1)}, u32[]{:S(2)}, u32[]{:S(2)}) collective-permute-start(bf16[768,1152]{1,0:T(8,128)(2,1)} %bitcast.46), channel_id=1, source_target_pairs={{0,16},{16,0},{32,48},{48,32},{64,80},{80,64},{96,112},{112,96},{1... | collective-permute-start | bytes 5308424 | tf_op jit(solution)/shard_map/ppermute | solution.py:10
  441.5 299.1 %collective-permute-start.8 = (bf16[768,1152]{1,0:T(8,128)(2,1)S(1)}, bf16[768,1152]{1,0:T(8,128)(2,1)S(1)}, u32[]{:S(2)}, u32[]{:S(2)}) collective-permute-start(bf16[768,1152]{1,0:T(8,128)(2,1)S(1)} %select_select_fusion), channel_id=1, source_target_pairs={{0,16},{16,0},{32,48},{48,32},{64,80},{80,64},{96,112},{112,96},{1... | collective-permute-start | bytes 5308424 | tf_op jit(solution)/shard_map/ppermute | solution.py:10
  594.0 184.4 %collective-permute-start.9 = (bf16[768,1152]{1,0:T(8,128)(2,1)S(1)}, bf16[768,1152]{1,0:T(8,128)(2,1)S(1)}, u32[]{:S(2)}, u32[]{:S(2)}) collective-permute-start(bf16[768,1152]{1,0:T(8,128)(2,1)S(1)} %get-tuple-element.5), channel_id=1, source_target_pairs={{0,16},{16,0},{32,48},{48,32},{64,80},{80,64},{96,112},{112,96},{1... | collective-permute-start | bytes 5308424 | tf_op jit(solution)/shard_map/ppermute | solution.py:10
where the time goes:
time: 780 us
  waiting for transfers between devices  716 us (92%)
  starting transfers between devices  31.7 us (4%)
  matrix products  15.9 us (2%)
  other arithmetic  13.4 us (2%)
    ppermute x6, waiting for transfers between devices, from_partner(): return lax.ppermute(value, axis, pairs)  682 us
    ppermute x4, waiting for transfers between devices, shifted(): return lax.ppermute(shard, axis, pairs)  34.3 us
    ppermute x4, starting transfers between devices, shifted(): return lax.ppermute(shard, axis, pairs)  25.7 us
  transfers between devices with their start and end apart: 10, of which 7 were waited for; matrix products, arithmetic and copies ran while one was open for 3% of the time, Pallas kernels for 0%

commit v1 on v0

v1 whole, which is shorter than its diff:
```python
import jax
import jax.numpy as jnp
from jax import lax
from jax.sharding import PartitionSpec as P


def relay_pairs(count):
    order = list(range(0, count, 2)) + list(range(count - 1, 0, -2))
    return list(zip(order[:-1], order[1:]))


def local(
    section_inputs, mirror_held, section_cotangents, next_batch, loss_cotangent, join_weights
):
    count = lax.axis_size("section")
    replicas = lax.axis_size("dp")
    position = lax.axis_index("section")
    is_early = position % 2 == 0
    weights = join_weights[0]
    rows = next_batch.shape[0] // replicas
    start = lax.axis_index("dp") * rows

    ahead = relay_pairs(count)
    back = [(b, a) for a, b in ahead]
    mirror = [(i, i ^ 1) for i in range(count)]

    def times(left):
        return jnp.dot(left, weights, preferred_element_type=jnp.float32)

    def times_t(left):
        return lax.dot_general(
            left, weights, (((1,), (1,)), ((), ())), preferred_element_type=jnp.float32
        )

    def forward(arriving, pending):
        product = times(arriving)
        joined = (product + pending.astype(jnp.float32)).astype(jnp.bfloat16)
        return jnp.where(is_early, arriving, joined), product.astype(jnp.bfloat16)

    def backward(cotangent, returned):
        product = times_t(jnp.where(is_early, returned, cotangent))
        return jnp.where(is_early, cotangent.astype(jnp.float32) + product, product).astype(
            jnp.bfloat16
        )

    def part(whole):
        return lax.dynamic_slice_in_dim(whole, start, rows, 0)

    a, held, cot = section_inputs[0], mirror_held[0], section_cotangents[0]
    a_part, held_part, cot_part = part(a), part(held), part(cot)
    out_part, skip_part = forward(a_part, held_part)
    grad_part = backward(cot_part, held_part)
    came_out = lax.ppermute(out_part, "section", ahead)
    came_grad = lax.ppermute(grad_part, "section", back)
    came_mirror = lax.ppermute(jnp.where(is_early, skip_part, cot_part), "section", mirror)
    second_in = jnp.where(position == 0, part(next_batch), came_out)
    second_cot = jnp.where(position == 1, part(loss_cotangent), came_grad)
    second_out, second_skip = forward(second_in, came_mirror)
    second_grad = backward(second_cot, came_mirror)
    arrived = lax.ppermute(jnp.where(is_early, second_skip, second_cot), "section", mirror)
    parts = jnp.stack([second_out, second_grad, arrived], axis=0)
    whole = lax.all_gather(parts, "dp", axis=1, tiled=True)

    first_out, _ = forward(a, held)
    first_grad = backward(cot, held)
    section_outputs = jnp.stack([first_out, whole[0]], axis=0)[None]
    section_gradients = jnp.stack([first_grad, whole[1]], axis=0)[None]
    return (section_outputs, section_gradients, whole[2][None])


def solution(mesh):
    in_specs = (
        P("section", None, None),
        P("section", None, None),
        P("section", None, None),
        P(),
        P(),
        P("section", None, None),
    )
    out_specs = (
        P(("dp", "section"), None, None, None),
        P(("dp", "section"), None, None, None),
        P(("dp", "section"), None, None),
    )
    return jax.shard_map(local, mesh=mesh, in_specs=in_specs, out_specs=out_specs, check_vma=False)
```

time: 780 us -> 102 us (0.13)
  the two profiles are of different devices: /device:TPU:11 before, /device:TPU:1 now
where the time goes in v1:
time: 102 us
  waiting for transfers between devices  39.7 us (39%)
  starting transfers between devices  20.6 us (20%)
  matrix products  17.5 us (17%)
  between operations  14.1 us (14%)
  local copies, waits for them, and re-layouts  6.01 us (6%)
  other arithmetic  4.11 us (4%)
    all_gather x1, waiting for transfers between devices, local(): whole = lax.all_gather(parts, 'dp', axis=1, tiled=True)  30.9 us
    dot_general x3, matrix products, times(): return jnp.dot(left, weights, preferred_element_type=jnp.float32)  9.78 us
    ppermute x1, starting transfers between devices, local(): lax.ppermute(jnp.where(is_early, skip_part, cot_part), 'section', mirror)  9.63 us
    dot_general x3, matrix products, times_t(): lax.dot_general(left, weights, (((1,), (1,)), ((), ())), preferred_elemen...  7.76 us
    ppermute x1, starting transfers between devices, local(): lax.ppermute(jnp.where(is_early, second_skip, second_cot), 'section', mir...  6.51 us
    ppermute x1, waiting for transfers between devices, local(): lax.ppermute(jnp.where(is_early, skip_part, cot_part), 'section', mirror)  5.07 us
    slice x1, local copies, waits for them, and re-layouts, local(): return (section_outputs, section_gradients, whole[2][None])  4.3 us
    ppermute x1, waiting for transfers between devices, local(): lax.ppermute(jnp.where(is_early, second_skip, second_cot), 'section', mir...  3.65 us
  transfers between devices with their start and end apart: 5, of which 3 were waited for; matrix products, arithmetic and copies ran while one was open for 14% of the time, Pallas kernels for 0%

profile of v1, /device:TPU:1, one launch (start us, length us, event | category | flops | bytes accessed | tf_op | source)
XLA Modules:
  0.0 102.0 jit_solution(10804402269663658548)
XLA Ops:
  7.2 0.0 copy-start
  7.2 0.0 all-gather.2.cloned.1.call-start
  7.2 1.7 %copy-done = bf16[1,1152,1152]{2,1,0:T(8,128)(2,1)S(1)} copy-done((bf16[1,1152,1152]{2,1,0:T(8,128)(2,1)S(1)}, bf16[1,1152,1152]{2,1,0:T(8,128)(2,1)}, u32[]{:S(2)}) %copy-start) | copy-done | bytes 2654232
  8.9 1.9 %fusion.34 = bf16[48,1152]{1,0:T(8,128)(2,1)S(1)} fusion(bf16[1,1152,1152]{2,1,0:T(8,128)(2,1)S(1)} %copy-done, pred[]{:T(512)S(6)} %eq.11, bf16[1,768,1152]{2,1,0:T(8,128)(2,1)} %param.8, s32[]{:T(128)S(6)} %select_n.97, bf16[1,768,1152]{2,1,0:T(8,128)(2,1)} %param.7), kind=kOutput, calls=%fused_computation.29 | convolution fusion | flops 127678464 | bytes 3098624 | tf_op jit(solution)/shard_map/dot_general | solution.py:31
  10.8 1.3 %collective-permute-start.2 = (bf16[48,1152]{1,0:T(8,128)(2,1)S(1)}, bf16[48,1152]{1,0:T(8,128)(2,1)S(1)}, u32[]{:S(2)}, u32[]{:S(2)}) collective-permute-start(bf16[48,1152]{1,0:T(8,128)(2,1)S(1)} %fusion.34), channel_id=1, source_target_pairs={{32,0},{64,32},{96,64},{128,96},{160,128},{192,160},{224,192},{240... | collective-permute-start | bytes 331784 | tf_op jit(solution)/shard_map/ppermute | solution.py:54
  12.1 1.6 %bitcast_select_fusion = (bf16[48,1152]{1,0:T(8,128)(2,1)S(1)}, bf16[48,1152]{1,0:T(8,128)(2,1)S(1)}) fusion(pred[]{:T(512)S(6)} %eq.11, bf16[1,768,1152]{2,1,0:T(8,128)(2,1)} %param.8, s32[]{:T(128)S(6)} %select_n.97, bf16[1,768,1152]{2,1,0:T(8,128)(2,1)} %param.7, bf16[1,768,1152]{2,1,0:T(8,128)(2,1)} %param.6, bf16[1,1152,1152]{2,1,0:T(8,128)(2,1)S(1)} %copy-done), kind=kOutput, calls=%fused_computation.37 | convolution fusion | flops 127733760 | bytes 3319296 | tf_op jit(solution)/shard_map/dot_general | solution.py:28
  13.8 9.6 %collective-permute-start.1 = (bf16[48,1152]{1,0:T(8,128)(2,1)S(1)}, bf16[48,1152]{1,0:T(8,128)(2,1)S(1)}, u32[]{:S(2)}, u32[]{:S(2)}) collective-permute-start(bf16[48,1152]{1,0:T(8,128)(2,1)S(1)} %get-tuple-element.8), channel_id=1, source_target_pairs={{0,16},{16,0},{32,48},{48,32},{64,80},{80,64},{96,112},{112,96},{1... | collective-permute-start | bytes 331784 | tf_op jit(solution)/shard_map/ppermute | solution.py:55
  23.4 3.1 %collective-permute-start = (bf16[48,1152]{1,0:T(8,128)(2,1)S(1)}, bf16[48,1152]{1,0:T(8,128)(2,1)S(1)}, u32[]{:S(2)}, u32[]{:S(2)}) collective-permute-start(bf16[48,1152]{1,0:T(8,128)(2,1)S(1)} %get-tuple-element.9), channel_id=1, source_target_pairs={{0,32},{32,64},{64,96},{96,128},{128,160},{160,192},{192,224},{224... | collective-permute-start | bytes 331784 | tf_op jit(solution)/shard_map/ppermute | solution.py:53
  26.5 0.0 collective-permute-done.2
  26.5 5.1 %collective-permute-done.1 = bf16[48,1152]{1,0:T(8,128)(2,1)S(1)} collective-permute-done((bf16[48,1152]{1,0:T(8,128)(2,1)S(1)}, bf16[48,1152]{1,0:T(8,128)(2,1)S(1)}, u32[]{:S(2)}, u32[]{:S(2)}) %collective-permute-start.1) | collective-permute-done | bytes 110624 | tf_op jit(solution)/shard_map/ppermute | solution.py:55
  31.6 0.0 collective-permute-done
  31.6 1.6 %fusion.39 = (bf16[1,48,1152]{2,1,0:T(8,128)(2,1)S(1)}, bf16[48,1152]{1,0:T(8,128)(2,1)S(1)}) fusion(bf16[48,1152]{1,0:T(8,128)(2,1)S(1)} %collective-permute-done.1, pred[]{:T(512)S(6)} %eq.11, bf16[48,1152]{1,0:T(8,128)(2,1)S(1)} %collective-permute-done, bf16[768,1152]{1,0:T(8,128)(2,1)} %param.9, s32[]{:T(128)S(6)} %select_n.97, pred[]{:T(512)S(6)} %eq.12, ...), kind=kOutput, calls=%fused_computation.34 | convolution fusion | flops 127899648 | bytes 3652608 | tf_op jit(solution)/shard_map/dot_general | solution.py:28
  33.2 6.5 %collective-permute-start.3 = (bf16[48,1152]{1,0:T(8,128)(2,1)S(1)}, bf16[48,1152]{1,0:T(8,128)(2,1)S(1)}, u32[]{:S(2)}, u32[]{:S(2)}) collective-permute-start(bf16[48,1152]{1,0:T(8,128)(2,1)S(1)} %get-tuple-element.7), channel_id=1, source_target_pairs={{0,16},{16,0},{32,48},{48,32},{64,80},{80,64},{96,112},{112,96},{1... | collective-permute-start | bytes 331784 | tf_op jit(solution)/shard_map/ppermute | solution.py:60
  39.7 1.9 %fusion.29 = bf16[1,48,1152]{2,1,0:T(8,128)(2,1)S(1)} fusion(bf16[1,1152,1152]{2,1,0:T(8,128)(2,1)S(1)} %copy-done, bf16[48,1152]{1,0:T(8,128)(2,1)S(1)} %collective-permute-done.1, pred[]{:T(512)S(6)} %eq.11, bf16[48,1152]{1,0:T(8,128)(2,1)S(1)} %collective-permute-done.2, bf16[768,1152]{1,0:T(8,128)(2,1)} %param.10, s32[]{:T(128)S(6)} %select_n.97, ...), kind=kOutput, calls=%fused_computation.27 | convolution fusion | flops 127789056 | bytes 3320832 | tf_op jit(solution)/shard_map/dot_general | solution.py:31
  41.6 3.7 %collective-permute-done.3 = bf16[48,1152]{1,0:T(8,128)(2,1)S(1)} collective-permute-done((bf16[48,1152]{1,0:T(8,128)(2,1)S(1)}, bf16[48,1152]{1,0:T(8,128)(2,1)S(1)}, u32[]{:S(2)}, u32[]{:S(2)}) %collective-permute-start.3) | collective-permute-done | bytes 110624 | tf_op jit(solution)/shard_map/ppermute | solution.py:60
  45.2 0.8 pad_maximum_fusion
  46.0 0.0 all-gather.2.cloned.1.call-update
  46.0 0.0 copy-start.3
  46.0 0.0 copy-start.4
  46.0 6.6 %fusion.3 = bf16[1,768,1152]{2,1,0:T(8,128)(2,1)} fusion(bf16[1,1152,1152]{2,1,0:T(8,128)(2,1)S(1)} %copy-done, bf16[1,768,1152]{2,1,0:T(8,128)(2,1)} %param.7, bf16[1,768,1152]{2,1,0:T(8,128)(2,1)} %param.6, pred[]{:T(512)S(6)} %eq.11), kind=kOutput, calls=%fused_computation.7 | convolution fusion | flops 2041970688 | bytes 7962625 | tf_op jit(solution)/shard_map/dot_general | solution.py:28
  52.6 0.0 copy-done.3
  52.6 0.0 copy-done.4
  52.6 4.0 %fusion.17 = bf16[1,768,1152]{2,1,0:T(8,128)(2,1)} fusion(bf16[1,1152,1152]{2,1,0:T(8,128)(2,1)S(1)} %copy-done, bf16[1,768,1152]{2,1,0:T(8,128)(2,1)S(1)} %copy-done.3, bf16[1,768,1152]{2,1,0:T(8,128)(2,1)S(1)} %copy-done.4, pred[]{:T(512)S(6)} %eq.11), kind=kOutput, calls=%fused_computation.19 | convolution fusion | flops 2042855424 | bytes 7962625 | tf_op jit(solution)/shard_map/dot_general | solution.py:31
  56.6 30.9 %all-gather.2.cloned.1.call-done = bf16[3,768,1152]{2,1,0:T(8,128)(2,1)} async-done(((bf16[3,48,1152]{2,1,0:T(8,128)(2,1)}), bf16[3,768,1152]{2,1,0:T(8,128)(2,1)}) %all-gather.2.cloned.1.call-update) | async-done | bytes 5308432 | tf_op jit(solution)/shard_map/all_gather | solution.py:62
  87.5 0.0 copy-start.1
  87.5 0.0 copy-start.2
  87.5 4.3 %fusion.54 = (bf16[1,768,1152]{2,1,0:T(8,128)(2,1)}, bf16[1,768,1152]{2,1,0:T(8,128)(2,1)S(1)}, bf16[1,768,1152]{2,1,0:T(8,128)(2,1)S(1)}) fusion(bf16[3,768,1152]{2,1,0:T(8,128)(2,1)} %all-gather.2.cloned.1.call-done), kind=kLoop, calls=%fused_computation.53 | loop fusion | bytes 10616832 | tf_op jit(solution)/shard_map/slice | solution.py:68
  91.8 0.0 copy-done.1
  91.8 0.0 copy-done.2
  91.8 3.3 %maximum_bitcast_fusion = (bf16[1,2,768,1152]{3,2,1,0:T(8,128)(2,1)}, bf16[1,2,768,1152]{3,2,1,0:T(8,128)(2,1)}) fusion(bf16[1,768,1152]{2,1,0:T(8,128)(2,1)S(1)} %get-tuple-element.5, bf16[1,768,1152]{2,1,0:T(8,128)(2,1)S(1)} %copy-done.1, bf16[1,768,1152]{2,1,0:T(8,128)(2,1)S(1)} %get-tuple-element.4, bf16[1,768,1152]{2,1,0:T(8,128)(2,1)S(1)} %copy-done.2), kind=kLoop, calls=%fused_computation.3 | loop fusion | flops 3538944 | bytes 14155776 | tf_op jit(solution)/shard_map/broadcast_in_dim | solution.py:66
Async XLA Ops:
  7.2 1.8 %copy-start = (bf16[1,1152,1152]{2,1,0:T(8,128)(2,1)S(1)}, bf16[1,1152,1152]{2,1,0:T(8,128)(2,1)}, u32[]{:S(2)}) copy-start(bf16[1,1152,1152]{2,1,0:T(8,128)(2,1)} %param.11) | copy-start | bytes 7962628
  7.2 80.3 %all-gather.2.cloned.1.call-start = ((), (), s32[]{:S(2)}) async-start(), calls=%async_computation | async-start | bytes 5640192 | tf_op jit(solution)/shard_map/all_gather | solution.py:62
  10.8 15.7 %collective-permute-start.2 = (bf16[48,1152]{1,0:T(8,128)(2,1)S(1)}, bf16[48,1152]{1,0:T(8,128)(2,1)S(1)}, u32[]{:S(2)}, u32[]{:S(2)}) collective-permute-start(bf16[48,1152]{1,0:T(8,128)(2,1)S(1)} %fusion.34), channel_id=1, source_target_pairs={{32,0},{64,32},{96,64},{128,96},{160,128},{192,160},{224,192},{240... | collective-permute-start | bytes 331784 | tf_op jit(solution)/shard_map/ppermute | solution.py:54
  13.8 17.8 %collective-permute-start.1 = (bf16[48,1152]{1,0:T(8,128)(2,1)S(1)}, bf16[48,1152]{1,0:T(8,128)(2,1)S(1)}, u32[]{:S(2)}, u32[]{:S(2)}) collective-permute-start(bf16[48,1152]{1,0:T(8,128)(2,1)S(1)} %get-tuple-element.8), channel_id=1, source_target_pairs={{0,16},{16,0},{32,48},{48,32},{64,80},{80,64},{96,112},{112,96},{1... | collective-permute-start | bytes 331784 | tf_op jit(solution)/shard_map/ppermute | solution.py:55
  23.4 8.2 %collective-permute-start = (bf16[48,1152]{1,0:T(8,128)(2,1)S(1)}, bf16[48,1152]{1,0:T(8,128)(2,1)S(1)}, u32[]{:S(2)}, u32[]{:S(2)}) collective-permute-start(bf16[48,1152]{1,0:T(8,128)(2,1)S(1)} %get-tuple-element.9), channel_id=1, source_target_pairs={{0,32},{32,64},{64,96},{96,128},{128,160},{160,192},{192,224},{224... | collective-permute-start | bytes 331784 | tf_op jit(solution)/shard_map/ppermute | solution.py:53
  33.2 12.1 %collective-permute-start.3 = (bf16[48,1152]{1,0:T(8,128)(2,1)S(1)}, bf16[48,1152]{1,0:T(8,128)(2,1)S(1)}, u32[]{:S(2)}, u32[]{:S(2)}) collective-permute-start(bf16[48,1152]{1,0:T(8,128)(2,1)S(1)} %get-tuple-element.7), channel_id=1, source_target_pairs={{0,16},{16,0},{32,48},{48,32},{64,80},{80,64},{96,112},{112,96},{1... | collective-permute-start | bytes 331784 | tf_op jit(solution)/shard_map/ppermute | solution.py:60
  46.0 6.6 %copy-start.3 = (bf16[1,768,1152]{2,1,0:T(8,128)(2,1)S(1)}, bf16[1,768,1152]{2,1,0:T(8,128)(2,1)}, u32[]{:S(2)}) copy-start(bf16[1,768,1152]{2,1,0:T(8,128)(2,1)} %param.8) | copy-start | bytes 5308420
  46.0 6.6 %copy-start.4 = (bf16[1,768,1152]{2,1,0:T(8,128)(2,1)S(1)}, bf16[1,768,1152]{2,1,0:T(8,128)(2,1)}, u32[]{:S(2)}) copy-start(bf16[1,768,1152]{2,1,0:T(8,128)(2,1)} %param.7) | copy-start | bytes 5308420
  87.5 4.3 %copy-start.1 = (bf16[1,768,1152]{2,1,0:T(8,128)(2,1)S(1)}, bf16[1,768,1152]{2,1,0:T(8,128)(2,1)}, u32[]{:S(2)}) copy-start(bf16[1,768,1152]{2,1,0:T(8,128)(2,1)} %fusion.3) | copy-start | bytes 5308420
  87.5 4.3 %copy-start.2 = (bf16[1,768,1152]{2,1,0:T(8,128)(2,1)S(1)}, bf16[1,768,1152]{2,1,0:T(8,128)(2,1)}, u32[]{:S(2)}) copy-start(bf16[1,768,1152]{2,1,0:T(8,128)(2,1)} %fusion.17) | copy-start | bytes 5308420
Sparse Core Ops, SparseCore 0:
  46.1 41.3 all-gather.1

commit v2 on v1

v2 whole, which is shorter than its diff:
```python
import functools

import jax
import jax.numpy as jnp
from jax import lax
from jax.experimental import pallas as pl
from jax.experimental.pallas import tpu as pltpu
from jax.sharding import PartitionSpec as P

AXES = ("section", "dp")
BF16 = jnp.bfloat16
F32 = jnp.float32
CORE, Y_NEAR, Y_FAR, Z = 1, 2, 6, 8


def next_slot(count):
    order = list(range(0, count, 2)) + list(range(count - 1, 0, -2))
    return dict(zip(order[:-1], order[1:]))


def times(left, weights):
    return jnp.dot(left, weights, preferred_element_type=F32)


def times_t(left, weights):
    return lax.dot_general(left, weights, (((1,), (1,)), ((), ())), preferred_element_type=F32)


def first_kernel(early_ref, a_ref, h_ref, g_ref, w_ref, out_ref, grad_ref):
    early = early_ref[0] == 1

    @pl.when(early)
    def _():
        out_ref[0, 0] = a_ref[0]
        product = times_t(h_ref[0], w_ref[0])
        grad_ref[0, 0] = (g_ref[0].astype(F32) + product).astype(BF16)

    @pl.when(jnp.logical_not(early))
    def _():
        product = times(a_ref[0], w_ref[0])
        out_ref[0, 0] = (product + h_ref[0].astype(F32)).astype(BF16)
        grad_ref[0, 0] = times_t(g_ref[0], w_ref[0]).astype(BF16)


def first_tick(early, a, held, cot, weights):
    _, height, width = a.shape
    block = height // 4
    rows = pl.BlockSpec((1, block, width), lambda i: (0, i, 0))
    wide = pl.BlockSpec((1, 1, block, width), lambda i: (0, 0, i, 0))
    both = jax.ShapeDtypeStruct((1, 2, height, width), BF16)
    return pl.pallas_call(
        first_kernel,
        grid=(4,),
        in_specs=[
            pl.BlockSpec(memory_space=pltpu.SMEM),
            rows,
            rows,
            rows,
            pl.BlockSpec((1, width, width), lambda i: (0, 0, 0)),
        ],
        out_specs=[wide, wide],
        out_shape=[both, both],
        cost_estimate=pl.CostEstimate(
            flops=4 * height * width * width, bytes_accessed=14 * height * width, transcendentals=0
        ),
        name="first_tick",
    )(early, a, held, cot, weights)


def place_kernel(masks, rows, replica_ref, *refs):
    pieces = [refs[4 * k : 4 * k + 4] for k in range(3)]
    out_ref, grad_ref, arrived_ref, sem = refs[14:]
    replica = replica_ref[0]
    copies = []
    for target, four, owners in zip((out_ref.at[0, 1], grad_ref.at[0, 1], arrived_ref.at[0]), pieces, masks):
        for piece, owned in zip(four, owners):
            for k, mask in enumerate(owned):
                at = pl.multiple_of((replica ^ mask) * rows, rows)
                copies.append(
                    pltpu.make_async_copy(
                        piece.at[pl.ds(k * rows, rows)],
                        target.at[pl.ds(at, rows)],
                        sem.at[len(copies)],
                    )
                )
    for copy in copies:
        copy.start()
    for copy in copies:
        copy.wait()


def place(replica, pieces, masks, outs, grads, rows):
    anywhere = pl.BlockSpec(memory_space=pl.ANY)
    flat = [piece for four in pieces for piece in four]
    return pl.pallas_call(
        functools.partial(place_kernel, masks, rows),
        in_specs=[pl.BlockSpec(memory_space=pltpu.SMEM)]
        + [pl.BlockSpec(memory_space=pltpu.VMEM)] * 12
        + [anywhere] * 2,
        out_specs=[anywhere] * 3,
        out_shape=[
            jax.ShapeDtypeStruct(outs.shape, BF16),
            jax.ShapeDtypeStruct(grads.shape, BF16),
            jax.ShapeDtypeStruct((1,) + outs.shape[2:], BF16),
        ],
        scratch_shapes=[pltpu.SemaphoreType.DMA((48,))],
        input_output_aliases={13: 0, 14: 1},
        name="place",
    )(replica, *flat, outs, grads)


def local(
    section_inputs, mirror_held, section_cotangents, next_batch, loss_cotangent, join_weights
):
    count = lax.axis_size("section")
    replicas = lax.axis_size("dp")
    position = lax.axis_index("section")
    replica = lax.axis_index("dp")
    is_early = position % 2 == 0
    weights = join_weights[0]
    rows = next_batch.shape[0] // replicas

    def pairs(slots, flip):
        return [
            (s * replicas + d, t * replicas + (d ^ flip))
            for s, t in slots
            for d in range(replicas)
        ]

    def send(value, *moves):
        return lax.ppermute(value, AXES, sum((pairs(slots, flip) for slots, flip in moves), []))

    def part(whole, of):
        return lax.dynamic_slice_in_dim(whole, of * rows, rows, 0)

    after = next_slot(count)
    early = range(0, count, 2)
    late = range(1, count, 2)
    a_ahead = [(s, after[s]) for s in early]
    out_ahead = [(s, after[s]) for s in late if s in after]
    grad_back = [(t, s) for s, t in after.items()]
    to_late = [(s, s + 1) for s in early]
    to_early = [(s, s - 1) for s in late]
    grad_across = [(s, s + 1) for s in late if s + 1 < count]

    sent = replica ^ Z
    a, held, cot = section_inputs[0], mirror_held[0], section_cotangents[0]
    a_part, held_part, cot_part = part(a, sent), part(held, sent), part(cot, sent)
    came_in = send(a_part, (a_ahead, Z))
    product = times(a_part, weights)
    came_mirror = send(
        jnp.where(is_early, product.astype(BF16), cot_part), (to_late, Z), (to_early, Z)
    )
    late_out = (product + held_part.astype(F32)).astype(BF16)
    product = times_t(jnp.where(is_early, held_part, cot_part), weights)
    grad = jnp.where(is_early, cot_part.astype(F32) + product, product).astype(BF16)
    early_back = [(s, t) for s, t in grad_back if s % 2 == 0]
    late_back = [(s, t) for s, t in grad_back if s % 2 == 1]
    came_low = send(jnp.where(is_early, grad, late_out), (early_back, Z), (out_ahead, Z))
    came_high = send(grad, (late_back, Z))

    early_in = jnp.where(position == 0, part(next_batch, replica), came_in)
    skip = times(early_in, weights).astype(BF16)
    came_across = send(jnp.where(is_early, skip, grad), (to_late, 0), (grad_across, Z))
    loss_part = part(loss_cotangent, replica)
    arrived = jnp.where(position == 0, loss_part, came_across)
    late_in = jnp.where(position == count - 1, came_in, came_low)
    late_out = (times(late_in, weights) + came_mirror.astype(F32)).astype(BF16)
    second_out = jnp.where(is_early, early_in, late_out)
    early_cot = jnp.where(position == count - 2, came_high, came_low)
    second_cot = jnp.where(is_early, early_cot, jnp.where(position == 1, loss_part, came_high))
    product = times_t(jnp.where(is_early, came_mirror, second_cot), weights)
    second_grad = jnp.where(is_early, second_cot.astype(F32) + product, product).astype(BF16)

    everyone = [(s, s) for s in range(count)]
    orders = ((Y_NEAR, Y_FAR, Z), (Y_FAR, Z, Y_NEAR), (Z, Y_NEAR, Y_FAR))
    held_rows = [second_out, second_grad, arrived]
    masks = [[0], [0], [0]]
    for step in range(2):
        came = [send(x, (everyone, order[step])) for x, order in zip(held_rows, orders)]
        held_rows = [jnp.concatenate([x, y], axis=0) for x, y in zip(held_rows, came)]
        masks = [m + [k ^ order[step] for k in m] for m, order in zip(masks, orders)]
    last = [send(x, (everyone, order[2])) for x, order in zip(held_rows, orders)]
    last_masks = [[k ^ order[2] for k in m] for m, order in zip(masks, orders)]
    pieces, owners = [], []
    for x, y, m, n in zip(held_rows, last, masks, last_masks):
        pieces.append([x, y, send(x, (everyone, CORE)), send(y, (everyone, CORE))])
        owners.append([m, n, [k ^ CORE for k in m], [k ^ CORE for k in n]])

    outs, grads = first_tick(
        jnp.reshape(is_early.astype(jnp.int32), (1,)),
        section_inputs,
        mirror_held,
        section_cotangents,
        join_weights,
    )
    return tuple(place(jnp.reshape(replica, (1,)), pieces, owners, outs, grads, rows))


def solution(mesh):
    in_specs = (
        P("section", None, None),
        P("section", None, None),
        P("section", None, None),
        P(),
        P(),
        P("section", None, None),
    )
    out_specs = (
        P(("dp", "section"), None, None, None),
        P(("dp", "section"), None, None, None),
        P(("dp", "section"), None, None),
    )
    return jax.shard_map(local, mesh=mesh, in_specs=in_specs, out_specs=out_specs, check_vma=False)
```

time: 102 us -> 79.1 us (0.78)
  waiting for transfers between devices: 39.7 us -> 14.6 us
  starting transfers between devices: 20.6 us -> 37.5 us
  Pallas kernels: 0 us -> 13.5 us
  between operations: 14.1 us -> 0.98 us
  matrix products: 17.5 us -> 9.09 us
  local copies, waits for them, and re-layouts: 6.01 us -> 1.83 us
  other arithmetic: 4.11 us -> 1.1 us
    all_gather x1 -> x0, waiting for transfers between devices: 30.9 us -> none  [local(): whole = lax.all_gather(parts, 'dp', axis=1, tiled=True)]
    ppermute x4 -> x20, starting transfers between devices: 20.5 us -> 37.5 us  [send(): lax.ppermute(value, AXES, sum((pairs(slots, flip) for slots, flip in move...]
    pallas_call x0 -> x2, Pallas kernels: none -> 13.5 us  [the longest x1 8.29 us: first_tick(): pl.pallas_call(first_kernel, grid=(4,), in_specs=[pl.BlockSpec(memory_spa...]
    ppermute x4 -> x20, waiting for transfers between devices: 8.73 us -> 14.6 us  [send(): lax.ppermute(value, AXES, sum((pairs(slots, flip) for slots, flip in move...]
    dot_general x3, matrix products: 9.78 us -> 5.24 us  [times(): return jnp.dot(left, weights, preferred_element_type=F32)]
    slice x1 -> x0, local copies, waits for them, and re-layouts: 4.3 us -> none  [local(): return (section_outputs, section_gradients, whole[2][None])]
    dot_general x3 -> x2, matrix products: 7.76 us -> 3.85 us  [times_t(): lax.dot_general(left, weights, (((1,), (1,)), ((), ())), preferred_elemen...]
    broadcast_in_dim x1 -> x0, other arithmetic: 3.34 us -> none  [local(): section_outputs = jnp.stack([first_out, whole[0]], axis=0)[None]]
  transfers between devices with their start and end apart: 5 -> 20, of which waited for: 3 -> 4; matrix products, arithmetic and copies ran while one was open for 14% -> 13% of each run, Pallas kernels for 0% -> 11%
where the time goes in v2:
time: 79.1 us; the launch traced here: 78.6 us
  starting transfers between devices  37.5 us (47%)
  waiting for transfers between devices  14.6 us (18%)
  Pallas kernels  13.5 us (17%)
  matrix products  9.09 us (11%)
  local copies, waits for them, and re-layouts  1.83 us (2%)
  other arithmetic  1.1 us (1%)
  between operations  0.98 us (1%)
    ppermute x20, starting transfers between devices, send(): lax.ppermute(value, AXES, sum((pairs(slots, flip) for slots, flip in move...  37.5 us
    ppermute x20, waiting for transfers between devices, send(): lax.ppermute(value, AXES, sum((pairs(slots, flip) for slots, flip in move...  14.6 us
    pallas_call x1, Pallas kernels, first_tick(): pl.pallas_call(first_kernel, grid=(4,), in_specs=[pl.BlockSpec(memory_spa...  8.29 us
    dot_general x3, matrix products, times(): return jnp.dot(left, weights, preferred_element_type=F32)  5.24 us
    pallas_call x1, Pallas kernels, place(): pl.pallas_call(functools.partial(place_kernel, masks, rows), in_specs=[pl...  5.23 us
    dot_general x2, matrix products, times_t(): lax.dot_general(left, weights, (((1,), (1,)), ((), ())), preferred_elemen...  3.85 us
  transfers between devices with their start and end apart: 20, of which 4 were waited for; matrix products, arithmetic and copies ran while one was open for 13% of the time, Pallas kernels for 11%

profile of v2, /device:TPU:1, one launch (start us, length us, event | category | flops | bytes accessed | tf_op | source)
XLA Modules:
  0.0 78.6 jit_solution(4470871371822477907)
XLA Ops:
  0.6 0.0 copy-start
  0.7 1.1 %dynamic-slice_bitcast_fusion = bf16[48,1152]{1,0:T(8,128)(2,1)S(1)} fusion(bf16[1,768,1152]{2,1,0:T(8,128)(2,1)} %a_ref.1, s32[]{:T(128)S(6)} %select_n.95), kind=kLoop, calls=%fused_computation.36 | loop fusion | bytes 221188 | tf_op jit(solution)/shard_map/dynamic_slice | solution.py:134
  1.7 9.2 %collective-permute-start = (bf16[48,1152]{1,0:T(8,128)(2,1)S(1)}, bf16[48,1152]{1,0:T(8,128)(2,1)S(1)}, u32[]{:S(2)}, u32[]{:S(2)}) collective-permute-start(bf16[48,1152]{1,0:T(8,128)(2,1)S(1)} %dynamic-slice_bitcast_fusion), channel_id=1, source_target_pairs={{0,40},{1,41},{2,42},{3,43},{4,44},{5,45},{6,46},{7,47},{8,32},{9,... | collective-permute-start | bytes 331784 | tf_op jit(solution)/shard_map/ppermute | solution.py:131
  10.9 2.3 %fusion.6 = f32[48,1152]{1,0:T(8,128)S(1)} fusion(bf16[48,1152]{1,0:T(8,128)(2,1)S(1)} %dynamic-slice_bitcast_fusion, bf16[1,1152,1152]{2,1,0:T(8,128)(2,1)} %w_ref.1), kind=kOutput, calls=%fused_computation.6 | convolution fusion | flops 127401984 | bytes 2985984 | tf_op jit(solution)/shard_map/dot_general | solution.py:22
  13.3 0.0 copy-done
  13.3 2.0 %fusion.36 = (bf16[48,1152]{1,0:T(8,128)(2,1)S(1)}, bf16[48,1152]{1,0:T(8,128)(2,1)S(1)}, bf16[48,1152]{1,0:T(8,128)(2,1)S(1)}) fusion(f32[48,1152]{1,0:T(8,128)S(1)} %fusion.6, pred[]{:T(512)S(6)} %eq.18, bf16[1,768,1152]{2,1,0:T(8,128)(2,1)} %h_ref.1, s32[]{:T(128)S(6)} %select_n.95, bf16[1,768,1152]{2,1,0:T(8,128)(2,1)} %g_ref.1, ...), kind=kOutput, calls=%fused_computation.27 | convolution fusion | flops 128010240 | bytes 3651584 | tf_op jit(solution)/shard_map/dot_general | solution.py:26
  15.3 1.3 %collective-permute-start.1 = (bf16[48,1152]{1,0:T(8,128)(2,1)S(1)}, bf16[48,1152]{1,0:T(8,128)(2,1)S(1)}, u32[]{:S(2)}, u32[]{:S(2)}) collective-permute-start(bf16[48,1152]{1,0:T(8,128)(2,1)S(1)} %get-tuple-element.7), channel_id=1, source_target_pairs={{32,8},{33,9},{34,10},{35,11},{36,12},{37,13},{38,14},{39,15},{40,... | collective-permute-start | bytes 331784 | tf_op jit(solution)/shard_map/ppermute | solution.py:131
  16.6 0.1 collective-permute-start.2
  16.7 0.7 collective-permute-start.8
  17.3 0.0 collective-permute-done
  17.4 1.5 %fusion.19 = bf16[48,1152]{1,0:T(8,128)(2,1)S(1)} fusion(bf16[48,1152]{1,0:T(8,128)(2,1)S(1)} %get-tuple-element.9, bf16[1,1152,1152]{2,1,0:T(8,128)(2,1)S(1)} %copy-done, pred[]{:T(512)S(6)} %eq.18, bf16[48,1152]{1,0:T(8,128)(2,1)S(1)} %collective-permute-done, bf16[768,1152]{1,0:T(8,128)(2,1)} %param.9, s32[]{:T(128)S(6)} %select_n.94, pred[]{:T(512)S(6)} %eq.19), kind=kOutput, calls=%fused_computation.13 | convolution fusion | flops 127567872 | bytes 3096582 | tf_op jit(solution)/shard_map/dot_general | solution.py:22
  18.8 11.0 %collective-permute-start.14 = (bf16[48,1152]{1,0:T(8,128)(2,1)S(1)}, bf16[48,1152]{1,0:T(8,128)(2,1)S(1)}, u32[]{:S(2)}, u32[]{:S(2)}) collective-permute-start(bf16[48,1152]{1,0:T(8,128)(2,1)S(1)} %fusion.19), channel_id=1, source_target_pairs={{0,16},{1,17},{2,18},{3,19},{4,20},{5,21},{6,22},{7,23},{8,24},{9,... | collective-permute-start | bytes 331784 | tf_op jit(solution)/shard_map/ppermute | solution.py:131
  29.9 0.0 collective-permute-done.1
  29.9 0.0 collective-permute-done.2
  29.9 1.5 %fusion.22 = bf16[48,1152]{1,0:T(8,128)(2,1)S(1)} fusion(bf16[1,1152,1152]{2,1,0:T(8,128)(2,1)S(1)} %copy-done, bf16[48,1152]{1,0:T(8,128)(2,1)S(1)} %collective-permute-done.2, bf16[48,1152]{1,0:T(8,128)(2,1)S(1)} %collective-permute-done, bf16[48,1152]{1,0:T(8,128)(2,1)S(1)} %collective-permute-done.1, pred[]{:T(512)S(6)} %eq.20, pred[]{:T(512)S(6)} %eq.18, ...), kind=kOutput, calls=%fused_computation.14 | convolution fusion | flops 127733760 | bytes 3317767 | tf_op jit(solution)/shard_map/dot_general | solution.py:22
  31.3 1.4 %collective-permute-start.3 = (bf16[48,1152]{1,0:T(8,128)(2,1)S(1)}, bf16[48,1152]{1,0:T(8,128)(2,1)S(1)}, u32[]{:S(2)}, u32[]{:S(2)}) collective-permute-start(bf16[48,1152]{1,0:T(8,128)(2,1)S(1)} %fusion.22), channel_id=1, source_target_pairs={{0,2},{1,3},{2,0},{3,1},{4,6},{5,7},{6,4},{7,5},{8,10},{9,11},{10,... | collective-permute-start | bytes 331784 | tf_op jit(solution)/shard_map/ppermute | solution.py:131
  32.7 0.0 collective-permute-done.8
  32.7 1.9 %fusion.27 = bf16[48,1152]{1,0:T(8,128)(2,1)S(1)} fusion(bf16[1,1152,1152]{2,1,0:T(8,128)(2,1)S(1)} %copy-done, bf16[48,1152]{1,0:T(8,128)(2,1)S(1)} %collective-permute-done.2, bf16[48,1152]{1,0:T(8,128)(2,1)S(1)} %collective-permute-done.8, bf16[48,1152]{1,0:T(8,128)(2,1)S(1)} %collective-permute-done.1, pred[]{:T(512)S(6)} %eq.22, pred[]{:T(512)S(6)} %eq.21, ...), kind=kOutput, calls=%fused_computation.19 | convolution fusion | flops 128010240 | bytes 3543040 | tf_op jit(solution)/shard_map/dot_general | solution.py:26
  34.6 2.0 %collective-permute-start.9 = (bf16[48,1152]{1,0:T(8,128)(2,1)S(1)}, bf16[48,1152]{1,0:T(8,128)(2,1)S(1)}, u32[]{:S(2)}, u32[]{:S(2)}) collective-permute-start(bf16[48,1152]{1,0:T(8,128)(2,1)S(1)} %fusion.27), channel_id=1, source_target_pairs={{0,6},{1,7},{2,4},{3,5},{4,2},{5,3},{6,0},{7,1},{8,14},{9,15},{10,... | collective-permute-start | bytes 331784 | tf_op jit(solution)/shard_map/ppermute | solution.py:131
  36.6 0.0 collective-permute-done.14
  36.6 0.9 %broadcast_select_fusion = bf16[48,1152]{1,0:T(8,128)(2,1)S(1)} fusion(bf16[48,1152]{1,0:T(8,128)(2,1)S(1)} %collective-permute-done.14, pred[]{:T(512)S(6)} %eq.19, bf16[768,1152]{1,0:T(8,128)(2,1)} %param.10, s32[]{:T(128)S(6)} %select_n.94), kind=kLoop, calls=%fused_computation.42 | loop fusion | flops 55296 | bytes 331781 | tf_op jit(solution)/shard_map/jit(_where)/select_n | solution.py:166
  37.5 0.1 collective-permute-start.15
  37.6 0.0 collective-permute-done.3
  37.7 0.9 %collective-permute-start.4 = (bf16[96,1152]{1,0:T(8,128)(2,1)S(1)}, bf16[96,1152]{1,0:T(8,128)(2,1)S(1)}, u32[]{:S(2)}, u32[]{:S(2)}) collective-permute-start(bf16[96,1152]{1,0:T(8,128)(2,1)S(1)} %pad_maximum_fusion.3), channel_id=1, source_target_pairs={{0,6},{1,7},{2,4},{3,5},{4,2},{5,3},{6,0},{7,1},{8,14},{9,15},{10,... | collective-permute-start | bytes 663560 | tf_op jit(solution)/shard_map/ppermute | solution.py:131
  38.5 1.0 %collective-permute-done.9 = bf16[48,1152]{1,0:T(8,128)(2,1)S(1)} collective-permute-done((bf16[48,1152]{1,0:T(8,128)(2,1)S(1)}, bf16[48,1152]{1,0:T(8,128)(2,1)S(1)}, u32[]{:S(2)}, u32[]{:S(2)}) %collective-permute-start.9) | collective-permute-done | bytes 110624 | tf_op jit(solution)/shard_map/ppermute | solution.py:131
  39.5 0.6 collective-permute-start.10
  40.1 1.4 %collective-permute-done.15 = bf16[48,1152]{1,0:T(8,128)(2,1)S(1)} collective-permute-done((bf16[48,1152]{1,0:T(8,128)(2,1)S(1)}, bf16[48,1152]{1,0:T(8,128)(2,1)S(1)}, u32[]{:S(2)}, u32[]{:S(2)}) %collective-permute-start.15) | collective-permute-done | bytes 110624 | tf_op jit(solution)/shard_map/ppermute | solution.py:131
  41.5 0.5 collective-permute-start.16
  42.0 3.9 %collective-permute-done.10 = bf16[96,1152]{1,0:T(8,128)(2,1)S(1)} collective-permute-done((bf16[96,1152]{1,0:T(8,128)(2,1)S(1)}, bf16[96,1152]{1,0:T(8,128)(2,1)S(1)}, u32[]{:S(2)}, u32[]{:S(2)}) %collective-permute-start.10) | collective-permute-done | bytes 221216 | tf_op jit(solution)/shard_map/ppermute | solution.py:131
  45.9 0.0 copy-start.1
  45.9 4.2 %collective-permute-start.12 = (bf16[192,1152]{1,0:T(8,128)(2,1)S(1)}, bf16[192,1152]{1,0:T(8,128)(2,1)S(1)}, u32[]{:S(2)}, u32[]{:S(2)}) collective-permute-start(bf16[192,1152]{1,0:T(8,128)(2,1)S(1)} %pad_maximum_fusion.1.refs_4_), channel_id=1, source_target_pairs={{0,1},{1,0},{2,3},{3,2},{4,5},{5,4},{6,7},{7,6},{8,9},{9,8},{10,11... | collective-permute-start | bytes 1327112 | tf_op jit(solution)/shard_map/ppermute | solution.py:131
  50.1 0.0 collective-permute-start.11
  50.1 0.0 collective-permute-done.4
  50.2 0.0 copy-start.2
  50.2 0.1 collective-permute-start.5
  50.3 0.0 collective-permute-done.16
  50.3 0.0 copy-start.3
  50.4 2.2 %collective-permute-start.17 = (bf16[192,1152]{1,0:T(8,128)(2,1)S(1)}, bf16[192,1152]{1,0:T(8,128)(2,1)S(1)}, u32[]{:S(2)}, u32[]{:S(2)}) collective-permute-start(bf16[192,1152]{1,0:T(8,128)(2,1)S(1)} %pad_maximum_fusion.2.refs_8_), channel_id=1, source_target_pairs={{0,6},{1,7},{2,4},{3,5},{4,2},{5,3},{6,0},{7,1},{8,14},{9,15},{10,... | collective-permute-start | bytes 1327112 | tf_op jit(solution)/shard_map/ppermute | solution.py:131
  52.6 0.8 %collective-permute-start.6 = (bf16[192,1152]{1,0:T(8,128)(2,1)S(1)}, bf16[192,1152]{1,0:T(8,128)(2,1)S(1)}, u32[]{:S(2)}, u32[]{:S(2)}) collective-permute-start(bf16[192,1152]{1,0:T(8,128)(2,1)S(1)} %pad_maximum_fusion.refs_0_), channel_id=1, source_target_pairs={{0,1},{1,0},{2,3},{3,2},{4,5},{5,4},{6,7},{7,6},{8,9},{9,8},{10,11... | collective-permute-start | bytes 1327112 | tf_op jit(solution)/shard_map/ppermute | solution.py:131
  53.4 0.0 collective-permute-done.12.refs_6_
  53.4 0.0 copy-start.4
  53.4 0.1 collective-permute-start.18
  53.5 8.3 %collective-permute-done.11.refs_5_ = bf16[192,1152]{1,0:T(8,128)(2,1)S(1)} collective-permute-done((bf16[192,1152]{1,0:T(8,128)(2,1)S(1)}, bf16[192,1152]{1,0:T(8,128)(2,1)S(1)}, u32[]{:S(2)}, u32[]{:S(2)}) %collective-permute-start.11) | collective-permute-done | bytes 442400 | tf_op jit(solution)/shard_map/ppermute | solution.py:131
  61.8 1.0 %collective-permute-start.13 = (bf16[192,1152]{1,0:T(8,128)(2,1)S(1)}, bf16[192,1152]{1,0:T(8,128)(2,1)}, u32[]{:S(2)}, u32[]{:S(2)}) collective-permute-start(bf16[192,1152]{1,0:T(8,128)(2,1)S(1)} %collective-permute-done.11.refs_5_), channel_id=1, source_target_pairs={{0,1},{1,0},{2,3},{3,2},{4,5},{5,4},{6,7},{7,6},{8,9},{9,8},{10,11... | collective-permute-start | bytes 1327112 | tf_op jit(solution)/shard_map/ppermute | solution.py:131
  62.7 0.0 collective-permute-done.5.refs_1_
  62.7 0.1 collective-permute-start.7
  62.9 0.0 collective-permute-done.17.refs_9_
  62.9 1.4 %collective-permute-start.19 = (bf16[192,1152]{1,0:T(8,128)(2,1)S(1)}, bf16[192,1152]{1,0:T(8,128)(2,1)}, u32[]{:S(2)}, u32[]{:S(2)}) collective-permute-start(bf16[192,1152]{1,0:T(8,128)(2,1)S(1)} %collective-permute-done.17.refs_9_), channel_id=1, source_target_pairs={{0,1},{1,0},{2,3},{3,2},{4,5},{5,4},{6,7},{7,6},{8,9},{9,8},{10,11... | collective-permute-start | bytes 1327112 | tf_op jit(solution)/shard_map/ppermute | solution.py:131
  64.2 8.3 %first_tick.1 = (bf16[1,2,768,1152]{3,2,1,0:T(8,128)(2,1)}, bf16[1,2,768,1152]{3,2,1,0:T(8,128)(2,1)}) custom-call(s32[1]{0:T(128)} %bitcast.6.early_ref, bf16[1,768,1152]{2,1,0:T(8,128)(2,1)} %a_ref.1, bf16[1,768,1152]{2,1,0:T(8,128)(2,1)} %h_ref.1, bf16[1,768,1152]{2,1,0:T(8,128)(2,1)} %g_ref.1, bf16[1,1152,1152]{2,1,0:T(8,128)(2,1)} %w_ref.1), custom_call_target="tpu_custom_call" | custom-call | flops 4076863488 | bytes 12386304 | tf_op jit(solution)/shard_map/first_tick/pallas_call | solution.py:51
  72.5 0.0 copy-done.1
  72.5 0.0 copy-done.2
  72.5 0.0 copy-done.3
  72.5 0.0 copy-done.4
  72.6 0.0 copy-done.5
  72.6 0.0 copy-done.6
  72.6 0.0 copy-done.7
  72.6 0.0 collective-permute-done.6.refs_2_
  72.6 0.0 copy-start.8
  72.6 0.0 collective-permute-done.18.refs_10_
  72.6 0.0 collective-permute-done.13.refs_7_
  72.6 0.0 collective-permute-done.7.refs_3_
  72.6 0.0 collective-permute-done.19.refs_11_
  72.6 0.7 copy-done.8
  73.4 5.2 %place.1 = (bf16[1,2,768,1152]{3,2,1,0:T(8,128)(2,1)}, bf16[1,2,768,1152]{3,2,1,0:T(8,128)(2,1)}, bf16[1,768,1152]{2,1,0:T(8,128)(2,1)}) custom-call(s32[1]{0:T(128)} %bitcast.replica_ref, bf16[192,1152]{1,0:T(8,128)(2,1)} %copy-done.2, bf16[192,1152]{1,0:T(8,128)(2,1)} %copy-done.6, ...), custom_call_target="tpu_custom_call", output_to_operand_aliasing={{0}: (13, {}), {1}: (14, {})} | custom-call | tf_op jit(solution)/shard_map/place/pallas_call | solution.py:95
  (9 shorter events, 0.2 us)
Async XLA Ops:
  0.6 12.6 %copy-start = (bf16[1,1152,1152]{2,1,0:T(8,128)(2,1)S(1)}, bf16[1,1152,1152]{2,1,0:T(8,128)(2,1)}, u32[]{:S(2)}) copy-start(bf16[1,1152,1152]{2,1,0:T(8,128)(2,1)} %w_ref.1) | copy-start | bytes 7962628
  1.7 15.6 %collective-permute-start = (bf16[48,1152]{1,0:T(8,128)(2,1)S(1)}, bf16[48,1152]{1,0:T(8,128)(2,1)S(1)}, u32[]{:S(2)}, u32[]{:S(2)}) collective-permute-start(bf16[48,1152]{1,0:T(8,128)(2,1)S(1)} %dynamic-slice_bitcast_fusion), channel_id=1, source_target_pairs={{0,40},{1,41},{2,42},{3,43},{4,44},{5,45},{6,46},{7,47},{8,32},{9,... | collective-permute-start | bytes 331784 | tf_op jit(solution)/shard_map/ppermute | solution.py:131
  15.3 14.6 %collective-permute-start.1 = (bf16[48,1152]{1,0:T(8,128)(2,1)S(1)}, bf16[48,1152]{1,0:T(8,128)(2,1)S(1)}, u32[]{:S(2)}, u32[]{:S(2)}) collective-permute-start(bf16[48,1152]{1,0:T(8,128)(2,1)S(1)} %get-tuple-element.7), channel_id=1, source_target_pairs={{32,8},{33,9},{34,10},{35,11},{36,12},{37,13},{38,14},{39,15},{40,... | collective-permute-start | bytes 331784 | tf_op jit(solution)/shard_map/ppermute | solution.py:131
  16.6 13.3 %collective-permute-start.2 = (bf16[48,1152]{1,0:T(8,128)(2,1)S(1)}, bf16[48,1152]{1,0:T(8,128)(2,1)S(1)}, u32[]{:S(2)}, u32[]{:S(2)}) collective-permute-start(bf16[48,1152]{1,0:T(8,128)(2,1)S(1)} %get-tuple-element.8), channel_id=1, source_target_pairs={{0,24},{1,25},{2,26},{3,27},{4,28},{5,29},{6,30},{7,31},{8,16},{9,... | collective-permute-start | bytes 331784 | tf_op jit(solution)/shard_map/ppermute | solution.py:131
  16.7 16.1 %collective-permute-start.8 = (bf16[48,1152]{1,0:T(8,128)(2,1)S(1)}, bf16[48,1152]{1,0:T(8,128)(2,1)S(1)}, u32[]{:S(2)}, u32[]{:S(2)}) collective-permute-start(bf16[48,1152]{1,0:T(8,128)(2,1)S(1)} %get-tuple-element.9), channel_id=1, source_target_pairs={{240,232},{241,233},{242,234},{243,235},{244,236},{245,237},{246,2... | collective-permute-start | bytes 331784 | tf_op jit(solution)/shard_map/ppermute | solution.py:131
  18.8 17.8 %collective-permute-start.14 = (bf16[48,1152]{1,0:T(8,128)(2,1)S(1)}, bf16[48,1152]{1,0:T(8,128)(2,1)S(1)}, u32[]{:S(2)}, u32[]{:S(2)}) collective-permute-start(bf16[48,1152]{1,0:T(8,128)(2,1)S(1)} %fusion.19), channel_id=1, source_target_pairs={{0,16},{1,17},{2,18},{3,19},{4,20},{5,21},{6,22},{7,23},{8,24},{9,... | collective-permute-start | bytes 331784 | tf_op jit(solution)/shard_map/ppermute | solution.py:131
  31.3 6.3 %collective-permute-start.3 = (bf16[48,1152]{1,0:T(8,128)(2,1)S(1)}, bf16[48,1152]{1,0:T(8,128)(2,1)S(1)}, u32[]{:S(2)}, u32[]{:S(2)}) collective-permute-start(bf16[48,1152]{1,0:T(8,128)(2,1)S(1)} %fusion.22), channel_id=1, source_target_pairs={{0,2},{1,3},{2,0},{3,1},{4,6},{5,7},{6,4},{7,5},{8,10},{9,11},{10,... | collective-permute-start | bytes 331784 | tf_op jit(solution)/shard_map/ppermute | solution.py:131
  34.6 4.9 %collective-permute-start.9 = (bf16[48,1152]{1,0:T(8,128)(2,1)S(1)}, bf16[48,1152]{1,0:T(8,128)(2,1)S(1)}, u32[]{:S(2)}, u32[]{:S(2)}) collective-permute-start(bf16[48,1152]{1,0:T(8,128)(2,1)S(1)} %fusion.27), channel_id=1, source_target_pairs={{0,6},{1,7},{2,4},{3,5},{4,2},{5,3},{6,0},{7,1},{8,14},{9,15},{10,... | collective-permute-start | bytes 331784 | tf_op jit(solution)/shard_map/ppermute | solution.py:131
  37.5 4.0 %collective-permute-start.15 = (bf16[48,1152]{1,0:T(8,128)(2,1)S(1)}, bf16[48,1152]{1,0:T(8,128)(2,1)S(1)}, u32[]{:S(2)}, u32[]{:S(2)}) collective-permute-start(bf16[48,1152]{1,0:T(8,128)(2,1)S(1)} %broadcast_select_fusion), channel_id=1, source_target_pairs={{0,8},{1,9},{2,10},{3,11},{4,12},{5,13},{6,14},{7,15},{8,0},{9,1},... | collective-permute-start | bytes 331784 | tf_op jit(solution)/shard_map/ppermute | solution.py:131
  37.7 12.5 %collective-permute-start.4 = (bf16[96,1152]{1,0:T(8,128)(2,1)S(1)}, bf16[96,1152]{1,0:T(8,128)(2,1)S(1)}, u32[]{:S(2)}, u32[]{:S(2)}) collective-permute-start(bf16[96,1152]{1,0:T(8,128)(2,1)S(1)} %pad_maximum_fusion.3), channel_id=1, source_target_pairs={{0,6},{1,7},{2,4},{3,5},{4,2},{5,3},{6,0},{7,1},{8,14},{9,15},{10,... | collective-permute-start | bytes 663560 | tf_op jit(solution)/shard_map/ppermute | solution.py:131
  39.5 6.4 %collective-permute-start.10 = (bf16[96,1152]{1,0:T(8,128)(2,1)S(1)}, bf16[96,1152]{1,0:T(8,128)(2,1)S(1)}, u32[]{:S(2)}, u32[]{:S(2)}) collective-permute-start(bf16[96,1152]{1,0:T(8,128)(2,1)S(1)} %pad_maximum_fusion.4), channel_id=1, source_target_pairs={{0,8},{1,9},{2,10},{3,11},{4,12},{5,13},{6,14},{7,15},{8,0},{9,1},... | collective-permute-start | bytes 663560 | tf_op jit(solution)/shard_map/ppermute | solution.py:131
  41.5 8.8 %collective-permute-start.16 = (bf16[96,1152]{1,0:T(8,128)(2,1)S(1)}, bf16[96,1152]{1,0:T(8,128)(2,1)S(1)}, u32[]{:S(2)}, u32[]{:S(2)}) collective-permute-start(bf16[96,1152]{1,0:T(8,128)(2,1)S(1)} %pad_maximum_fusion.5), channel_id=1, source_target_pairs={{0,2},{1,3},{2,0},{3,1},{4,6},{5,7},{6,4},{7,5},{8,10},{9,11},{10,... | collective-permute-start | bytes 663560 | tf_op jit(solution)/shard_map/ppermute | solution.py:131
  45.9 26.6 %copy-start.1 = (bf16[192,1152]{1,0:T(8,128)(2,1)}, bf16[192,1152]{1,0:T(8,128)(2,1)S(1)}, u32[]{:S(2)}) copy-start(bf16[192,1152]{1,0:T(8,128)(2,1)S(1)} %pad_maximum_fusion.1.refs_4_) | copy-start | bytes 1327108
  45.9 7.5 %collective-permute-start.12 = (bf16[192,1152]{1,0:T(8,128)(2,1)S(1)}, bf16[192,1152]{1,0:T(8,128)(2,1)S(1)}, u32[]{:S(2)}, u32[]{:S(2)}) collective-permute-start(bf16[192,1152]{1,0:T(8,128)(2,1)S(1)} %pad_maximum_fusion.1.refs_4_), channel_id=1, source_target_pairs={{0,1},{1,0},{2,3},{3,2},{4,5},{5,4},{6,7},{7,6},{8,9},{9,8},{10,11... | collective-permute-start | bytes 1327112 | tf_op jit(solution)/shard_map/ppermute | solution.py:131
  50.1 11.6 %collective-permute-start.11 = (bf16[192,1152]{1,0:T(8,128)(2,1)S(1)}, bf16[192,1152]{1,0:T(8,128)(2,1)S(1)}, u32[]{:S(2)}, u32[]{:S(2)}) collective-permute-start(bf16[192,1152]{1,0:T(8,128)(2,1)S(1)} %pad_maximum_fusion.1.refs_4_), channel_id=1, source_target_pairs={{0,2},{1,3},{2,0},{3,1},{4,6},{5,7},{6,4},{7,5},{8,10},{9,11},{10,... | collective-permute-start | bytes 1327112 | tf_op jit(solution)/shard_map/ppermute | solution.py:131
  50.2 22.4 %copy-start.2 = (bf16[192,1152]{1,0:T(8,128)(2,1)}, bf16[192,1152]{1,0:T(8,128)(2,1)S(1)}, u32[]{:S(2)}) copy-start(bf16[192,1152]{1,0:T(8,128)(2,1)S(1)} %pad_maximum_fusion.refs_0_) | copy-start | bytes 1327108
  50.2 12.5 %collective-permute-start.5 = (bf16[192,1152]{1,0:T(8,128)(2,1)S(1)}, bf16[192,1152]{1,0:T(8,128)(2,1)S(1)}, u32[]{:S(2)}, u32[]{:S(2)}) collective-permute-start(bf16[192,1152]{1,0:T(8,128)(2,1)S(1)} %pad_maximum_fusion.refs_0_), channel_id=1, source_target_pairs={{0,8},{1,9},{2,10},{3,11},{4,12},{5,13},{6,14},{7,15},{8,0},{9,1},... | collective-permute-start | bytes 1327112 | tf_op jit(solution)/shard_map/ppermute | solution.py:131
  50.3 22.2 %copy-start.3 = (bf16[192,1152]{1,0:T(8,128)(2,1)}, bf16[192,1152]{1,0:T(8,128)(2,1)S(1)}, u32[]{:S(2)}) copy-start(bf16[192,1152]{1,0:T(8,128)(2,1)S(1)} %pad_maximum_fusion.2.refs_8_) | copy-start | bytes 1327108
  50.4 12.5 %collective-permute-start.17 = (bf16[192,1152]{1,0:T(8,128)(2,1)S(1)}, bf16[192,1152]{1,0:T(8,128)(2,1)S(1)}, u32[]{:S(2)}, u32[]{:S(2)}) collective-permute-start(bf16[192,1152]{1,0:T(8,128)(2,1)S(1)} %pad_maximum_fusion.2.refs_8_), channel_id=1, source_target_pairs={{0,6},{1,7},{2,4},{3,5},{4,2},{5,3},{6,0},{7,1},{8,14},{9,15},{10,... | collective-permute-start | bytes 1327112 | tf_op jit(solution)/shard_map/ppermute | solution.py:131
  52.6 20.0 %collective-permute-start.6 = (bf16[192,1152]{1,0:T(8,128)(2,1)S(1)}, bf16[192,1152]{1,0:T(8,128)(2,1)S(1)}, u32[]{:S(2)}, u32[]{:S(2)}) collective-permute-start(bf16[192,1152]{1,0:T(8,128)(2,1)S(1)} %pad_maximum_fusion.refs_0_), channel_id=1, source_target_pairs={{0,1},{1,0},{2,3},{3,2},{4,5},{5,4},{6,7},{7,6},{8,9},{9,8},{10,11... | collective-permute-start | bytes 1327112 | tf_op jit(solution)/shard_map/ppermute | solution.py:131
  53.4 19.1 %copy-start.4 = (bf16[192,1152]{1,0:T(8,128)(2,1)}, bf16[192,1152]{1,0:T(8,128)(2,1)S(1)}, u32[]{:S(2)}) copy-start(bf16[192,1152]{1,0:T(8,128)(2,1)S(1)} %collective-permute-done.12.refs_6_) | copy-start | bytes 1327108
  53.4 19.2 %collective-permute-start.18 = (bf16[192,1152]{1,0:T(8,128)(2,1)S(1)}, bf16[192,1152]{1,0:T(8,128)(2,1)}, u32[]{:S(2)}, u32[]{:S(2)}) collective-permute-start(bf16[192,1152]{1,0:T(8,128)(2,1)S(1)} %pad_maximum_fusion.2.refs_8_), channel_id=1, source_target_pairs={{0,1},{1,0},{2,3},{3,2},{4,5},{5,4},{6,7},{7,6},{8,9},{9,8},{10,11... | collective-permute-start | bytes 1327112 | tf_op jit(solution)/shard_map/ppermute | solution.py:131
  61.8 10.8 %copy-start.5 = (bf16[192,1152]{1,0:T(8,128)(2,1)}, bf16[192,1152]{1,0:T(8,128)(2,1)S(1)}, u32[]{:S(2)}) copy-start(bf16[192,1152]{1,0:T(8,128)(2,1)S(1)} %collective-permute-done.11.refs_5_) | copy-start | bytes 1327108
  61.8 10.9 %collective-permute-start.13 = (bf16[192,1152]{1,0:T(8,128)(2,1)S(1)}, bf16[192,1152]{1,0:T(8,128)(2,1)}, u32[]{:S(2)}, u32[]{:S(2)}) collective-permute-start(bf16[192,1152]{1,0:T(8,128)(2,1)S(1)} %collective-permute-done.11.refs_5_), channel_id=1, source_target_pairs={{0,1},{1,0},{2,3},{3,2},{4,5},{5,4},{6,7},{7,6},{8,9},{9,8},{10,11... | collective-permute-start | bytes 1327112 | tf_op jit(solution)/shard_map/ppermute | solution.py:131
  62.7 9.8 %copy-start.6 = (bf16[192,1152]{1,0:T(8,128)(2,1)}, bf16[192,1152]{1,0:T(8,128)(2,1)S(1)}, u32[]{:S(2)}) copy-start(bf16[192,1152]{1,0:T(8,128)(2,1)S(1)} %collective-permute-done.5.refs_1_) | copy-start | bytes 1327108
  62.7 9.9 %collective-permute-start.7 = (bf16[192,1152]{1,0:T(8,128)(2,1)S(1)}, bf16[192,1152]{1,0:T(8,128)(2,1)}, u32[]{:S(2)}, u32[]{:S(2)}) collective-permute-start(bf16[192,1152]{1,0:T(8,128)(2,1)S(1)} %collective-permute-done.5.refs_1_), channel_id=1, source_target_pairs={{0,1},{1,0},{2,3},{3,2},{4,5},{5,4},{6,7},{7,6},{8,9},{9,8},{10,11... | collective-permute-start | bytes 1327112 | tf_op jit(solution)/shard_map/ppermute | solution.py:131
  62.9 9.7 %copy-start.7 = (bf16[192,1152]{1,0:T(8,128)(2,1)}, bf16[192,1152]{1,0:T(8,128)(2,1)S(1)}, u32[]{:S(2)}) copy-start(bf16[192,1152]{1,0:T(8,128)(2,1)S(1)} %collective-permute-done.17.refs_9_) | copy-start | bytes 1327108
  62.9 9.8 %collective-permute-start.19 = (bf16[192,1152]{1,0:T(8,128)(2,1)S(1)}, bf16[192,1152]{1,0:T(8,128)(2,1)}, u32[]{:S(2)}, u32[]{:S(2)}) collective-permute-start(bf16[192,1152]{1,0:T(8,128)(2,1)S(1)} %collective-permute-done.17.refs_9_), channel_id=1, source_target_pairs={{0,1},{1,0},{2,3},{3,2},{4,5},{5,4},{6,7},{7,6},{8,9},{9,8},{10,11... | collective-permute-start | bytes 1327112 | tf_op jit(solution)/shard_map/ppermute | solution.py:131
  72.6 0.8 copy-start.8

commit v3 on v2

--- a/solution.py
+++ b/solution.py
@@ -63,50 +63,56 @@
         cost_estimate=pl.CostEstimate(
             flops=4 * height * width * width, bytes_accessed=14 * height * width, transcendentals=0
         ),
+        compiler_params=pltpu.CompilerParams(vmem_limit_bytes=60 << 20),
         name="first_tick",
     )(early, a, held, cot, weights)
 
 
 def place_kernel(masks, rows, replica_ref, *refs):
-    pieces = [refs[4 * k : 4 * k + 4] for k in range(3)]
-    out_ref, grad_ref, arrived_ref, sem = refs[14:]
+    count = sum(len(owners) for owners in masks)
+    pieces, targets, sem = refs[:count], refs[-4:-1], refs[-1]
     replica = replica_ref[0]
-    copies = []
-    for target, four, owners in zip((out_ref.at[0, 1], grad_ref.at[0, 1], arrived_ref.at[0]), pieces, masks):
-        for piece, owned in zip(four, owners):
+    views = (targets[0].at[0, 1], targets[1].at[0, 1], targets[2].at[0])
+    copies, at_piece = [], 0
+    for target, owners in zip(views, masks):
+        for owned in owners:
             for k, mask in enumerate(owned):
                 at = pl.multiple_of((replica ^ mask) * rows, rows)
                 copies.append(
                     pltpu.make_async_copy(
-                        piece.at[pl.ds(k * rows, rows)],
+                        pieces[at_piece].at[pl.ds(k * rows, rows)],
                         target.at[pl.ds(at, rows)],
                         sem.at[len(copies)],
                     )
                 )
+            at_piece += 1
     for copy in copies:
         copy.start()
     for copy in copies:
         copy.wait()
 
 
-def place(replica, pieces, masks, outs, grads, rows):
+def place(replica, pieces, masks, targets, rows):
     anywhere = pl.BlockSpec(memory_space=pl.ANY)
-    flat = [piece for four in pieces for piece in four]
+    flat = [piece for some in pieces for piece in some]
+    width = targets[0].shape[-1]
+    arrived = jax.ShapeDtypeStruct((1,) + targets[0].shape[2:], BF16)
+    chunks = sum(len(owned) for owners in masks for owned in owners)
     return pl.pallas_call(
         functools.partial(place_kernel, masks, rows),
         in_specs=[pl.BlockSpec(memory_space=pltpu.SMEM)]
-        + [pl.BlockSpec(memory_space=pltpu.VMEM)] * 12
-        + [anywhere] * 2,
+        + [pl.BlockSpec(memory_space=pltpu.VMEM)] * len(flat)
+        + [anywhere] * len(targets),
         out_specs=[anywhere] * 3,
-        out_shape=[
-            jax.ShapeDtypeStruct(outs.shape, BF16),
-            jax.ShapeDtypeStruct(grads.shape, BF16),
-            jax.ShapeDtypeStruct((1,) + outs.shape[2:], BF16),
-        ],
-        scratch_shapes=[pltpu.SemaphoreType.DMA((48,))],
-        input_output_aliases={13: 0, 14: 1},
+        out_shape=[jax.ShapeDtypeStruct(x.shape, BF16) for x in targets[:2]] + [arrived],
+        scratch_shapes=[pltpu.SemaphoreType.DMA((chunks,))],
+        input_output_aliases={1 + len(flat) + k: k for k in range(len(targets))},
+        compiler_params=pltpu.CompilerParams(vmem_limit_bytes=8 << 20),
+        cost_estimate=pl.CostEstimate(
+            flops=0, bytes_accessed=4 * chunks * rows * width, transcendentals=0
+        ),
         name="place",
-    )(replica, *flat, outs, grads)
+    )(replica, *flat, *targets)
 
 
 def local(
@@ -182,19 +188,18 @@
         masks = [m + [k ^ order[step] for k in m] for m, order in zip(masks, orders)]
     last = [send(x, (everyone, order[2])) for x, order in zip(held_rows, orders)]
     last_masks = [[k ^ order[2] for k in m] for m, order in zip(masks, orders)]
-    pieces, owners = [], []
-    for x, y, m, n in zip(held_rows, last, masks, last_masks):
-        pieces.append([x, y, send(x, (everyone, CORE)), send(y, (everyone, CORE))])
-        owners.append([m, n, [k ^ CORE for k in m], [k ^ CORE for k in n]])
-
-    outs, grads = first_tick(
-        jnp.reshape(is_early.astype(jnp.int32), (1,)),
-        section_inputs,
-        mirror_held,
-        section_cotangents,
-        join_weights,
-    )
-    return tuple(place(jnp.reshape(replica, (1,)), pieces, owners, outs, grads, rows))
+    near = [send(x, (everyone, CORE)) for x in held_rows]
+    operands = (section_inputs, mirror_held, section_cotangents, join_weights)
+    held_rows, operands = lax.optimization_barrier((held_rows, operands))
+    outs, grads = first_tick(jnp.reshape(is_early.astype(jnp.int32), (1,)), *operands)
+    last, near, outs, grads = lax.optimization_barrier((last, near, outs, grads))
+    far = [send(x, (everyone, CORE)) for x in last]
+    here = jnp.reshape(replica, (1,))
+    ready = [list(three) for three in zip(held_rows, last, near)]
+    owners = [[m, n, [k ^ CORE for k in m]] for m, n in zip(masks, last_masks)]
+    targets = place(here, ready, owners, (outs, grads), rows)
+    owners = [[[k ^ CORE for k in n]] for n in last_masks]
+    return tuple(place(here, [[x] for x in far], owners, targets, rows))
 
 
 def solution(mesh):

time: 79.1 us -> 71.6 us (0.905)
  waiting for transfers between devices: 14.6 us -> 9.49 us
  Pallas kernels: 13.5 us -> 12.7 us
    ppermute x20, waiting for transfers between devices: 14.6 us -> 9.49 us  [send(): lax.ppermute(value, AXES, sum((pairs(slots, flip) for slots, flip in move...]
    pallas_call x1 -> x2, Pallas kernels: 5.23 us -> 4.41 us  [place(): pl.pallas_call(functools.partial(place_kernel, masks, rows), in_specs=[pl...]
  transfers between devices with their start and end apart: 20 -> 20, of which waited for: 4 -> 4; matrix products, arithmetic and copies ran while one was open for 13% -> 14% of each run, Pallas kernels for 11% -> 16%
where the time goes in v3:
time: 71.6 us; the launch traced here: 71.1 us
  starting transfers between devices  36.8 us (51%)
  Pallas kernels  12.7 us (18%)
  waiting for transfers between devices  9.49 us (13%)
  matrix products  9.09 us (13%)
  other arithmetic  1.1 us (2%)
  local copies, waits for them, and re-layouts  1.07 us (1%)
  between operations  0.9 us (1%)
    ppermute x20, starting transfers between devices, send(): lax.ppermute(value, AXES, sum((pairs(slots, flip) for slots, flip in move...  36.8 us
    ppermute x20, waiting for transfers between devices, send(): lax.ppermute(value, AXES, sum((pairs(slots, flip) for slots, flip in move...  9.49 us
    pallas_call x1, Pallas kernels, first_tick(): pl.pallas_call(first_kernel, grid=(4,), in_specs=[pl.BlockSpec(memory_spa...  8.29 us
    dot_general x3, matrix products, times(): return jnp.dot(left, weights, preferred_element_type=F32)  5.24 us
    pallas_call x2, Pallas kernels, place(): pl.pallas_call(functools.partial(place_kernel, masks, rows), in_specs=[pl...  4.41 us
    dot_general x2, matrix products, times_t(): lax.dot_general(left, weights, (((1,), (1,)), ((), ())), preferred_elemen...  3.85 us
  transfers between devices with their start and end apart: 20, of which 4 were waited for; matrix products, arithmetic and copies ran while one was open for 14% of the time, Pallas kernels for 16%

profile of v3, /device:TPU:1, one launch (start us, length us, event | category | flops | bytes accessed | tf_op | source)
XLA Modules:
  0.0 71.1 jit_solution(10756653489322529876)
XLA Ops:
  0.6 0.0 copy-start
  0.7 1.1 %dynamic-slice_bitcast_fusion = bf16[48,1152]{1,0:T(8,128)(2,1)S(1)} fusion(bf16[1,768,1152]{2,1,0:T(8,128)(2,1)} %a_ref, s32[]{:T(128)S(6)} %select_n.95), kind=kLoop, calls=%fused_computation.36 | loop fusion | bytes 221188 | tf_op jit(solution)/shard_map/dynamic_slice | solution.py:140
  1.7 9.2 %collective-permute-start = (bf16[48,1152]{1,0:T(8,128)(2,1)S(1)}, bf16[48,1152]{1,0:T(8,128)(2,1)S(1)}, u32[]{:S(2)}, u32[]{:S(2)}) collective-permute-start(bf16[48,1152]{1,0:T(8,128)(2,1)S(1)} %dynamic-slice_bitcast_fusion), channel_id=1, source_target_pairs={{0,40},{1,41},{2,42},{3,43},{4,44},{5,45},{6,46},{7,47},{8,32},{9,... | collective-permute-start | bytes 331784 | tf_op jit(solution)/shard_map/ppermute | solution.py:137
  10.9 2.3 %fusion.6 = f32[48,1152]{1,0:T(8,128)S(1)} fusion(bf16[48,1152]{1,0:T(8,128)(2,1)S(1)} %dynamic-slice_bitcast_fusion, bf16[1,1152,1152]{2,1,0:T(8,128)(2,1)} %w_ref), kind=kOutput, calls=%fused_computation.6 | convolution fusion | flops 127401984 | bytes 2985984 | tf_op jit(solution)/shard_map/dot_general | solution.py:22
  13.3 0.0 copy-done
  13.3 2.0 %fusion.36 = (bf16[48,1152]{1,0:T(8,128)(2,1)S(1)}, bf16[48,1152]{1,0:T(8,128)(2,1)S(1)}, bf16[48,1152]{1,0:T(8,128)(2,1)S(1)}) fusion(f32[48,1152]{1,0:T(8,128)S(1)} %fusion.6, pred[]{:T(512)S(6)} %eq.18, bf16[1,768,1152]{2,1,0:T(8,128)(2,1)} %h_ref, s32[]{:T(128)S(6)} %select_n.95, bf16[1,768,1152]{2,1,0:T(8,128)(2,1)} %g_ref, ...), kind=kOutput, calls=%fused_computation.27 | convolution fusion | flops 128010240 | bytes 3651584 | tf_op jit(solution)/shard_map/dot_general | solution.py:26
  15.3 1.3 %collective-permute-start.1 = (bf16[48,1152]{1,0:T(8,128)(2,1)S(1)}, bf16[48,1152]{1,0:T(8,128)(2,1)S(1)}, u32[]{:S(2)}, u32[]{:S(2)}) collective-permute-start(bf16[48,1152]{1,0:T(8,128)(2,1)S(1)} %get-tuple-element.43), channel_id=1, source_target_pairs={{32,8},{33,9},{34,10},{35,11},{36,12},{37,13},{38,14},{39,15},{40,... | collective-permute-start | bytes 331784 | tf_op jit(solution)/shard_map/ppermute | solution.py:137
  16.6 0.1 collective-permute-start.2
  16.7 0.7 collective-permute-start.6
  17.3 0.0 collective-permute-done
  17.4 1.5 %fusion.19 = bf16[48,1152]{1,0:T(8,128)(2,1)S(1)} fusion(bf16[48,1152]{1,0:T(8,128)(2,1)S(1)} %get-tuple-element.45, bf16[1,1152,1152]{2,1,0:T(8,128)(2,1)S(1)} %copy-done, pred[]{:T(512)S(6)} %eq.18, bf16[48,1152]{1,0:T(8,128)(2,1)S(1)} %collective-permute-done, bf16[768,1152]{1,0:T(8,128)(2,1)} %param.9, s32[]{:T(128)S(6)} %select_n.94, pred[]{:T(512)S(6)} %eq.19), kind=kOutput, calls=%fused_computation.13 | convolution fusion | flops 127567872 | bytes 3096582 | tf_op jit(solution)/shard_map/dot_general | solution.py:22
  18.8 11.0 %collective-permute-start.10 = (bf16[48,1152]{1,0:T(8,128)(2,1)S(1)}, bf16[48,1152]{1,0:T(8,128)(2,1)S(1)}, u32[]{:S(2)}, u32[]{:S(2)}) collective-permute-start(bf16[48,1152]{1,0:T(8,128)(2,1)S(1)} %fusion.19), channel_id=1, source_target_pairs={{0,16},{1,17},{2,18},{3,19},{4,20},{5,21},{6,22},{7,23},{8,24},{9,... | collective-permute-start | bytes 331784 | tf_op jit(solution)/shard_map/ppermute | solution.py:137
  29.9 0.0 collective-permute-done.1
  29.9 0.0 collective-permute-done.2
  29.9 1.5 %fusion.22 = bf16[48,1152]{1,0:T(8,128)(2,1)S(1)} fusion(bf16[1,1152,1152]{2,1,0:T(8,128)(2,1)S(1)} %copy-done, bf16[48,1152]{1,0:T(8,128)(2,1)S(1)} %collective-permute-done.2, bf16[48,1152]{1,0:T(8,128)(2,1)S(1)} %collective-permute-done, bf16[48,1152]{1,0:T(8,128)(2,1)S(1)} %collective-permute-done.1, pred[]{:T(512)S(6)} %eq.20, pred[]{:T(512)S(6)} %eq.18, ...), kind=kOutput, calls=%fused_computation.14 | convolution fusion | flops 127733760 | bytes 3317767 | tf_op jit(solution)/shard_map/dot_general | solution.py:22
  31.3 1.4 %collective-permute-start.3 = (bf16[48,1152]{1,0:T(8,128)(2,1)S(1)}, bf16[48,1152]{1,0:T(8,128)(2,1)S(1)}, u32[]{:S(2)}, u32[]{:S(2)}) collective-permute-start(bf16[48,1152]{1,0:T(8,128)(2,1)S(1)} %fusion.22), channel_id=1, source_target_pairs={{0,2},{1,3},{2,0},{3,1},{4,6},{5,7},{6,4},{7,5},{8,10},{9,11},{10,... | collective-permute-start | bytes 331784 | tf_op jit(solution)/shard_map/ppermute | solution.py:137
  32.7 0.0 collective-permute-done.6
  32.7 1.9 %fusion.27 = bf16[48,1152]{1,0:T(8,128)(2,1)S(1)} fusion(bf16[1,1152,1152]{2,1,0:T(8,128)(2,1)S(1)} %copy-done, bf16[48,1152]{1,0:T(8,128)(2,1)S(1)} %collective-permute-done.2, bf16[48,1152]{1,0:T(8,128)(2,1)S(1)} %collective-permute-done.6, bf16[48,1152]{1,0:T(8,128)(2,1)S(1)} %collective-permute-done.1, pred[]{:T(512)S(6)} %eq.22, pred[]{:T(512)S(6)} %eq.21, ...), kind=kOutput, calls=%fused_computation.19 | convolution fusion | flops 128010240 | bytes 3543040 | tf_op jit(solution)/shard_map/dot_general | solution.py:26
  34.6 2.0 %collective-permute-start.7 = (bf16[48,1152]{1,0:T(8,128)(2,1)S(1)}, bf16[48,1152]{1,0:T(8,128)(2,1)S(1)}, u32[]{:S(2)}, u32[]{:S(2)}) collective-permute-start(bf16[48,1152]{1,0:T(8,128)(2,1)S(1)} %fusion.27), channel_id=1, source_target_pairs={{0,6},{1,7},{2,4},{3,5},{4,2},{5,3},{6,0},{7,1},{8,14},{9,15},{10,... | collective-permute-start | bytes 331784 | tf_op jit(solution)/shard_map/ppermute | solution.py:137
  36.6 0.0 collective-permute-done.10
  36.6 0.9 %broadcast_select_fusion = bf16[48,1152]{1,0:T(8,128)(2,1)S(1)} fusion(bf16[48,1152]{1,0:T(8,128)(2,1)S(1)} %collective-permute-done.10, pred[]{:T(512)S(6)} %eq.19, bf16[768,1152]{1,0:T(8,128)(2,1)} %param.10, s32[]{:T(128)S(6)} %select_n.94), kind=kLoop, calls=%fused_computation.42 | loop fusion | flops 55296 | bytes 331781 | tf_op jit(solution)/shard_map/jit(_where)/select_n | solution.py:172
  37.5 0.1 collective-permute-start.11
  37.6 0.0 collective-permute-done.3
  37.7 0.9 %collective-permute-start.4 = (bf16[96,1152]{1,0:T(8,128)(2,1)S(1)}, bf16[96,1152]{1,0:T(8,128)(2,1)S(1)}, u32[]{:S(2)}, u32[]{:S(2)}) collective-permute-start(bf16[96,1152]{1,0:T(8,128)(2,1)S(1)} %pad_maximum_fusion.3), channel_id=1, source_target_pairs={{0,6},{1,7},{2,4},{3,5},{4,2},{5,3},{6,0},{7,1},{8,14},{9,15},{10,... | collective-permute-start | bytes 663560 | tf_op jit(solution)/shard_map/ppermute | solution.py:137
  38.5 1.0 %collective-permute-done.7 = bf16[48,1152]{1,0:T(8,128)(2,1)S(1)} collective-permute-done((bf16[48,1152]{1,0:T(8,128)(2,1)S(1)}, bf16[48,1152]{1,0:T(8,128)(2,1)S(1)}, u32[]{:S(2)}, u32[]{:S(2)}) %collective-permute-start.7) | collective-permute-done | bytes 110624 | tf_op jit(solution)/shard_map/ppermute | solution.py:137
  39.5 0.6 collective-permute-start.8
  40.1 1.4 %collective-permute-done.11 = bf16[48,1152]{1,0:T(8,128)(2,1)S(1)} collective-permute-done((bf16[48,1152]{1,0:T(8,128)(2,1)S(1)}, bf16[48,1152]{1,0:T(8,128)(2,1)S(1)}, u32[]{:S(2)}, u32[]{:S(2)}) %collective-permute-start.11) | collective-permute-done | bytes 110624 | tf_op jit(solution)/shard_map/ppermute | solution.py:137
  41.5 0.5 collective-permute-start.12
  42.0 3.9 %collective-permute-done.8 = bf16[96,1152]{1,0:T(8,128)(2,1)S(1)} collective-permute-done((bf16[96,1152]{1,0:T(8,128)(2,1)S(1)}, bf16[96,1152]{1,0:T(8,128)(2,1)S(1)}, u32[]{:S(2)}, u32[]{:S(2)}) %collective-permute-start.8) | collective-permute-done | bytes 221216 | tf_op jit(solution)/shard_map/ppermute | solution.py:137
  45.9 4.2 %collective-permute-start.15 = (bf16[192,1152]{1,0:T(8,128)(2,1)S(1)}, bf16[192,1152]{1,0:T(8,128)(2,1)S(1)}, u32[]{:S(2)}, u32[]{:S(2)}) collective-permute-start(bf16[192,1152]{1,0:T(8,128)(2,1)S(1)} %pad_maximum_fusion.1.refs_3_), channel_id=1, source_target_pairs={{0,1},{1,0},{2,3},{3,2},{4,5},{5,4},{6,7},{7,6},{8,9},{9,8},{10,11... | collective-permute-start | bytes 1327112 | tf_op jit(solution)/shard_map/ppermute | solution.py:137
  50.1 0.0 collective-permute-start.9
  50.1 0.0 collective-permute-done.4
  50.2 0.2 collective-permute-start.14
  50.4 0.0 collective-permute-start.5
  50.4 0.0 collective-permute-done.12
  50.4 1.9 %collective-permute-start.16 = (bf16[192,1152]{1,0:T(8,128)(2,1)S(1)}, bf16[192,1152]{1,0:T(8,128)(2,1)}, u32[]{:S(2)}, u32[]{:S(2)}) collective-permute-start(bf16[192,1152]{1,0:T(8,128)(2,1)S(1)} %pad_maximum_fusion.2.refs_6_), channel_id=1, source_target_pairs={{0,1},{1,0},{2,3},{3,2},{4,5},{5,4},{6,7},{7,6},{8,9},{9,8},{10,11... | collective-permute-start | bytes 1327112 | tf_op jit(solution)/shard_map/ppermute | solution.py:137
  52.4 0.0 collective-permute-done.15.refs_5_
  52.4 1.3 %collective-permute-start.13 = (bf16[192,1152]{1,0:T(8,128)(2,1)S(1)}, bf16[192,1152]{1,0:T(8,128)(2,1)S(1)}, u32[]{:S(2)}, u32[]{:S(2)}) collective-permute-start(bf16[192,1152]{1,0:T(8,128)(2,1)S(1)} %pad_maximum_fusion.2.refs_6_), channel_id=1, source_target_pairs={{0,6},{1,7},{2,4},{3,5},{4,2},{5,3},{6,0},{7,1},{8,14},{9,15},{10,... | collective-permute-start | bytes 1327112 | tf_op jit(solution)/shard_map/ppermute | solution.py:137
  53.7 8.3 %first_tick.1 = (bf16[1,2,768,1152]{3,2,1,0:T(8,128)(2,1)}, bf16[1,2,768,1152]{3,2,1,0:T(8,128)(2,1)}) custom-call(s32[1]{0:T(128)} %bitcast.6.early_ref, bf16[1,768,1152]{2,1,0:T(8,128)(2,1)} %a_ref, bf16[1,768,1152]{2,1,0:T(8,128)(2,1)} %h_ref, bf16[1,768,1152]{2,1,0:T(8,128)(2,1)} %g_ref, bf16[1,1152,1152]{2,1,0:T(8,128)(2,1)} %w_ref), custom_call_target="tpu_custom_call" | custom-call | flops 4076863488 | bytes 12386304 | tf_op jit(solution)/shard_map/first_tick/pallas_call | solution.py:51
  62.0 0.0 collective-permute-done.9.refs_4_
  62.0 0.0 collective-permute-done.14.refs_2_
  62.0 0.0 collective-permute-done.5.refs_1_
  62.0 0.0 collective-permute-done.16.refs_8_
  62.0 3.2 %collective-permute-done.13.refs_7_ = bf16[192,1152]{1,0:T(8,128)(2,1)S(1)} collective-permute-done((bf16[192,1152]{1,0:T(8,128)(2,1)S(1)}, bf16[192,1152]{1,0:T(8,128)(2,1)S(1)}, u32[]{:S(2)}, u32[]{:S(2)}) %collective-permute-start.13) | collective-permute-done | bytes 442400 | tf_op jit(solution)/shard_map/ppermute | solution.py:137
  65.2 1.0 %collective-permute-start.17 = (bf16[192,1152]{1,0:T(8,128)(2,1)S(1)}, bf16[192,1152]{1,0:T(8,128)(2,1)S(1)}, u32[]{:S(2)}, u32[]{:S(2)}) collective-permute-start(bf16[192,1152]{1,0:T(8,128)(2,1)S(1)} %collective-permute-done.5.refs_1_), channel_id=1, source_target_pairs={{0,1},{1,0},{2,3},{3,2},{4,5},{5,4},{6,7},{7,6},{8,9},{9,8},{10,11... | collective-permute-start | bytes 1327112 | tf_op jit(solution)/shard_map/ppermute | solution.py:137
  66.2 0.0 collective-permute-start.18
  66.2 0.5 collective-permute-start.19
  66.7 3.2 %place.2 = (bf16[1,2,768,1152]{3,2,1,0:T(8,128)(2,1)}, bf16[1,2,768,1152]{3,2,1,0:T(8,128)(2,1)}, bf16[1,768,1152]{2,1,0:T(8,128)(2,1)}) custom-call(s32[1]{0:T(128)} %bitcast.replica_ref, bf16[192,1152]{1,0:T(8,128)(2,1)S(1)} %pad_maximum_fusion.refs_0_, ...), custom_call_target="tpu_custom_call", output_to_operand_aliasing={{0}: (10, {}), {1}: (11, {})} | custom-call | bytes 7962624 | tf_op jit(solution)/shard_map/place/pallas_call | solution.py:101
  69.9 0.0 collective-permute-done.17.refs_0_
  69.9 0.0 collective-permute-done.18.refs_1_
  70.0 0.0 collective-permute-done.19.refs_2_
  70.0 1.2 %place.3 = (bf16[1,2,768,1152]{3,2,1,0:T(8,128)(2,1)}, bf16[1,2,768,1152]{3,2,1,0:T(8,128)(2,1)}, bf16[1,768,1152]{2,1,0:T(8,128)(2,1)}) custom-call(s32[1]{0:T(128)} %bitcast.replica_ref, bf16[192,1152]{1,0:T(8,128)(2,1)S(1)} %collective-permute-done.17.refs_0_, ...), custom_call_target="tpu_custom_call", output_to_operand_aliasing={{0}: (4, {}), {1}: (5, {}), {2}: (6, {})} | custom-call | bytes 2654208 | tf_op jit(solution)/shard_map/place/pallas_call | solution.py:101
  (6 shorter events, 0.2 us)
Async XLA Ops:
  0.6 12.6 %copy-start = (bf16[1,1152,1152]{2,1,0:T(8,128)(2,1)S(1)}, bf16[1,1152,1152]{2,1,0:T(8,128)(2,1)}, u32[]{:S(2)}) copy-start(bf16[1,1152,1152]{2,1,0:T(8,128)(2,1)} %w_ref) | copy-start | bytes 7962628
  1.7 15.6 %collective-permute-start = (bf16[48,1152]{1,0:T(8,128)(2,1)S(1)}, bf16[48,1152]{1,0:T(8,128)(2,1)S(1)}, u32[]{:S(2)}, u32[]{:S(2)}) collective-permute-start(bf16[48,1152]{1,0:T(8,128)(2,1)S(1)} %dynamic-slice_bitcast_fusion), channel_id=1, source_target_pairs={{0,40},{1,41},{2,42},{3,43},{4,44},{5,45},{6,46},{7,47},{8,32},{9,... | collective-permute-start | bytes 331784 | tf_op jit(solution)/shard_map/ppermute | solution.py:137
  15.3 14.6 %collective-permute-start.1 = (bf16[48,1152]{1,0:T(8,128)(2,1)S(1)}, bf16[48,1152]{1,0:T(8,128)(2,1)S(1)}, u32[]{:S(2)}, u32[]{:S(2)}) collective-permute-start(bf16[48,1152]{1,0:T(8,128)(2,1)S(1)} %get-tuple-element.43), channel_id=1, source_target_pairs={{32,8},{33,9},{34,10},{35,11},{36,12},{37,13},{38,14},{39,15},{40,... | collective-permute-start | bytes 331784 | tf_op jit(solution)/shard_map/ppermute | solution.py:137
  16.6 13.3 %collective-permute-start.2 = (bf16[48,1152]{1,0:T(8,128)(2,1)S(1)}, bf16[48,1152]{1,0:T(8,128)(2,1)S(1)}, u32[]{:S(2)}, u32[]{:S(2)}) collective-permute-start(bf16[48,1152]{1,0:T(8,128)(2,1)S(1)} %get-tuple-element.44), channel_id=1, source_target_pairs={{0,24},{1,25},{2,26},{3,27},{4,28},{5,29},{6,30},{7,31},{8,16},{9,... | collective-permute-start | bytes 331784 | tf_op jit(solution)/shard_map/ppermute | solution.py:137
  16.7 16.1 %collective-permute-start.6 = (bf16[48,1152]{1,0:T(8,128)(2,1)S(1)}, bf16[48,1152]{1,0:T(8,128)(2,1)S(1)}, u32[]{:S(2)}, u32[]{:S(2)}) collective-permute-start(bf16[48,1152]{1,0:T(8,128)(2,1)S(1)} %get-tuple-element.45), channel_id=1, source_target_pairs={{240,232},{241,233},{242,234},{243,235},{244,236},{245,237},{246,2... | collective-permute-start | bytes 331784 | tf_op jit(solution)/shard_map/ppermute | solution.py:137
  18.8 17.8 %collective-permute-start.10 = (bf16[48,1152]{1,0:T(8,128)(2,1)S(1)}, bf16[48,1152]{1,0:T(8,128)(2,1)S(1)}, u32[]{:S(2)}, u32[]{:S(2)}) collective-permute-start(bf16[48,1152]{1,0:T(8,128)(2,1)S(1)} %fusion.19), channel_id=1, source_target_pairs={{0,16},{1,17},{2,18},{3,19},{4,20},{5,21},{6,22},{7,23},{8,24},{9,... | collective-permute-start | bytes 331784 | tf_op jit(solution)/shard_map/ppermute | solution.py:137
  31.3 6.3 %collective-permute-start.3 = (bf16[48,1152]{1,0:T(8,128)(2,1)S(1)}, bf16[48,1152]{1,0:T(8,128)(2,1)S(1)}, u32[]{:S(2)}, u32[]{:S(2)}) collective-permute-start(bf16[48,1152]{1,0:T(8,128)(2,1)S(1)} %fusion.22), channel_id=1, source_target_pairs={{0,2},{1,3},{2,0},{3,1},{4,6},{5,7},{6,4},{7,5},{8,10},{9,11},{10,... | collective-permute-start | bytes 331784 | tf_op jit(solution)/shard_map/ppermute | solution.py:137
  34.6 4.9 %collective-permute-start.7 = (bf16[48,1152]{1,0:T(8,128)(2,1)S(1)}, bf16[48,1152]{1,0:T(8,128)(2,1)S(1)}, u32[]{:S(2)}, u32[]{:S(2)}) collective-permute-start(bf16[48,1152]{1,0:T(8,128)(2,1)S(1)} %fusion.27), channel_id=1, source_target_pairs={{0,6},{1,7},{2,4},{3,5},{4,2},{5,3},{6,0},{7,1},{8,14},{9,15},{10,... | collective-permute-start | bytes 331784 | tf_op jit(solution)/shard_map/ppermute | solution.py:137
  37.5 4.0 %collective-permute-start.11 = (bf16[48,1152]{1,0:T(8,128)(2,1)S(1)}, bf16[48,1152]{1,0:T(8,128)(2,1)S(1)}, u32[]{:S(2)}, u32[]{:S(2)}) collective-permute-start(bf16[48,1152]{1,0:T(8,128)(2,1)S(1)} %broadcast_select_fusion), channel_id=1, source_target_pairs={{0,8},{1,9},{2,10},{3,11},{4,12},{5,13},{6,14},{7,15},{8,0},{9,1},... | collective-permute-start | bytes 331784 | tf_op jit(solution)/shard_map/ppermute | solution.py:137
  37.7 12.5 %collective-permute-start.4 = (bf16[96,1152]{1,0:T(8,128)(2,1)S(1)}, bf16[96,1152]{1,0:T(8,128)(2,1)S(1)}, u32[]{:S(2)}, u32[]{:S(2)}) collective-permute-start(bf16[96,1152]{1,0:T(8,128)(2,1)S(1)} %pad_maximum_fusion.3), channel_id=1, source_target_pairs={{0,6},{1,7},{2,4},{3,5},{4,2},{5,3},{6,0},{7,1},{8,14},{9,15},{10,... | collective-permute-start | bytes 663560 | tf_op jit(solution)/shard_map/ppermute | solution.py:137
  39.5 6.4 %collective-permute-start.8 = (bf16[96,1152]{1,0:T(8,128)(2,1)S(1)}, bf16[96,1152]{1,0:T(8,128)(2,1)S(1)}, u32[]{:S(2)}, u32[]{:S(2)}) collective-permute-start(bf16[96,1152]{1,0:T(8,128)(2,1)S(1)} %pad_maximum_fusion.4), channel_id=1, source_target_pairs={{0,8},{1,9},{2,10},{3,11},{4,12},{5,13},{6,14},{7,15},{8,0},{9,1},... | collective-permute-start | bytes 663560 | tf_op jit(solution)/shard_map/ppermute | solution.py:137
  41.5 8.8 %collective-permute-start.12 = (bf16[96,1152]{1,0:T(8,128)(2,1)S(1)}, bf16[96,1152]{1,0:T(8,128)(2,1)S(1)}, u32[]{:S(2)}, u32[]{:S(2)}) collective-permute-start(bf16[96,1152]{1,0:T(8,128)(2,1)S(1)} %pad_maximum_fusion.5), channel_id=1, source_target_pairs={{0,2},{1,3},{2,0},{3,1},{4,6},{5,7},{6,4},{7,5},{8,10},{9,11},{10,... | collective-permute-start | bytes 663560 | tf_op jit(solution)/shard_map/ppermute | solution.py:137
  45.9 6.4 %collective-permute-start.15 = (bf16[192,1152]{1,0:T(8,128)(2,1)S(1)}, bf16[192,1152]{1,0:T(8,128)(2,1)S(1)}, u32[]{:S(2)}, u32[]{:S(2)}) collective-permute-start(bf16[192,1152]{1,0:T(8,128)(2,1)S(1)} %pad_maximum_fusion.1.refs_3_), channel_id=1, source_target_pairs={{0,1},{1,0},{2,3},{3,2},{4,5},{5,4},{6,7},{7,6},{8,9},{9,8},{10,11... | collective-permute-start | bytes 1327112 | tf_op jit(solution)/shard_map/ppermute | solution.py:137
  50.1 11.9 %collective-permute-start.9 = (bf16[192,1152]{1,0:T(8,128)(2,1)S(1)}, bf16[192,1152]{1,0:T(8,128)(2,1)S(1)}, u32[]{:S(2)}, u32[]{:S(2)}) collective-permute-start(bf16[192,1152]{1,0:T(8,128)(2,1)S(1)} %pad_maximum_fusion.1.refs_3_), channel_id=1, source_target_pairs={{0,2},{1,3},{2,0},{3,1},{4,6},{5,7},{6,4},{7,5},{8,10},{9,11},{10,... | collective-permute-start | bytes 1327112 | tf_op jit(solution)/shard_map/ppermute | solution.py:137
  50.2 11.8 %collective-permute-start.14 = (bf16[192,1152]{1,0:T(8,128)(2,1)S(1)}, bf16[192,1152]{1,0:T(8,128)(2,1)S(1)}, u32[]{:S(2)}, u32[]{:S(2)}) collective-permute-start(bf16[192,1152]{1,0:T(8,128)(2,1)S(1)} %pad_maximum_fusion.refs_0_), channel_id=1, source_target_pairs={{0,1},{1,0},{2,3},{3,2},{4,5},{5,4},{6,7},{7,6},{8,9},{9,8},{10,11... | collective-permute-start | bytes 1327112 | tf_op jit(solution)/shard_map/ppermute | solution.py:137
  50.4 11.6 %collective-permute-start.5 = (bf16[192,1152]{1,0:T(8,128)(2,1)S(1)}, bf16[192,1152]{1,0:T(8,128)(2,1)S(1)}, u32[]{:S(2)}, u32[]{:S(2)}) collective-permute-start(bf16[192,1152]{1,0:T(8,128)(2,1)S(1)} %pad_maximum_fusion.refs_0_), channel_id=1, source_target_pairs={{0,8},{1,9},{2,10},{3,11},{4,12},{5,13},{6,14},{7,15},{8,0},{9,1},... | collective-permute-start | bytes 1327112 | tf_op jit(solution)/shard_map/ppermute | solution.py:137
  50.4 11.6 %collective-permute-start.16 = (bf16[192,1152]{1,0:T(8,128)(2,1)S(1)}, bf16[192,1152]{1,0:T(8,128)(2,1)}, u32[]{:S(2)}, u32[]{:S(2)}) collective-permute-start(bf16[192,1152]{1,0:T(8,128)(2,1)S(1)} %pad_maximum_fusion.2.refs_6_), channel_id=1, source_target_pairs={{0,1},{1,0},{2,3},{3,2},{4,5},{5,4},{6,7},{7,6},{8,9},{9,8},{10,11... | collective-permute-start | bytes 1327112 | tf_op jit(solution)/shard_map/ppermute | solution.py:137
  52.4 12.8 %collective-permute-start.13 = (bf16[192,1152]{1,0:T(8,128)(2,1)S(1)}, bf16[192,1152]{1,0:T(8,128)(2,1)S(1)}, u32[]{:S(2)}, u32[]{:S(2)}) collective-permute-start(bf16[192,1152]{1,0:T(8,128)(2,1)S(1)} %pad_maximum_fusion.2.refs_6_), channel_id=1, source_target_pairs={{0,6},{1,7},{2,4},{3,5},{4,2},{5,3},{6,0},{7,1},{8,14},{9,15},{10,... | collective-permute-start | bytes 1327112 | tf_op jit(solution)/shard_map/ppermute | solution.py:137
  65.2 4.7 %collective-permute-start.17 = (bf16[192,1152]{1,0:T(8,128)(2,1)S(1)}, bf16[192,1152]{1,0:T(8,128)(2,1)S(1)}, u32[]{:S(2)}, u32[]{:S(2)}) collective-permute-start(bf16[192,1152]{1,0:T(8,128)(2,1)S(1)} %collective-permute-done.5.refs_1_), channel_id=1, source_target_pairs={{0,1},{1,0},{2,3},{3,2},{4,5},{5,4},{6,7},{7,6},{8,9},{9,8},{10,11... | collective-permute-start | bytes 1327112 | tf_op jit(solution)/shard_map/ppermute | solution.py:137
  66.2 3.8 %collective-permute-start.18 = (bf16[192,1152]{1,0:T(8,128)(2,1)S(1)}, bf16[192,1152]{1,0:T(8,128)(2,1)S(1)}, u32[]{:S(2)}, u32[]{:S(2)}) collective-permute-start(bf16[192,1152]{1,0:T(8,128)(2,1)S(1)} %collective-permute-done.9.refs_4_), channel_id=1, source_target_pairs={{0,1},{1,0},{2,3},{3,2},{4,5},{5,4},{6,7},{7,6},{8,9},{9,8},{10,11... | collective-permute-start | bytes 1327112 | tf_op jit(solution)/shard_map/ppermute | solution.py:137
  66.2 3.8 %collective-permute-start.19 = (bf16[192,1152]{1,0:T(8,128)(2,1)S(1)}, bf16[192,1152]{1,0:T(8,128)(2,1)S(1)}, u32[]{:S(2)}, u32[]{:S(2)}) collective-permute-start(bf16[192,1152]{1,0:T(8,128)(2,1)S(1)} %collective-permute-done.13.refs_7_), channel_id=1, source_target_pairs={{0,1},{1,0},{2,3},{3,2},{4,5},{5,4},{6,7},{7,6},{8,9},{9,8},{10,11... | collective-permute-start | bytes 1327112 | tf_op jit(solution)/shard_map/ppermute | solution.py:137

commit v4 on v3

v4 whole, which is shorter than its diff:
```python
import functools

import jax
import jax.numpy as jnp
from jax import lax
from jax.experimental import pallas as pl
from jax.experimental.pallas import tpu as pltpu
from jax.sharding import PartitionSpec as P


AXES = ("section", "dp")
BF16 = jnp.bfloat16
F32 = jnp.float32
CORE, Y_NEAR, Y_FAR, Z = 1, 2, 6, 8


def next_slot(count):
    order = list(range(0, count, 2)) + list(range(count - 1, 0, -2))
    return dict(zip(order[:-1], order[1:]))


def times(left, weights):
    return jnp.dot(left, weights, preferred_element_type=F32)


def times_t(left, weights):
    return lax.dot_general(left, weights, (((1,), (1,)), ((), ())), preferred_element_type=F32)


def first_kernel(early_ref, a_ref, h_ref, g_ref, w_ref, out_ref, grad_ref, turned_ref):
    early = early_ref[0] == 1

    @pl.when(pl.program_id(0) == 0)
    def _():
        turned_ref[...] = w_ref[0].T

    @pl.when(early)
    def _():
        out_ref[0, 0] = a_ref[0]
        product = times(h_ref[0], turned_ref[...])
        grad_ref[0, 0] = (g_ref[0].astype(F32) + product).astype(BF16)

    @pl.when(jnp.logical_not(early))
    def _():
        product = times(a_ref[0], w_ref[0])
        out_ref[0, 0] = (product + h_ref[0].astype(F32)).astype(BF16)
        grad_ref[0, 0] = times(g_ref[0], turned_ref[...]).astype(BF16)


def first_tick(early, a, held, cot, weights):
    _, height, width = a.shape
    block = height // 4
    rows = pl.BlockSpec((1, block, width), lambda i: (0, i, 0))
    wide = pl.BlockSpec((1, 1, block, width), lambda i: (0, 0, i, 0))
    both = jax.ShapeDtypeStruct((1, 2, height, width), BF16)
    return pl.pallas_call(
        first_kernel,
        grid=(4,),
        in_specs=[
            pl.BlockSpec(memory_space=pltpu.SMEM),
            rows,
            rows,
            rows,
            pl.BlockSpec((1, width, width), lambda i: (0, 0, 0)),
        ],
        out_specs=[wide, wide],
        out_shape=[both, both],
        scratch_shapes=[pltpu.VMEM((width, width), BF16)],
        cost_estimate=pl.CostEstimate(
            flops=4 * height * width * width, bytes_accessed=14 * height * width, transcendentals=0
        ),
        compiler_params=pltpu.CompilerParams(vmem_limit_bytes=60 << 20),
        name="first_tick",
    )(jnp.reshape(early.astype(jnp.int32), (1,)), a, held, cot, weights)


def place_kernel(plan, rows, replica_ref, *refs):
    pieces, targets, sem = refs[: len(plan)], refs[-4:-1], refs[-1]
    replica = replica_ref[0]
    views = (targets[0].at[0, 1], targets[1].at[0, 1], targets[2].at[0])
    copies = []
    for piece, blocks in zip(pieces, plan):
        for k, (output, mask) in enumerate(blocks):
            at = pl.multiple_of((replica ^ mask) * rows, rows)
            copies.append(
                pltpu.make_async_copy(
                    piece.at[pl.ds(k * rows, rows)],
                    views[output].at[pl.ds(at, rows)],
                    sem.at[len(copies)],
                )
            )
    for copy in copies:
        copy.start()
    for copy in copies:
        copy.wait()


def place(replica, pieces, plan, targets, rows):
    anywhere = pl.BlockSpec(memory_space=pl.ANY)
    width = targets[0].shape[-1]
    arrived = jax.ShapeDtypeStruct((1,) + targets[0].shape[2:], BF16)
    blocks = sum(len(some) for some in plan)
    return pl.pallas_call(
        functools.partial(place_kernel, plan, rows),
        in_specs=[pl.BlockSpec(memory_space=pltpu.SMEM)]
        + [pl.BlockSpec(memory_space=pltpu.VMEM)] * len(pieces)
        + [anywhere] * len(targets),
        out_specs=[anywhere] * 3,
        out_shape=[jax.ShapeDtypeStruct(x.shape, BF16) for x in targets[:2]] + [arrived],
        scratch_shapes=[pltpu.SemaphoreType.DMA((blocks,))],
        input_output_aliases={1 + len(pieces) + k: k for k in range(len(targets))},
        compiler_params=pltpu.CompilerParams(vmem_limit_bytes=8 << 20),
        cost_estimate=pl.CostEstimate(
            flops=0, bytes_accessed=4 * blocks * rows * width, transcendentals=0
        ),
    )(replica, *pieces, *targets)


def local(
    section_inputs, mirror_held, section_cotangents, next_batch, loss_cotangent, join_weights
):
    count = lax.axis_size("section")
    replicas = lax.axis_size("dp")
    position = lax.axis_index("section")
    replica = lax.axis_index("dp")
    is_early = position % 2 == 0
    weights = join_weights[0]
    rows = next_batch.shape[0] // replicas
    end = count - 1
    tie = lax.optimization_barrier

    def send(value, *moves):
        chosen = []
        for slots, flip in moves:
            for s, t in slots:
                chosen += [(s * replicas + d, t * replicas + (d ^ flip)) for d in range(replicas)]
        return lax.ppermute(value, AXES, chosen)

    after = next_slot(count)
    early = range(0, count, 2)
    late = range(1, count, 2)
    ahead = list(after.items())
    back = [(t, s) for s, t in ahead] + [(0, 1)]
    ahead += [(1, 0)]
    to_late = [(s, s + 1) for s in early]
    to_early = [(s, s - 1) for s in late]
    across = [(s, (s + 1) % count) for s in late]

    def part(whole, of):
        return lax.dynamic_slice_in_dim(whole, of * rows, rows, 0)

    sent = replica ^ Z
    a, held, cot = section_inputs[0], mirror_held[0], section_cotangents[0]
    a_part, held_part, cot_part = part(a, sent), part(held, sent), part(cot, sent)
    loss_part, batch_part = part(loss_cotangent, sent), part(next_batch, sent)
    product = times(a_part, weights)
    skip = product.astype(BF16)
    late_out = (product + held_part.astype(F32)).astype(BF16)
    out = jnp.where(is_early, a_part, jnp.where(position == 1, batch_part, late_out))
    level = jnp.where(is_early, skip, cot_part)
    came_out = send(out, (ahead, Z))
    came_level = send(level, (to_late, Z), (to_early, Z))
    product = times_t(jnp.where(is_early, held_part, cot_part), weights)
    grad = jnp.where(is_early, cot_part.astype(F32) + product, product).astype(BF16)
    grad_back = jnp.where(position == 0, loss_part, grad)
    grad_across = jnp.where(position == end, loss_part, grad)
    grad_back, grad_across = tie((grad_back, grad_across))
    came_grad = send(grad_back, (back, Z))

    product = times(came_out, weights)
    sent_on = jnp.where(is_early, product.astype(BF16), grad_across)
    arrived = send(sent_on, (to_late, 0), (across, Z))
    late_out = (product + came_level.astype(F32)).astype(BF16)
    second_out = jnp.where(is_early, came_out, late_out)
    product = times_t(jnp.where(is_early, came_level, came_grad), weights)
    second_grad = jnp.where(is_early, came_grad.astype(F32) + product, product).astype(BF16)

    everyone = [(s, s) for s in range(count)]

    def hop(value, mask):
        return send(value, (everyone, mask))

    orders = ((Y_NEAR, Y_FAR, Z), (Y_FAR, Z, Y_NEAR), (Z, Y_NEAR, Y_FAR))
    held_rows = [second_out, second_grad, arrived]
    masks = [[0], [0], [0]]
    for step in range(2):
        came = [hop(x, orders[k][step]) for k, x in enumerate(held_rows)]
        held_rows = [jnp.concatenate([x, y], axis=0) for x, y in zip(held_rows, came)]
        masks = [m + [k ^ order[step] for k in m] for m, order in zip(masks, orders)]
    last = [hop(x, orders[k][2]) for k, x in enumerate(held_rows)]
    plan = [[(k, m) for m in some] for k, some in enumerate(masks)]
    last_plan = [[(k, m ^ orders[k][2]) for k, m in blocks] for blocks in plan]
    partner = lambda plans: [[(k, m ^ CORE) for k, m in blocks] for blocks in plans]

    outs, grads = first_tick(
        is_early, section_inputs, mirror_held, section_cotangents, join_weights
    )
    near = [hop(x, CORE) for x in held_rows]
    here = jnp.reshape(replica, (1,))
    targets = place(here, held_rows + near, plan + partner(plan), (outs, grads), rows)
    last, targets = tie((last, targets))
    far = [hop(x, CORE) for x in last]
    targets = place(here, last, last_plan, targets, rows)
    return tuple(place(here, far, partner(last_plan), targets, rows))


def solution(mesh):
    in_specs = (
        P("section", None, None),
        P("section", None, None),
        P("section", None, None),
        P(),
        P(),
        P("section", None, None),
    )
    out_specs = (
        P(("dp", "section"), None, None, None),
        P(("dp", "section"), None, None, None),
        P(("dp", "section"), None, None),
    )
    return jax.shard_map(local, mesh=mesh, in_specs=in_specs, out_specs=out_specs, check_vma=False)
```

time: 71.6 us -> 70.8 us (0.989)
  waiting for transfers between devices: 9.49 us -> 13.1 us
  matrix products: 9.09 us -> 6.03 us
  local copies, waits for them, and re-layouts: 1.07 us -> 0.06 us
  other arithmetic: 1.1 us -> 0.13 us
    ppermute x20 -> x19, waiting for transfers between devices: 9.49 us -> 13.1 us  [send(): return lax.ppermute(value, AXES, chosen)]
    dot_general x3 -> x2, matrix products: 5.24 us -> 3.16 us  [times(): return jnp.dot(left, weights, preferred_element_type=F32)]
    dynamic_slice x1 -> x0, local copies, waits for them, and re-layouts: 1.06 us -> none  [part(): return lax.dynamic_slice_in_dim(whole, of * rows, rows, 0)]
    dot_general x2, matrix products: 3.85 us -> 2.87 us  [times_t(): lax.dot_general(left, weights, (((1,), (1,)), ((), ())), preferred_elemen...]
    select_n x1 -> x0, other arithmetic: 0.93 us -> none  [local(): arrived = jnp.where(position == 0, loss_part, came_across)]
    pallas_call x2 -> x3, Pallas kernels: 4.41 us -> 5.01 us  [place(): pl.pallas_call(functools.partial(place_kernel, plan, rows), in_specs=[pl....]
    ppermute x20 -> x19, starting transfers between devices: 36.8 us -> 36.9 us  [send(): return lax.ppermute(value, AXES, chosen)]
  transfers between devices with their start and end apart: 20 -> 19, of which waited for: 4 -> 6; matrix products, arithmetic and copies ran while one was open for 14% -> 5% of each run, Pallas kernels for 16% -> 17%
where the time goes in v4:
time: 70.8 us; the launch traced here: 70.5 us
  starting transfers between devices  36.9 us (52%)
  Pallas kernels  13.3 us (19%)
  waiting for transfers between devices  13.1 us (19%)
  matrix products  6.03 us (9%)
  between operations  0.95 us (1%)
    ppermute x19, starting transfers between devices, send(): return lax.ppermute(value, AXES, chosen)  36.9 us
    ppermute x19, waiting for transfers between devices, send(): return lax.ppermute(value, AXES, chosen)  13.1 us
    pallas_call x1, Pallas kernels, first_tick(): pl.pallas_call(first_kernel, grid=(4,), in_specs=[pl.BlockSpec(memory_spa...  8.33 us
    pallas_call x3, Pallas kernels, place(): pl.pallas_call(functools.partial(place_kernel, plan, rows), in_specs=[pl....  5.01 us
    dot_general x2, matrix products, times(): return jnp.dot(left, weights, preferred_element_type=F32)  3.16 us
    dot_general x2, matrix products, times_t(): lax.dot_general(left, weights, (((1,), (1,)), ((), ())), preferred_elemen...  2.87 us
  transfers between devices with their start and end apart: 19, of which 6 were waited for; matrix products, arithmetic and copies ran while one was open for 5% of the time, Pallas kernels for 17%

profile of v4, /device:TPU:1, one launch (start us, length us, event | category | flops | bytes accessed | tf_op | source)
XLA Modules:
  0.0 70.5 jit_solution(1155899382369784488)
XLA Ops:
  0.6 0.0 copy-start
  0.7 2.6 %bitcast_select_fusion = (bf16[48,1152]{1,0:T(8,128)(2,1)S(1)}, bf16[48,1152]{1,0:T(8,128)(2,1)S(1)}) fusion(pred[]{:T(512)S(6)} %eq.14, bf16[1,768,1152]{2,1,0:T(8,128)(2,1)} %g_ref.1, s32[]{:T(128)S(6)} %select_n.77, bf16[1,768,1152]{2,1,0:T(8,128)(2,1)} %h_ref.1, bf16[768,1152]{1,0:T(8,128)(2,1)} %param.9, pred[]{:T(512)S(6)} %eq.15, ...), kind=kOutput, calls=%fused_computation.24 | convolution fusion | flops 127789056 | bytes 3430400 | tf_op jit(solution)/shard_map/dot_general | solution.py:23
  3.2 5.3 %collective-permute-start.1 = (bf16[48,1152]{1,0:T(8,128)(2,1)S(1)}, bf16[48,1152]{1,0:T(8,128)(2,1)S(1)}, u32[]{:S(2)}, u32[]{:S(2)}) collective-permute-start(bf16[48,1152]{1,0:T(8,128)(2,1)S(1)} %get-tuple-element.39), channel_id=1, source_target_pairs={{0,24},{1,25},{2,26},{3,27},{4,28},{5,29},{6,30},{7,31},{8,16},{9,... | collective-permute-start | bytes 331784 | tf_op jit(solution)/shard_map/ppermute | solution.py:137
  8.5 0.0 copy-done
  8.5 2.0 %broadcast_select_fusion = (bf16[48,1152]{1,0:T(8,128)(2,1)S(1)}, bf16[48,1152]{1,0:T(8,128)(2,1)S(1)}) fusion(pred[]{:T(512)S(6)} %eq.17, bf16[768,1152]{1,0:T(8,128)(2,1)} %param.10, s32[]{:T(128)S(6)} %select_n.77, pred[]{:T(512)S(6)} %eq.16, bf16[1,1152,1152]{2,1,0:T(8,128)(2,1)S(1)} %copy-done, pred[]{:T(512)S(6)} %eq.14, ...), kind=kOutput, calls=%fused_computation.29 | convolution fusion | flops 127789056 | bytes 3320832 | tf_op jit(solution)/shard_map/dot_general | solution.py:27
  10.5 0.1 collective-permute-start.5
  10.6 4.4 %collective-permute-start = (bf16[48,1152]{1,0:T(8,128)(2,1)S(1)}, bf16[48,1152]{1,0:T(8,128)(2,1)S(1)}, u32[]{:S(2)}, u32[]{:S(2)}) collective-permute-start(bf16[48,1152]{1,0:T(8,128)(2,1)S(1)} %get-tuple-element.40), channel_id=1, source_target_pairs={{0,40},{1,41},{2,42},{3,43},{4,44},{5,45},{6,46},{7,47},{8,32},{9,... | collective-permute-start | bytes 331784 | tf_op jit(solution)/shard_map/ppermute | solution.py:137
  15.0 0.0 collective-permute-done.1
  15.0 6.1 %collective-permute-done.5 = bf16[48,1152]{1,0:T(8,128)(2,1)S(1)} collective-permute-done((bf16[48,1152]{1,0:T(8,128)(2,1)S(1)}, bf16[48,1152]{1,0:T(8,128)(2,1)S(1)}, u32[]{:S(2)}, u32[]{:S(2)}) %collective-permute-start.5) | collective-permute-done | bytes 110624 | tf_op jit(solution)/shard_map/ppermute | solution.py:137
  21.2 0.9 %fusion.10 = bf16[48,1152]{1,0:T(8,128)(2,1)S(1)} fusion(bf16[1,1152,1152]{2,1,0:T(8,128)(2,1)S(1)} %copy-done, bf16[48,1152]{1,0:T(8,128)(2,1)S(1)} %collective-permute-done.5, bf16[48,1152]{1,0:T(8,128)(2,1)S(1)} %collective-permute-done.1, pred[]{:T(512)S(6)} %eq.14), kind=kOutput, calls=%fused_computation.11 | convolution fusion | flops 127678464 | bytes 2985985 | tf_op jit(solution)/shard_map/dot_general | solution.py:27
  22.1 2.8 %collective-permute-start.6 = (bf16[48,1152]{1,0:T(8,128)(2,1)S(1)}, bf16[48,1152]{1,0:T(8,128)(2,1)S(1)}, u32[]{:S(2)}, u32[]{:S(2)}) collective-permute-start(bf16[48,1152]{1,0:T(8,128)(2,1)S(1)} %fusion.10), channel_id=1, source_target_pairs={{0,6},{1,7},{2,4},{3,5},{4,2},{5,3},{6,0},{7,1},{8,14},{9,15},{10,... | collective-permute-start | bytes 331784 | tf_op jit(solution)/shard_map/ppermute | solution.py:137
  24.9 0.0 collective-permute-done
  24.9 0.6 convert_select_fusion
  25.5 3.6 %collective-permute-start.9 = (bf16[48,1152]{1,0:T(8,128)(2,1)S(1)}, bf16[48,1152]{1,0:T(8,128)(2,1)S(1)}, u32[]{:S(2)}, u32[]{:S(2)}) collective-permute-start(bf16[48,1152]{1,0:T(8,128)(2,1)S(1)} %get-tuple-element.37), channel_id=1, source_target_pairs={{0,16},{1,17},{2,18},{3,19},{4,20},{5,21},{6,22},{7,23},{8,24},{9,... | collective-permute-start | bytes 331784 | tf_op jit(solution)/shard_map/ppermute | solution.py:137
  29.0 0.0 collective-permute-start.2
  29.0 0.0 collective-permute-done.6
  29.1 1.2 %collective-permute-start.7 = (bf16[96,1152]{1,0:T(8,128)(2,1)S(1)}, bf16[96,1152]{1,0:T(8,128)(2,1)S(1)}, u32[]{:S(2)}, u32[]{:S(2)}) collective-permute-start(bf16[96,1152]{1,0:T(8,128)(2,1)S(1)} %pad_maximum_fusion.3), channel_id=1, source_target_pairs={{0,8},{1,9},{2,10},{3,11},{4,12},{5,13},{6,14},{7,15},{8,0},{9,1},... | collective-permute-start | bytes 663560 | tf_op jit(solution)/shard_map/ppermute | solution.py:137
  30.2 2.4 %collective-permute-done.2 = bf16[48,1152]{1,0:T(8,128)(2,1)S(1)} collective-permute-done((bf16[48,1152]{1,0:T(8,128)(2,1)S(1)}, bf16[48,1152]{1,0:T(8,128)(2,1)S(1)}, u32[]{:S(2)}, u32[]{:S(2)}) %collective-permute-start.2) | collective-permute-done | bytes 110624 | tf_op jit(solution)/shard_map/ppermute | solution.py:137
  32.7 1.8 %collective-permute-start.3 = (bf16[96,1152]{1,0:T(8,128)(2,1)S(1)}, bf16[96,1152]{1,0:T(8,128)(2,1)S(1)}, u32[]{:S(2)}, u32[]{:S(2)}) collective-permute-start(bf16[96,1152]{1,0:T(8,128)(2,1)S(1)} %pad_maximum_fusion.2), channel_id=1, source_target_pairs={{0,6},{1,7},{2,4},{3,5},{4,2},{5,3},{6,0},{7,1},{8,14},{9,15},{10,... | collective-permute-start | bytes 663560 | tf_op jit(solution)/shard_map/ppermute | solution.py:137
  34.4 0.0 collective-permute-done.9
  34.4 5.0 %collective-permute-start.10 = (bf16[48,1152]{1,0:T(8,128)(2,1)S(1)}, bf16[48,1152]{1,0:T(8,128)(2,1)S(1)}, u32[]{:S(2)}, u32[]{:S(2)}) collective-permute-start(bf16[48,1152]{1,0:T(8,128)(2,1)S(1)} %collective-permute-done.9), channel_id=1, source_target_pairs={{0,8},{1,9},{2,10},{3,11},{4,12},{5,13},{6,14},{7,15},{8,0},{9,1},... | collective-permute-start | bytes 331784 | tf_op jit(solution)/shard_map/ppermute | solution.py:137
  39.4 2.4 %collective-permute-done.10 = bf16[48,1152]{1,0:T(8,128)(2,1)S(1)} collective-permute-done((bf16[48,1152]{1,0:T(8,128)(2,1)S(1)}, bf16[48,1152]{1,0:T(8,128)(2,1)S(1)}, u32[]{:S(2)}, u32[]{:S(2)}) %collective-permute-start.10) | collective-permute-done | bytes 110624 | tf_op jit(solution)/shard_map/ppermute | solution.py:137
  41.8 0.3 collective-permute-start.11
  42.2 0.0 collective-permute-done.7
  42.2 3.2 %collective-permute-start.14 = (bf16[192,1152]{1,0:T(8,128)(2,1)S(1)}, bf16[192,1152]{1,0:T(8,128)(2,1)S(1)}, u32[]{:S(2)}, u32[]{:S(2)}) collective-permute-start(bf16[192,1152]{1,0:T(8,128)(2,1)S(1)} %pad_maximum_fusion.1.refs_1_), channel_id=1, source_target_pairs={{0,1},{1,0},{2,3},{3,2},{4,5},{5,4},{6,7},{7,6},{8,9},{9,8},{10,11... | collective-permute-start | bytes 1327112 | tf_op jit(solution)/shard_map/ppermute | solution.py:137
  45.4 0.0 collective-permute-done.3
  45.4 0.1 collective-permute-start.13
  45.5 1.2 %collective-permute-done.11 = bf16[96,1152]{1,0:T(8,128)(2,1)S(1)} collective-permute-done((bf16[96,1152]{1,0:T(8,128)(2,1)S(1)}, bf16[96,1152]{1,0:T(8,128)(2,1)S(1)}, u32[]{:S(2)}, u32[]{:S(2)}) %collective-permute-start.11) | collective-permute-done | bytes 221216 | tf_op jit(solution)/shard_map/ppermute | solution.py:137
  46.7 3.6 %collective-permute-start.15 = (bf16[192,1152]{1,0:T(8,128)(2,1)S(1)}, bf16[192,1152]{1,0:T(8,128)(2,1)}, u32[]{:S(2)}, u32[]{:S(2)}) collective-permute-start(bf16[192,1152]{1,0:T(8,128)(2,1)S(1)} %constant_dynamic-update-slice_fusion.refs_2_), channel_id=1, source_target_pairs={{0,1},{1,0},{2,3},{3,2},{4,5},{5,4},{6,7},{7,6},{8,9},{9,8},{10,11... | collective-permute-start | bytes 1327112 | tf_op jit(solution)/shard_map/ppermute | solution.py:137
  50.3 0.7 collective-permute-start.8
  51.0 1.7 %collective-permute-start.4 = (bf16[192,1152]{1,0:T(8,128)(2,1)S(1)}, bf16[192,1152]{1,0:T(8,128)(2,1)S(1)}, u32[]{:S(2)}, u32[]{:S(2)}) collective-permute-start(bf16[192,1152]{1,0:T(8,128)(2,1)S(1)} %pad_maximum_fusion.refs_0_), channel_id=1, source_target_pairs={{0,8},{1,9},{2,10},{3,11},{4,12},{5,13},{6,14},{7,15},{8,0},{9,1},... | collective-permute-start | bytes 1327112 | tf_op jit(solution)/shard_map/ppermute | solution.py:137
  52.7 0.0 collective-permute-done.14.refs_4_
  52.7 1.6 %collective-permute-start.12 = (bf16[192,1152]{1,0:T(8,128)(2,1)S(1)}, bf16[192,1152]{1,0:T(8,128)(2,1)S(1)}, u32[]{:S(2)}, u32[]{:S(2)}) collective-permute-start(bf16[192,1152]{1,0:T(8,128)(2,1)S(1)} %constant_dynamic-update-slice_fusion.refs_2_), channel_id=1, source_target_pairs={{0,6},{1,7},{2,4},{3,5},{4,2},{5,3},{6,0},{7,1},{8,14},{9,15},{10,... | collective-permute-start | bytes 1327112 | tf_op jit(solution)/shard_map/ppermute | solution.py:137
  54.4 8.3 %first_tick.1 = (bf16[1,2,768,1152]{3,2,1,0:T(8,128)(2,1)}, bf16[1,2,768,1152]{3,2,1,0:T(8,128)(2,1)}) custom-call(s32[1]{0:T(128)} %bitcast.6.early_ref, bf16[1,768,1152]{2,1,0:T(8,128)(2,1)} %a_ref.1, bf16[1,768,1152]{2,1,0:T(8,128)(2,1)} %h_ref.1, bf16[1,768,1152]{2,1,0:T(8,128)(2,1)} %g_ref.1, bf16[1,1152,1152]{2,1,0:T(8,128)(2,1)} %w_ref.1), custom_call_target="tpu_custom_call" | custom-call | flops 4076863488 | bytes 12386304 | tf_op jit(solution)/shard_map/first_tick/pallas_call | solution.py:56
  62.7 0.0 collective-permute-done.13.refs_3_
  62.7 0.0 collective-permute-done.15.refs_5_
  62.7 2.7 %shard_map.85 = (bf16[1,2,768,1152]{3,2,1,0:T(8,128)(2,1)}, bf16[1,2,768,1152]{3,2,1,0:T(8,128)(2,1)}, bf16[1,768,1152]{2,1,0:T(8,128)(2,1)}) custom-call(s32[1]{0:T(128)} %bitcast.replica_ref, bf16[192,1152]{1,0:T(8,128)(2,1)S(1)} %pad_maximum_fusion.refs_0_, ...), custom_call_target="tpu_custom_call", output_to_operand_aliasing={{0}: (7, {}), {1}: (8, {})} | custom-call | bytes 5308416 | tf_op jit(solution)/shard_map/pallas_call | solution.py:103
  65.4 0.0 collective-permute-done.8.refs_1_
  65.4 0.0 collective-permute-done.4.refs_0_
  65.4 0.0 collective-permute-done.12.refs_2_
  65.5 1.1 %collective-permute-start.16 = (bf16[192,1152]{1,0:T(8,128)(2,1)S(1)}, bf16[192,1152]{1,0:T(8,128)(2,1)S(1)}, u32[]{:S(2)}, u32[]{:S(2)}) collective-permute-start(bf16[192,1152]{1,0:T(8,128)(2,1)S(1)} %collective-permute-done.4.refs_0_), channel_id=1, source_target_pairs={{0,1},{1,0},{2,3},{3,2},{4,5},{5,4},{6,7},{7,6},{8,9},{9,8},{10,11... | collective-permute-start | bytes 1327112 | tf_op jit(solution)/shard_map/ppermute | solution.py:137
  66.5 0.1 collective-permute-start.17
  66.6 0.5 collective-permute-start.18
  67.0 1.1 %shard_map.86 = (bf16[1,2,768,1152]{3,2,1,0:T(8,128)(2,1)}, bf16[1,2,768,1152]{3,2,1,0:T(8,128)(2,1)}, bf16[1,768,1152]{2,1,0:T(8,128)(2,1)}) custom-call(s32[1]{0:T(128)} %bitcast.replica_ref, bf16[192,1152]{1,0:T(8,128)(2,1)S(1)} %collective-permute-done.4.refs_0_, ...), custom_call_target="tpu_custom_call", output_to_operand_aliasing={{0}: (4, {}), {1}: (5, {}), {2}: (6, {})} | custom-call | bytes 2654208 | tf_op jit(solution)/shard_map/pallas_call | solution.py:103
  68.2 0.0 collective-permute-done.16.refs_0_
  68.2 0.4 collective-permute-done.17.refs_1_
  68.6 0.6 collective-permute-done.18.refs_2_
  69.2 1.1 %shard_map.87 = (bf16[1,2,768,1152]{3,2,1,0:T(8,128)(2,1)}, bf16[1,2,768,1152]{3,2,1,0:T(8,128)(2,1)}, bf16[1,768,1152]{2,1,0:T(8,128)(2,1)}) custom-call(s32[1]{0:T(128)} %bitcast.replica_ref, bf16[192,1152]{1,0:T(8,128)(2,1)S(1)} %collective-permute-done.16.refs_0_, ...), custom_call_target="tpu_custom_call", output_to_operand_aliasing={{0}: (4, {}), {1}: (5, {}), {2}: (6, {})} | custom-call | bytes 2654208 | tf_op jit(solution)/shard_map/pallas_call | solution.py:103
  (8 shorter events, 0.2 us)
Async XLA Ops:
  0.6 7.9 %copy-start = (bf16[1,1152,1152]{2,1,0:T(8,128)(2,1)S(1)}, bf16[1,1152,1152]{2,1,0:T(8,128)(2,1)}, u32[]{:S(2)}) copy-start(bf16[1,1152,1152]{2,1,0:T(8,128)(2,1)} %w_ref.1) | copy-start | bytes 7962628
  3.2 11.8 %collective-permute-start.1 = (bf16[48,1152]{1,0:T(8,128)(2,1)S(1)}, bf16[48,1152]{1,0:T(8,128)(2,1)S(1)}, u32[]{:S(2)}, u32[]{:S(2)}) collective-permute-start(bf16[48,1152]{1,0:T(8,128)(2,1)S(1)} %get-tuple-element.39), channel_id=1, source_target_pairs={{0,24},{1,25},{2,26},{3,27},{4,28},{5,29},{6,30},{7,31},{8,16},{9,... | collective-permute-start | bytes 331784 | tf_op jit(solution)/shard_map/ppermute | solution.py:137
  10.5 10.7 %collective-permute-start.5 = (bf16[48,1152]{1,0:T(8,128)(2,1)S(1)}, bf16[48,1152]{1,0:T(8,128)(2,1)S(1)}, u32[]{:S(2)}, u32[]{:S(2)}) collective-permute-start(bf16[48,1152]{1,0:T(8,128)(2,1)S(1)} %get-tuple-element.19), channel_id=1, source_target_pairs={{32,8},{33,9},{34,10},{35,11},{36,12},{37,13},{38,14},{39,15},{40,... | collective-permute-start | bytes 331784 | tf_op jit(solution)/shard_map/ppermute | solution.py:137
  10.6 14.3 %collective-permute-start = (bf16[48,1152]{1,0:T(8,128)(2,1)S(1)}, bf16[48,1152]{1,0:T(8,128)(2,1)S(1)}, u32[]{:S(2)}, u32[]{:S(2)}) collective-permute-start(bf16[48,1152]{1,0:T(8,128)(2,1)S(1)} %get-tuple-element.40), channel_id=1, source_target_pairs={{0,40},{1,41},{2,42},{3,43},{4,44},{5,45},{6,46},{7,47},{8,32},{9,... | collective-permute-start | bytes 331784 | tf_op jit(solution)/shard_map/ppermute | solution.py:137
  22.1 7.0 %collective-permute-start.6 = (bf16[48,1152]{1,0:T(8,128)(2,1)S(1)}, bf16[48,1152]{1,0:T(8,128)(2,1)S(1)}, u32[]{:S(2)}, u32[]{:S(2)}) collective-permute-start(bf16[48,1152]{1,0:T(8,128)(2,1)S(1)} %fusion.10), channel_id=1, source_target_pairs={{0,6},{1,7},{2,4},{3,5},{4,2},{5,3},{6,0},{7,1},{8,14},{9,15},{10,... | collective-permute-start | bytes 331784 | tf_op jit(solution)/shard_map/ppermute | solution.py:137
  25.5 9.0 %collective-permute-start.9 = (bf16[48,1152]{1,0:T(8,128)(2,1)S(1)}, bf16[48,1152]{1,0:T(8,128)(2,1)S(1)}, u32[]{:S(2)}, u32[]{:S(2)}) collective-permute-start(bf16[48,1152]{1,0:T(8,128)(2,1)S(1)} %get-tuple-element.37), channel_id=1, source_target_pairs={{0,16},{1,17},{2,18},{3,19},{4,20},{5,21},{6,22},{7,23},{8,24},{9,... | collective-permute-start | bytes 331784 | tf_op jit(solution)/shard_map/ppermute | solution.py:137
  29.0 3.6 %collective-permute-start.2 = (bf16[48,1152]{1,0:T(8,128)(2,1)S(1)}, bf16[48,1152]{1,0:T(8,128)(2,1)S(1)}, u32[]{:S(2)}, u32[]{:S(2)}) collective-permute-start(bf16[48,1152]{1,0:T(8,128)(2,1)S(1)} %get-tuple-element.38), channel_id=1, source_target_pairs={{0,2},{1,3},{2,0},{3,1},{4,6},{5,7},{6,4},{7,5},{8,10},{9,11},{10,... | collective-permute-start | bytes 331784 | tf_op jit(solution)/shard_map/ppermute | solution.py:137
  29.1 13.1 %collective-permute-start.7 = (bf16[96,1152]{1,0:T(8,128)(2,1)S(1)}, bf16[96,1152]{1,0:T(8,128)(2,1)S(1)}, u32[]{:S(2)}, u32[]{:S(2)}) collective-permute-start(bf16[96,1152]{1,0:T(8,128)(2,1)S(1)} %pad_maximum_fusion.3), channel_id=1, source_target_pairs={{0,8},{1,9},{2,10},{3,11},{4,12},{5,13},{6,14},{7,15},{8,0},{9,1},... | collective-permute-start | bytes 663560 | tf_op jit(solution)/shard_map/ppermute | solution.py:137
  32.7 12.7 %collective-permute-start.3 = (bf16[96,1152]{1,0:T(8,128)(2,1)S(1)}, bf16[96,1152]{1,0:T(8,128)(2,1)S(1)}, u32[]{:S(2)}, u32[]{:S(2)}) collective-permute-start(bf16[96,1152]{1,0:T(8,128)(2,1)S(1)} %pad_maximum_fusion.2), channel_id=1, source_target_pairs={{0,6},{1,7},{2,4},{3,5},{4,2},{5,3},{6,0},{7,1},{8,14},{9,15},{10,... | collective-permute-start | bytes 663560 | tf_op jit(solution)/shard_map/ppermute | solution.py:137
  34.4 7.4 %collective-permute-start.10 = (bf16[48,1152]{1,0:T(8,128)(2,1)S(1)}, bf16[48,1152]{1,0:T(8,128)(2,1)S(1)}, u32[]{:S(2)}, u32[]{:S(2)}) collective-permute-start(bf16[48,1152]{1,0:T(8,128)(2,1)S(1)} %collective-permute-done.9), channel_id=1, source_target_pairs={{0,8},{1,9},{2,10},{3,11},{4,12},{5,13},{6,14},{7,15},{8,0},{9,1},... | collective-permute-start | bytes 331784 | tf_op jit(solution)/shard_map/ppermute | solution.py:137
  41.8 4.9 %collective-permute-start.11 = (bf16[96,1152]{1,0:T(8,128)(2,1)S(1)}, bf16[96,1152]{1,0:T(8,128)(2,1)S(1)}, u32[]{:S(2)}, u32[]{:S(2)}) collective-permute-start(bf16[96,1152]{1,0:T(8,128)(2,1)S(1)} %pad_maximum_fusion.4), channel_id=1, source_target_pairs={{0,2},{1,3},{2,0},{3,1},{4,6},{5,7},{6,4},{7,5},{8,10},{9,11},{10,... | collective-permute-start | bytes 663560 | tf_op jit(solution)/shard_map/ppermute | solution.py:137
  42.2 10.5 %collective-permute-start.14 = (bf16[192,1152]{1,0:T(8,128)(2,1)S(1)}, bf16[192,1152]{1,0:T(8,128)(2,1)S(1)}, u32[]{:S(2)}, u32[]{:S(2)}) collective-permute-start(bf16[192,1152]{1,0:T(8,128)(2,1)S(1)} %pad_maximum_fusion.1.refs_1_), channel_id=1, source_target_pairs={{0,1},{1,0},{2,3},{3,2},{4,5},{5,4},{6,7},{7,6},{8,9},{9,8},{10,11... | collective-permute-start | bytes 1327112 | tf_op jit(solution)/shard_map/ppermute | solution.py:137
  45.4 17.3 %collective-permute-start.13 = (bf16[192,1152]{1,0:T(8,128)(2,1)S(1)}, bf16[192,1152]{1,0:T(8,128)(2,1)S(1)}, u32[]{:S(2)}, u32[]{:S(2)}) collective-permute-start(bf16[192,1152]{1,0:T(8,128)(2,1)S(1)} %pad_maximum_fusion.refs_0_), channel_id=1, source_target_pairs={{0,1},{1,0},{2,3},{3,2},{4,5},{5,4},{6,7},{7,6},{8,9},{9,8},{10,11... | collective-permute-start | bytes 1327112 | tf_op jit(solution)/shard_map/ppermute | solution.py:137
  46.7 16.0 %collective-permute-start.15 = (bf16[192,1152]{1,0:T(8,128)(2,1)S(1)}, bf16[192,1152]{1,0:T(8,128)(2,1)}, u32[]{:S(2)}, u32[]{:S(2)}) collective-permute-start(bf16[192,1152]{1,0:T(8,128)(2,1)S(1)} %constant_dynamic-update-slice_fusion.refs_2_), channel_id=1, source_target_pairs={{0,1},{1,0},{2,3},{3,2},{4,5},{5,4},{6,7},{7,6},{8,9},{9,8},{10,11... | collective-permute-start | bytes 1327112 | tf_op jit(solution)/shard_map/ppermute | solution.py:137
  50.3 15.1 %collective-permute-start.8 = (bf16[192,1152]{1,0:T(8,128)(2,1)S(1)}, bf16[192,1152]{1,0:T(8,128)(2,1)S(1)}, u32[]{:S(2)}, u32[]{:S(2)}) collective-permute-start(bf16[192,1152]{1,0:T(8,128)(2,1)S(1)} %pad_maximum_fusion.1.refs_1_), channel_id=1, source_target_pairs={{0,2},{1,3},{2,0},{3,1},{4,6},{5,7},{6,4},{7,5},{8,10},{9,11},{10,... | collective-permute-start | bytes 1327112 | tf_op jit(solution)/shard_map/ppermute | solution.py:137
  51.0 14.5 %collective-permute-start.4 = (bf16[192,1152]{1,0:T(8,128)(2,1)S(1)}, bf16[192,1152]{1,0:T(8,128)(2,1)S(1)}, u32[]{:S(2)}, u32[]{:S(2)}) collective-permute-start(bf16[192,1152]{1,0:T(8,128)(2,1)S(1)} %pad_maximum_fusion.refs_0_), channel_id=1, source_target_pairs={{0,8},{1,9},{2,10},{3,11},{4,12},{5,13},{6,14},{7,15},{8,0},{9,1},... | collective-permute-start | bytes 1327112 | tf_op jit(solution)/shard_map/ppermute | solution.py:137
  52.7 12.7 %collective-permute-start.12 = (bf16[192,1152]{1,0:T(8,128)(2,1)S(1)}, bf16[192,1152]{1,0:T(8,128)(2,1)S(1)}, u32[]{:S(2)}, u32[]{:S(2)}) collective-permute-start(bf16[192,1152]{1,0:T(8,128)(2,1)S(1)} %constant_dynamic-update-slice_fusion.refs_2_), channel_id=1, source_target_pairs={{0,6},{1,7},{2,4},{3,5},{4,2},{5,3},{6,0},{7,1},{8,14},{9,15},{10,... | collective-permute-start | bytes 1327112 | tf_op jit(solution)/shard_map/ppermute | solution.py:137
  65.5 2.7 %collective-permute-start.16 = (bf16[192,1152]{1,0:T(8,128)(2,1)S(1)}, bf16[192,1152]{1,0:T(8,128)(2,1)S(1)}, u32[]{:S(2)}, u32[]{:S(2)}) collective-permute-start(bf16[192,1152]{1,0:T(8,128)(2,1)S(1)} %collective-permute-done.4.refs_0_), channel_id=1, source_target_pairs={{0,1},{1,0},{2,3},{3,2},{4,5},{5,4},{6,7},{7,6},{8,9},{9,8},{10,11... | collective-permute-start | bytes 1327112 | tf_op jit(solution)/shard_map/ppermute | solution.py:137
  66.5 2.1 %collective-permute-start.17 = (bf16[192,1152]{1,0:T(8,128)(2,1)S(1)}, bf16[192,1152]{1,0:T(8,128)(2,1)S(1)}, u32[]{:S(2)}, u32[]{:S(2)}) collective-permute-start(bf16[192,1152]{1,0:T(8,128)(2,1)S(1)} %collective-permute-done.8.refs_1_), channel_id=1, source_target_pairs={{0,1},{1,0},{2,3},{3,2},{4,5},{5,4},{6,7},{7,6},{8,9},{9,8},{10,11... | collective-permute-start | bytes 1327112 | tf_op jit(solution)/shard_map/ppermute | solution.py:137
  66.6 2.6 %collective-permute-start.18 = (bf16[192,1152]{1,0:T(8,128)(2,1)S(1)}, bf16[192,1152]{1,0:T(8,128)(2,1)S(1)}, u32[]{:S(2)}, u32[]{:S(2)}) collective-permute-start(bf16[192,1152]{1,0:T(8,128)(2,1)S(1)} %collective-permute-done.12.refs_2_), channel_id=1, source_target_pairs={{0,1},{1,0},{2,3},{3,2},{4,5},{5,4},{6,7},{7,6},{8,9},{9,8},{10,11... | collective-permute-start | bytes 1327112 | tf_op jit(solution)/shard_map/ppermute | solution.py:137

commit v5 on v4

--- a/solution.py
+++ b/solution.py
@@ -27,55 +27,82 @@
     return lax.dot_general(left, weights, (((1,), (1,)), ((), ())), preferred_element_type=F32)
 
 
-def first_kernel(early_ref, a_ref, h_ref, g_ref, w_ref, out_ref, grad_ref, turned_ref):
-    early = early_ref[0] == 1
-
-    @pl.when(pl.program_id(0) == 0)
-    def _():
-        turned_ref[...] = w_ref[0].T
+def first_kernel(
+    spec_ref, a_ref, h_ref, g_ref, w_ref, out_ref, grad_ref, mine_ref, a_in, h_in, g_in, w_in, out_buf, grad_buf, in_sem, out_sem
+):
+    early = spec_ref[0] == 1
+    height, width = a_in.shape
+    start = pl.multiple_of(spec_ref[1] * height, height)
+    part = width // 4
+    rows = pl.ds(start, height)
+    come = [
+        pltpu.make_async_copy(ref.at[0, rows], buf, in_sem.at[n])
+        for n, (ref, buf) in enumerate(((h_ref, h_in), (g_ref, g_in), (a_ref, a_in)))
+    ]
+    turn = [
+        pltpu.make_async_copy(
+            w_ref.at[0, pl.ds(k * part, part)], w_in.at[pl.ds(k * part, part)], in_sem.at[3 + k]
+        )
+        for k in range(4)
+    ]
+
+    def go(buf, ref, n):
+        return [
+            pltpu.make_async_copy(buf, ref.at[0, 0, rows], out_sem.at[n]),
+            pltpu.make_async_copy(buf, mine_ref.at[n], out_sem.at[2 + n]),
+        ]
+
+    for copy in turn[:2] + come + turn[2:]:
+        copy.start()
+    for copy in turn + come:
+        copy.wait()
 
     @pl.when(early)
     def _():
-        out_ref[0, 0] = a_ref[0]
-        product = times(h_ref[0], turned_ref[...])
-        grad_ref[0, 0] = (g_ref[0].astype(F32) + product).astype(BF16)
+        for copy in go(a_in, out_ref, 0):
+            copy.start()
+        product = times_t(h_in[...], w_in[...])
+        grad_buf[...] = (g_in[...].astype(F32) + product).astype(BF16)
 
     @pl.when(jnp.logical_not(early))
     def _():
-        product = times(a_ref[0], w_ref[0])
-        out_ref[0, 0] = (product + h_ref[0].astype(F32)).astype(BF16)
-        grad_ref[0, 0] = times(g_ref[0], turned_ref[...]).astype(BF16)
-
-
-def first_tick(early, a, held, cot, weights):
+        product = times(a_in[...], w_in[...])
+        out_buf[...] = (product + h_in[...].astype(F32)).astype(BF16)
+        for copy in go(out_buf, out_ref, 0):
+            copy.start()
+        grad_buf[...] = times_t(g_in[...], w_in[...]).astype(BF16)
+
+    for copy in go(grad_buf, grad_ref, 1):
+        copy.start()
+    for copy in go(out_buf, out_ref, 0) + go(grad_buf, grad_ref, 1):
+        copy.wait()
+
+
+def first_tick(early, core, a, held, cot, weights):
     _, height, width = a.shape
-    block = height // 4
-    rows = pl.BlockSpec((1, block, width), lambda i: (0, i, 0))
-    wide = pl.BlockSpec((1, 1, block, width), lambda i: (0, 0, i, 0))
+    half = height // 2
+    anywhere = pl.BlockSpec(memory_space=pl.ANY)
     both = jax.ShapeDtypeStruct((1, 2, height, width), BF16)
     return pl.pallas_call(
         first_kernel,
-        grid=(4,),
-        in_specs=[
-            pl.BlockSpec(memory_space=pltpu.SMEM),
-            rows,
-            rows,
-            rows,
-            pl.BlockSpec((1, width, width), lambda i: (0, 0, 0)),
-        ],
-        out_specs=[wide, wide],
-        out_shape=[both, both],
-        scratch_shapes=[pltpu.VMEM((width, width), BF16)],
+        in_specs=[pl.BlockSpec(memory_space=pltpu.SMEM)] + [anywhere] * 4,
+        out_specs=[anywhere] * 3,
+        out_shape=[both, both, jax.ShapeDtypeStruct((2, half, width), BF16)],
+        scratch_shapes=[pltpu.VMEM((half, width), BF16)] * 3
+        + [pltpu.VMEM((width, width), BF16)]
+        + [pltpu.VMEM((half, width), BF16)] * 2
+        + [pltpu.SemaphoreType.DMA((7,)), pltpu.SemaphoreType.DMA((4,))],
         cost_estimate=pl.CostEstimate(
-            flops=4 * height * width * width, bytes_accessed=14 * height * width, transcendentals=0
+            flops=2 * height * width * width, bytes_accessed=8 * height * width, transcendentals=0
         ),
         compiler_params=pltpu.CompilerParams(vmem_limit_bytes=60 << 20),
         name="first_tick",
-    )(jnp.reshape(early.astype(jnp.int32), (1,)), a, held, cot, weights)
-
-
-def place_kernel(plan, rows, replica_ref, *refs):
+    )(jnp.stack([early.astype(jnp.int32), core]), a, held, cot, weights)
+
+
+def place_kernel(plan, rows, halves, replica_ref, *refs):
     pieces, targets, sem = refs[: len(plan)], refs[-4:-1], refs[-1]
+    other = refs[len(plan)] if halves else None
     replica = replica_ref[0]
     views = (targets[0].at[0, 1], targets[1].at[0, 1], targets[2].at[0])
     copies = []
@@ -89,31 +116,39 @@
                     sem.at[len(copies)],
                 )
             )
+    if halves:
+        half = other.shape[1]
+        at = pl.ds(pl.multiple_of((1 - replica % 2) * half, half), half)
+        for k in range(2):
+            view = targets[k].at[0, 0, at]
+            copies.append(pltpu.make_async_copy(other.at[k], view, sem.at[len(copies)]))
     for copy in copies:
         copy.start()
     for copy in copies:
         copy.wait()
 
 
-def place(replica, pieces, plan, targets, rows):
+def place(replica, pieces, plan, targets, rows, halves=()):
     anywhere = pl.BlockSpec(memory_space=pl.ANY)
     width = targets[0].shape[-1]
     arrived = jax.ShapeDtypeStruct((1,) + targets[0].shape[2:], BF16)
     blocks = sum(len(some) for some in plan)
     return pl.pallas_call(
-        functools.partial(place_kernel, plan, rows),
+        functools.partial(place_kernel, plan, rows, len(halves) > 0),
         in_specs=[pl.BlockSpec(memory_space=pltpu.SMEM)]
-        + [pl.BlockSpec(memory_space=pltpu.VMEM)] * len(pieces)
+        + [pl.BlockSpec(memory_space=pltpu.VMEM)] * (len(pieces) + len(halves))
         + [anywhere] * len(targets),
         out_specs=[anywhere] * 3,
         out_shape=[jax.ShapeDtypeStruct(x.shape, BF16) for x in targets[:2]] + [arrived],
-        scratch_shapes=[pltpu.SemaphoreType.DMA((blocks,))],
-        input_output_aliases={1 + len(pieces) + k: k for k in range(len(targets))},
+        scratch_shapes=[pltpu.SemaphoreType.DMA((blocks + 2 * len(halves),))],
+        input_output_aliases={
+            1 + len(pieces) + len(halves) + k: k for k in range(len(targets))
+        },
         compiler_params=pltpu.CompilerParams(vmem_limit_bytes=8 << 20),
         cost_estimate=pl.CostEstimate(
             flops=0, bytes_accessed=4 * blocks * rows * width, transcendentals=0
         ),
-    )(replica, *pieces, *targets)
+    )(replica, *pieces, *halves, *targets)
 
 
 def local(
@@ -170,7 +205,8 @@
     product = times(came_out, weights)
     sent_on = jnp.where(is_early, product.astype(BF16), grad_across)
     arrived = send(sent_on, (to_late, 0), (across, Z))
-    late_out = (product + came_level.astype(F32)).astype(BF16)
+    came_out = tie(came_out)
+    late_out = (times(came_out, weights) + came_level.astype(F32)).astype(BF16)
     second_out = jnp.where(is_early, came_out, late_out)
     product = times_t(jnp.where(is_early, came_level, came_grad), weights)
     second_grad = jnp.where(is_early, came_grad.astype(F32) + product, product).astype(BF16)
@@ -192,16 +228,18 @@
     last_plan = [[(k, m ^ orders[k][2]) for k, m in blocks] for blocks in plan]
     partner = lambda plans: [[(k, m ^ CORE) for k, m in blocks] for blocks in plans]
 
-    outs, grads = first_tick(
-        is_early, section_inputs, mirror_held, section_cotangents, join_weights
+    outs, grads, mine = first_tick(
+        is_early, replica % 2, section_inputs, mirror_held, section_cotangents, join_weights
     )
+    other = hop(mine, CORE)
     near = [hop(x, CORE) for x in held_rows]
     here = jnp.reshape(replica, (1,))
     targets = place(here, held_rows + near, plan + partner(plan), (outs, grads), rows)
-    last, targets = tie((last, targets))
+    targets = place(here, [], [], targets, rows, (other,))
     far = [hop(x, CORE) for x in last]
-    targets = place(here, last, last_plan, targets, rows)
-    return tuple(place(here, far, partner(last_plan), targets, rows))
+    far_plan = partner(last_plan)
+    targets = place(here, last + far[:2], last_plan + far_plan[:2], targets, rows)
+    return tuple(place(here, far[2:], far_plan[2:], targets, rows))
 
 
 def solution(mesh):

time: 70.8 us -> 71.4 us (level)
  starting transfers between devices: 36.9 us -> 39.6 us
  Pallas kernels: 13.3 us -> 11.4 us
  waiting for transfers between devices: 13.1 us -> 11.8 us
    ppermute x19 -> x20, starting transfers between devices: 36.9 us -> 39.6 us  [send(): return lax.ppermute(value, AXES, chosen)]
    pallas_call x4 -> x5, Pallas kernels: 13.3 us -> 11.4 us  [the longest x1 6.12 us: first_tick(): pl.pallas_call(first_kernel, in_specs=[pl.BlockSpec(memory_space=pltpu.SM...]
    ppermute x19 -> x20, waiting for transfers between devices: 13.1 us -> 11.8 us  [send(): return lax.ppermute(value, AXES, chosen)]
    dot_general x2 -> x3, matrix products: 3.16 us -> 3.73 us  [times(): return jnp.dot(left, weights, preferred_element_type=F32)]
  transfers between devices with their start and end apart: 19 -> 20, of which waited for: 6 -> 3; matrix products, arithmetic and copies ran while one was open for 5% -> 7% of each run, Pallas kernels for 17% -> 15%
where the time goes in v5:
time: 71.4 us; the launch traced here: 71.2 us
  starting transfers between devices  39.6 us (55%)
  waiting for transfers between devices  11.8 us (17%)
  Pallas kernels  11.4 us (16%)
  matrix products  6.6 us (9%)
  between operations  0.99 us (1%)
  other arithmetic  0.79 us (1%)
    ppermute x20, starting transfers between devices, send(): return lax.ppermute(value, AXES, chosen)  39.6 us
    ppermute x20, waiting for transfers between devices, send(): return lax.ppermute(value, AXES, chosen)  11.8 us
    pallas_call x1, Pallas kernels, first_tick(): pl.pallas_call(first_kernel, in_specs=[pl.BlockSpec(memory_space=pltpu.SM...  6.12 us
    pallas_call x4, Pallas kernels, place(): pl.pallas_call(functools.partial(place_kernel, plan, rows, len(halves) >...  5.24 us
    dot_general x3, matrix products, times(): return jnp.dot(left, weights, preferred_element_type=F32)  3.73 us
    dot_general x2, matrix products, times_t(): lax.dot_general(left, weights, (((1,), (1,)), ((), ())), preferred_elemen...  2.87 us
  transfers between devices with their start and end apart: 20, of which 3 were waited for; matrix products, arithmetic and copies ran while one was open for 7% of the time, Pallas kernels for 15%

profile of v5, /device:TPU:1, one launch (start us, length us, event | category | flops | bytes accessed | tf_op | source)
XLA Modules:
  0.0 71.2 jit_solution(10744706741880656811)
XLA Ops:
  0.6 0.0 copy-start
  0.7 2.6 %bitcast_select_fusion = (bf16[48,1152]{1,0:T(8,128)(2,1)S(1)}, bf16[48,1152]{1,0:T(8,128)(2,1)S(1)}) fusion(pred[]{:T(512)S(6)} %eq.15, bf16[1,768,1152]{2,1,0:T(8,128)(2,1)} %g_ref.1, s32[]{:T(128)S(6)} %select_n.81, bf16[1,768,1152]{2,1,0:T(8,128)(2,1)} %h_ref.1, bf16[768,1152]{1,0:T(8,128)(2,1)} %param.9, pred[]{:T(512)S(6)} %eq.16, ...), kind=kOutput, calls=%fused_computation.29 | convolution fusion | flops 127789056 | bytes 3430400 | tf_op jit(solution)/shard_map/dot_general | solution.py:23
  3.2 5.3 %collective-permute-start.6 = (bf16[48,1152]{1,0:T(8,128)(2,1)S(1)}, bf16[48,1152]{1,0:T(8,128)(2,1)S(1)}, u32[]{:S(2)}, u32[]{:S(2)}) collective-permute-start(bf16[48,1152]{1,0:T(8,128)(2,1)S(1)} %get-tuple-element.33), channel_id=1, source_target_pairs={{0,24},{1,25},{2,26},{3,27},{4,28},{5,29},{6,30},{7,31},{8,16},{9,... | collective-permute-start | bytes 331784 | tf_op jit(solution)/shard_map/ppermute | solution.py:172
  8.5 2.9 %collective-permute-start = (bf16[48,1152]{1,0:T(8,128)(2,1)S(1)}, bf16[48,1152]{1,0:T(8,128)(2,1)S(1)}, u32[]{:S(2)}, u32[]{:S(2)}) collective-permute-start(bf16[48,1152]{1,0:T(8,128)(2,1)S(1)} %get-tuple-element.34), channel_id=1, source_target_pairs={{0,40},{1,41},{2,42},{3,43},{4,44},{5,45},{6,46},{7,47},{8,32},{9,... | collective-permute-start | bytes 331784 | tf_op jit(solution)/shard_map/ppermute | solution.py:172
  11.4 0.0 copy-done
  11.4 2.0 %broadcast_select_fusion = (bf16[48,1152]{1,0:T(8,128)(2,1)S(1)}, bf16[48,1152]{1,0:T(8,128)(2,1)S(1)}) fusion(pred[]{:T(512)S(6)} %eq.18, bf16[768,1152]{1,0:T(8,128)(2,1)} %param.10, s32[]{:T(128)S(6)} %select_n.81, pred[]{:T(512)S(6)} %eq.17, bf16[1,1152,1152]{2,1,0:T(8,128)(2,1)S(1)} %copy-done, pred[]{:T(512)S(6)} %eq.15, ...), kind=kOutput, calls=%fused_computation.33 | convolution fusion | flops 127789056 | bytes 3320832 | tf_op jit(solution)/shard_map/dot_general | solution.py:27
  13.3 0.5 collective-permute-start.10
  13.8 0.7 pad_add_fusion.spec_ref
  14.5 0.0 copy-start.1
  14.5 6.1 %first_tick.1 = (bf16[1,2,768,1152]{3,2,1,0:T(8,128)(2,1)}, bf16[1,2,768,1152]{3,2,1,0:T(8,128)(2,1)}, bf16[2,384,1152]{2,1,0:T(8,128)(2,1)}) custom-call(s32[2]{0:T(128)} %pad_add_fusion.spec_ref, bf16[1,768,1152]{2,1,0:T(8,128)(2,1)} %a_ref.1, bf16[1,768,1152]{2,1,0:T(8,128)(2,1)} %h_ref.1, bf16[1,768,1152]{2,1,0:T(8,128)(2,1)} %g_ref.1, ...), custom_call_target="tpu_custom_call" | custom-call | flops 2038431744 | bytes 7077888 | tf_op jit(solution)/shard_map/first_tick/pallas_call | solution.py:86
  20.6 1.6 %collective-permute-start.16 = (bf16[2,384,1152]{2,1,0:T(8,128)(2,1)}, bf16[2,384,1152]{2,1,0:T(8,128)(2,1)S(1)}, u32[]{:S(2)}, u32[]{:S(2)}) collective-permute-start(bf16[2,384,1152]{2,1,0:T(8,128)(2,1)} %get-tuple-element.19), channel_id=1, source_target_pairs={{0,1},{1,0},{2,3},{3,2},{4,5},{5,4},{6,7},{7,6},{8,9},{9,8},{10,11... | collective-permute-start | bytes 5308424 | tf_op jit(solution)/shard_map/ppermute | solution.py:172
  22.2 0.0 collective-permute-done
  22.2 0.0 collective-permute-done.6
  22.2 0.0 copy-done.1
  22.2 0.6 fusion.16
  22.8 1.4 %collective-permute-start.7 = (bf16[48,1152]{1,0:T(8,128)(2,1)S(1)}, bf16[48,1152]{1,0:T(8,128)(2,1)S(1)}, u32[]{:S(2)}, u32[]{:S(2)}) collective-permute-start(bf16[48,1152]{1,0:T(8,128)(2,1)S(1)} %fusion.16), channel_id=1, source_target_pairs={{0,2},{1,3},{2,0},{3,1},{4,6},{5,7},{6,4},{7,5},{8,10},{9,11},{10,... | collective-permute-start | bytes 331784 | tf_op jit(solution)/shard_map/ppermute | solution.py:172
  24.2 0.0 collective-permute-done.10
  24.2 0.9 %fusion.27 = bf16[48,1152]{1,0:T(8,128)(2,1)S(1)} fusion(bf16[1,1152,1152]{2,1,0:T(8,128)(2,1)S(1)} %copy-done.1, bf16[48,1152]{1,0:T(8,128)(2,1)S(1)} %collective-permute-done.10, bf16[48,1152]{1,0:T(8,128)(2,1)S(1)} %collective-permute-done.6, pred[]{:T(512)S(6)} %eq.15), kind=kOutput, calls=%fused_computation.18 | convolution fusion | flops 127678464 | bytes 2985985 | tf_op jit(solution)/shard_map/dot_general | solution.py:27
  25.1 2.2 %collective-permute-start.11 = (bf16[48,1152]{1,0:T(8,128)(2,1)S(1)}, bf16[48,1152]{1,0:T(8,128)(2,1)S(1)}, u32[]{:S(2)}, u32[]{:S(2)}) collective-permute-start(bf16[48,1152]{1,0:T(8,128)(2,1)S(1)} %fusion.27), channel_id=1, source_target_pairs={{0,6},{1,7},{2,4},{3,5},{4,2},{5,3},{6,0},{7,1},{8,14},{9,15},{10,... | collective-permute-start | bytes 331784 | tf_op jit(solution)/shard_map/ppermute | solution.py:172
  27.2 0.6 fusion.22
  27.8 2.5 %collective-permute-start.1 = (bf16[48,1152]{1,0:T(8,128)(2,1)S(1)}, bf16[48,1152]{1,0:T(8,128)(2,1)S(1)}, u32[]{:S(2)}, u32[]{:S(2)}) collective-permute-start(bf16[48,1152]{1,0:T(8,128)(2,1)S(1)} %fusion.22), channel_id=1, source_target_pairs={{0,16},{1,17},{2,18},{3,19},{4,20},{5,21},{6,22},{7,23},{8,24},{9,... | collective-permute-start | bytes 331784 | tf_op jit(solution)/shard_map/ppermute | solution.py:172
  30.3 0.0 collective-permute-done.7
  30.4 0.9 %collective-permute-start.8 = (bf16[96,1152]{1,0:T(8,128)(2,1)S(1)}, bf16[96,1152]{1,0:T(8,128)(2,1)S(1)}, u32[]{:S(2)}, u32[]{:S(2)}) collective-permute-start(bf16[96,1152]{1,0:T(8,128)(2,1)S(1)} %pad_maximum_fusion.3), channel_id=1, source_target_pairs={{0,6},{1,7},{2,4},{3,5},{4,2},{5,3},{6,0},{7,1},{8,14},{9,15},{10,... | collective-permute-start | bytes 663560 | tf_op jit(solution)/shard_map/ppermute | solution.py:172
  31.2 0.0 collective-permute-done.11
  31.3 1.5 %collective-permute-start.12 = (bf16[96,1152]{1,0:T(8,128)(2,1)S(1)}, bf16[96,1152]{1,0:T(8,128)(2,1)S(1)}, u32[]{:S(2)}, u32[]{:S(2)}) collective-permute-start(bf16[96,1152]{1,0:T(8,128)(2,1)S(1)} %pad_maximum_fusion.4), channel_id=1, source_target_pairs={{0,8},{1,9},{2,10},{3,11},{4,12},{5,13},{6,14},{7,15},{8,0},{9,1},... | collective-permute-start | bytes 663560 | tf_op jit(solution)/shard_map/ppermute | solution.py:172
  32.7 4.0 %collective-permute-done.1 = bf16[48,1152]{1,0:T(8,128)(2,1)S(1)} collective-permute-done((bf16[48,1152]{1,0:T(8,128)(2,1)S(1)}, bf16[48,1152]{1,0:T(8,128)(2,1)S(1)}, u32[]{:S(2)}, u32[]{:S(2)}) %collective-permute-start.1) | collective-permute-done | bytes 110624 | tf_op jit(solution)/shard_map/ppermute | solution.py:172
  36.7 6.6 %collective-permute-start.2 = (bf16[48,1152]{1,0:T(8,128)(2,1)S(1)}, bf16[48,1152]{1,0:T(8,128)(2,1)S(1)}, u32[]{:S(2)}, u32[]{:S(2)}) collective-permute-start(bf16[48,1152]{1,0:T(8,128)(2,1)S(1)} %collective-permute-done.1), channel_id=1, source_target_pairs={{0,8},{1,9},{2,10},{3,11},{4,12},{5,13},{6,14},{7,15},{8,0},{9,1},... | collective-permute-start | bytes 331784 | tf_op jit(solution)/shard_map/ppermute | solution.py:172
  43.3 2.1 %collective-permute-done.2 = bf16[48,1152]{1,0:T(8,128)(2,1)S(1)} collective-permute-done((bf16[48,1152]{1,0:T(8,128)(2,1)S(1)}, bf16[48,1152]{1,0:T(8,128)(2,1)S(1)}, u32[]{:S(2)}, u32[]{:S(2)}) %collective-permute-start.2) | collective-permute-done | bytes 110624 | tf_op jit(solution)/shard_map/ppermute | solution.py:172
  45.5 0.1 collective-permute-start.3
  45.6 0.0 collective-permute-done.8
  45.7 2.7 %collective-permute-start.17 = (bf16[192,1152]{1,0:T(8,128)(2,1)S(1)}, bf16[192,1152]{1,0:T(8,128)(2,1)S(1)}, u32[]{:S(2)}, u32[]{:S(2)}) collective-permute-start(bf16[192,1152]{1,0:T(8,128)(2,1)S(1)} %pad_maximum_fusion.refs_0_), channel_id=1, source_target_pairs={{0,1},{1,0},{2,3},{3,2},{4,5},{5,4},{6,7},{7,6},{8,9},{9,8},{10,11... | collective-permute-start | bytes 1327112 | tf_op jit(solution)/shard_map/ppermute | solution.py:172
  48.3 1.7 %collective-permute-start.9 = (bf16[192,1152]{1,0:T(8,128)(2,1)S(1)}, bf16[192,1152]{1,0:T(8,128)(2,1)S(1)}, u32[]{:S(2)}, u32[]{:S(2)}) collective-permute-start(bf16[192,1152]{1,0:T(8,128)(2,1)S(1)} %pad_maximum_fusion.refs_0_), channel_id=1, source_target_pairs={{0,8},{1,9},{2,10},{3,11},{4,12},{5,13},{6,14},{7,15},{8,0},{9,1},... | collective-permute-start | bytes 1327112 | tf_op jit(solution)/shard_map/ppermute | solution.py:172
  50.1 0.0 collective-permute-done.12
  50.1 0.5 collective-permute-start.18
  50.6 0.0 collective-permute-done.3
  50.6 1.2 %collective-permute-start.13 = (bf16[192,1152]{1,0:T(8,128)(2,1)S(1)}, bf16[192,1152]{1,0:T(8,128)(2,1)S(1)}, u32[]{:S(2)}, u32[]{:S(2)}) collective-permute-start(bf16[192,1152]{1,0:T(8,128)(2,1)S(1)} %pad_maximum_fusion.1.refs_1_), channel_id=1, source_target_pairs={{0,2},{1,3},{2,0},{3,1},{4,6},{5,7},{6,4},{7,5},{8,10},{9,11},{10,... | collective-permute-start | bytes 1327112 | tf_op jit(solution)/shard_map/ppermute | solution.py:172
  51.9 0.0 collective-permute-done.17.refs_3_
  51.9 0.7 collective-permute-start.4
  52.6 0.0 collective-permute-done.18.refs_4_
  52.6 2.4 %collective-permute-start.19 = (bf16[192,1152]{1,0:T(8,128)(2,1)S(1)}, bf16[192,1152]{1,0:T(8,128)(2,1)S(1)}, u32[]{:S(2)}, u32[]{:S(2)}) collective-permute-start(bf16[192,1152]{1,0:T(8,128)(2,1)S(1)} %constant_dynamic-update-slice_fusion.refs_2_), channel_id=1, source_target_pairs={{0,1},{1,0},{2,3},{3,2},{4,5},{5,4},{6,7},{7,6},{8,9},{9,8},{10,11... | collective-permute-start | bytes 1327112 | tf_op jit(solution)/shard_map/ppermute | solution.py:172
  54.9 5.6 %collective-permute-done.9.refs_0_ = bf16[192,1152]{1,0:T(8,128)(2,1)S(1)} collective-permute-done((bf16[192,1152]{1,0:T(8,128)(2,1)S(1)}, bf16[192,1152]{1,0:T(8,128)(2,1)S(1)}, u32[]{:S(2)}, u32[]{:S(2)}) %collective-permute-start.9) | collective-permute-done | bytes 442400 | tf_op jit(solution)/shard_map/ppermute | solution.py:172
  60.5 0.7 collective-permute-start.14
  61.2 0.0 collective-permute-done.13.refs_1_
  61.2 2.0 %collective-permute-start.15 = (bf16[192,1152]{1,0:T(8,128)(2,1)S(1)}, bf16[192,1152]{1,0:T(8,128)(2,1)S(1)}, u32[]{:S(2)}, u32[]{:S(2)}) collective-permute-start(bf16[192,1152]{1,0:T(8,128)(2,1)S(1)} %collective-permute-done.13.refs_1_), channel_id=1, source_target_pairs={{0,1},{1,0},{2,3},{3,2},{4,5},{5,4},{6,7},{7,6},{8,9},{9,8},{10,11... | collective-permute-start | bytes 1327112 | tf_op jit(solution)/shard_map/ppermute | solution.py:172
  63.2 0.0 collective-permute-done.4.refs_2_
  63.2 2.6 %collective-permute-start.5 = (bf16[192,1152]{1,0:T(8,128)(2,1)S(1)}, bf16[192,1152]{1,0:T(8,128)(2,1)S(1)}, u32[]{:S(2)}, u32[]{:S(2)}) collective-permute-start(bf16[192,1152]{1,0:T(8,128)(2,1)S(1)} %collective-permute-done.4.refs_2_), channel_id=1, source_target_pairs={{0,1},{1,0},{2,3},{3,2},{4,5},{5,4},{6,7},{7,6},{8,9},{9,8},{10,11... | collective-permute-start | bytes 1327112 | tf_op jit(solution)/shard_map/ppermute | solution.py:172
  65.7 0.0 collective-permute-done.19.refs_5_
  65.7 1.7 %shard_map.85 = (bf16[1,2,768,1152]{3,2,1,0:T(8,128)(2,1)}, bf16[1,2,768,1152]{3,2,1,0:T(8,128)(2,1)}, bf16[1,768,1152]{2,1,0:T(8,128)(2,1)}) custom-call(s32[1]{0:T(128)} %bitcast.replica_ref, bf16[192,1152]{1,0:T(8,128)(2,1)S(1)} %pad_maximum_fusion.refs_0_, ...), custom_call_target="tpu_custom_call", output_to_operand_aliasing={{0}: (7, {}), {1}: (8, {})} | custom-call | bytes 5308416 | tf_op jit(solution)/shard_map/pallas_call | solution.py:136
  67.5 0.0 collective-permute-done.16.refs_0_
  67.5 1.2 %shard_map.86 = (bf16[1,2,768,1152]{3,2,1,0:T(8,128)(2,1)}, bf16[1,2,768,1152]{3,2,1,0:T(8,128)(2,1)}, bf16[1,768,1152]{2,1,0:T(8,128)(2,1)}) custom-call(s32[1]{0:T(128)} %bitcast.replica_ref, bf16[2,384,1152]{2,1,0:T(8,128)(2,1)S(1)} %collective-permute-done.16.refs_0_, ...), custom_call_target="tpu_custom_call", output_to_operand_aliasing={{0}: (2, {}), {1}: (3, {}), {2}: (4, {})} | custom-call | tf_op jit(solution)/shard_map/pallas_call | solution.py:136
  68.7 0.0 collective-permute-done.14.refs_3_
  68.7 0.0 collective-permute-done.15.refs_4_
  68.7 1.5 %shard_map.87 = (bf16[1,2,768,1152]{3,2,1,0:T(8,128)(2,1)}, bf16[1,2,768,1152]{3,2,1,0:T(8,128)(2,1)}, bf16[1,768,1152]{2,1,0:T(8,128)(2,1)}) custom-call(s32[1]{0:T(128)} %bitcast.replica_ref, bf16[192,1152]{1,0:T(8,128)(2,1)S(1)} %collective-permute-done.9.refs_0_, ...), custom_call_target="tpu_custom_call", output_to_operand_aliasing={{0}: (6, {}), {1}: (7, {}), {2}: (8, {})} | custom-call | bytes 4423680 | tf_op jit(solution)/shard_map/pallas_call | solution.py:136
  70.3 0.0 collective-permute-done.5.refs_0_
  70.3 0.8 %shard_map.88 = (bf16[1,2,768,1152]{3,2,1,0:T(8,128)(2,1)}, bf16[1,2,768,1152]{3,2,1,0:T(8,128)(2,1)}, bf16[1,768,1152]{2,1,0:T(8,128)(2,1)}) custom-call(s32[1]{0:T(128)} %bitcast.replica_ref, bf16[192,1152]{1,0:T(8,128)(2,1)S(1)} %collective-permute-done.5.refs_0_, ...), custom_call_target="tpu_custom_call", output_to_operand_aliasing={{0}: (2, {}), {1}: (3, {}), {2}: (4, {})} | custom-call | bytes 884736 | tf_op jit(solution)/shard_map/pallas_call | solution.py:136
  (8 shorter events, 0.2 us)
Async XLA Ops:
  0.6 10.7 %copy-start = (bf16[1,1152,1152]{2,1,0:T(8,128)(2,1)S(1)}, bf16[1,1152,1152]{2,1,0:T(8,128)(2,1)}, u32[]{:S(2)}) copy-start(bf16[1,1152,1152]{2,1,0:T(8,128)(2,1)} %w_ref.1) | copy-start | bytes 7962628
  3.2 18.9 %collective-permute-start.6 = (bf16[48,1152]{1,0:T(8,128)(2,1)S(1)}, bf16[48,1152]{1,0:T(8,128)(2,1)S(1)}, u32[]{:S(2)}, u32[]{:S(2)}) collective-permute-start(bf16[48,1152]{1,0:T(8,128)(2,1)S(1)} %get-tuple-element.33), channel_id=1, source_target_pairs={{0,24},{1,25},{2,26},{3,27},{4,28},{5,29},{6,30},{7,31},{8,16},{9,... | collective-permute-start | bytes 331784 | tf_op jit(solution)/shard_map/ppermute | solution.py:172
  8.5 13.7 %collective-permute-start = (bf16[48,1152]{1,0:T(8,128)(2,1)S(1)}, bf16[48,1152]{1,0:T(8,128)(2,1)S(1)}, u32[]{:S(2)}, u32[]{:S(2)}) collective-permute-start(bf16[48,1152]{1,0:T(8,128)(2,1)S(1)} %get-tuple-element.34), channel_id=1, source_target_pairs={{0,40},{1,41},{2,42},{3,43},{4,44},{5,45},{6,46},{7,47},{8,32},{9,... | collective-permute-start | bytes 331784 | tf_op jit(solution)/shard_map/ppermute | solution.py:172
  13.3 10.8 %collective-permute-start.10 = (bf16[48,1152]{1,0:T(8,128)(2,1)S(1)}, bf16[48,1152]{1,0:T(8,128)(2,1)S(1)}, u32[]{:S(2)}, u32[]{:S(2)}) collective-permute-start(bf16[48,1152]{1,0:T(8,128)(2,1)S(1)} %get-tuple-element.18), channel_id=1, source_target_pairs={{32,8},{33,9},{34,10},{35,11},{36,12},{37,13},{38,14},{39,15},{40,... | collective-permute-start | bytes 331784 | tf_op jit(solution)/shard_map/ppermute | solution.py:172
  14.5 7.7 %copy-start.1 = (bf16[1,1152,1152]{2,1,0:T(8,128)(2,1)S(1)}, bf16[1,1152,1152]{2,1,0:T(8,128)(2,1)}, u32[]{:S(2)}) copy-start(bf16[1,1152,1152]{2,1,0:T(8,128)(2,1)} %w_ref.1) | copy-start | bytes 7962628
  20.6 46.9 %collective-permute-start.16 = (bf16[2,384,1152]{2,1,0:T(8,128)(2,1)}, bf16[2,384,1152]{2,1,0:T(8,128)(2,1)S(1)}, u32[]{:S(2)}, u32[]{:S(2)}) collective-permute-start(bf16[2,384,1152]{2,1,0:T(8,128)(2,1)} %get-tuple-element.19), channel_id=1, source_target_pairs={{0,1},{1,0},{2,3},{3,2},{4,5},{5,4},{6,7},{7,6},{8,9},{9,8},{10,11... | collective-permute-start | bytes 5308424 | tf_op jit(solution)/shard_map/ppermute | solution.py:172
  22.8 7.6 %collective-permute-start.7 = (bf16[48,1152]{1,0:T(8,128)(2,1)S(1)}, bf16[48,1152]{1,0:T(8,128)(2,1)S(1)}, u32[]{:S(2)}, u32[]{:S(2)}) collective-permute-start(bf16[48,1152]{1,0:T(8,128)(2,1)S(1)} %fusion.16), channel_id=1, source_target_pairs={{0,2},{1,3},{2,0},{3,1},{4,6},{5,7},{6,4},{7,5},{8,10},{9,11},{10,... | collective-permute-start | bytes 331784 | tf_op jit(solution)/shard_map/ppermute | solution.py:172
  25.1 6.1 %collective-permute-start.11 = (bf16[48,1152]{1,0:T(8,128)(2,1)S(1)}, bf16[48,1152]{1,0:T(8,128)(2,1)S(1)}, u32[]{:S(2)}, u32[]{:S(2)}) collective-permute-start(bf16[48,1152]{1,0:T(8,128)(2,1)S(1)} %fusion.27), channel_id=1, source_target_pairs={{0,6},{1,7},{2,4},{3,5},{4,2},{5,3},{6,0},{7,1},{8,14},{9,15},{10,... | collective-permute-start | bytes 331784 | tf_op jit(solution)/shard_map/ppermute | solution.py:172
  27.8 8.9 %collective-permute-start.1 = (bf16[48,1152]{1,0:T(8,128)(2,1)S(1)}, bf16[48,1152]{1,0:T(8,128)(2,1)S(1)}, u32[]{:S(2)}, u32[]{:S(2)}) collective-permute-start(bf16[48,1152]{1,0:T(8,128)(2,1)S(1)} %fusion.22), channel_id=1, source_target_pairs={{0,16},{1,17},{2,18},{3,19},{4,20},{5,21},{6,22},{7,23},{8,24},{9,... | collective-permute-start | bytes 331784 | tf_op jit(solution)/shard_map/ppermute | solution.py:172
  30.4 15.2 %collective-permute-start.8 = (bf16[96,1152]{1,0:T(8,128)(2,1)S(1)}, bf16[96,1152]{1,0:T(8,128)(2,1)S(1)}, u32[]{:S(2)}, u32[]{:S(2)}) collective-permute-start(bf16[96,1152]{1,0:T(8,128)(2,1)S(1)} %pad_maximum_fusion.3), channel_id=1, source_target_pairs={{0,6},{1,7},{2,4},{3,5},{4,2},{5,3},{6,0},{7,1},{8,14},{9,15},{10,... | collective-permute-start | bytes 663560 | tf_op jit(solution)/shard_map/ppermute | solution.py:172
  31.3 18.8 %collective-permute-start.12 = (bf16[96,1152]{1,0:T(8,128)(2,1)S(1)}, bf16[96,1152]{1,0:T(8,128)(2,1)S(1)}, u32[]{:S(2)}, u32[]{:S(2)}) collective-permute-start(bf16[96,1152]{1,0:T(8,128)(2,1)S(1)} %pad_maximum_fusion.4), channel_id=1, source_target_pairs={{0,8},{1,9},{2,10},{3,11},{4,12},{5,13},{6,14},{7,15},{8,0},{9,1},... | collective-permute-start | bytes 663560 | tf_op jit(solution)/shard_map/ppermute | solution.py:172
  36.7 8.7 %collective-permute-start.2 = (bf16[48,1152]{1,0:T(8,128)(2,1)S(1)}, bf16[48,1152]{1,0:T(8,128)(2,1)S(1)}, u32[]{:S(2)}, u32[]{:S(2)}) collective-permute-start(bf16[48,1152]{1,0:T(8,128)(2,1)S(1)} %collective-permute-done.1), channel_id=1, source_target_pairs={{0,8},{1,9},{2,10},{3,11},{4,12},{5,13},{6,14},{7,15},{8,0},{9,1},... | collective-permute-start | bytes 331784 | tf_op jit(solution)/shard_map/ppermute | solution.py:172
  45.5 5.1 %collective-permute-start.3 = (bf16[96,1152]{1,0:T(8,128)(2,1)S(1)}, bf16[96,1152]{1,0:T(8,128)(2,1)S(1)}, u32[]{:S(2)}, u32[]{:S(2)}) collective-permute-start(bf16[96,1152]{1,0:T(8,128)(2,1)S(1)} %pad_maximum_fusion.2), channel_id=1, source_target_pairs={{0,2},{1,3},{2,0},{3,1},{4,6},{5,7},{6,4},{7,5},{8,10},{9,11},{10,... | collective-permute-start | bytes 663560 | tf_op jit(solution)/shard_map/ppermute | solution.py:172
  45.7 6.2 %collective-permute-start.17 = (bf16[192,1152]{1,0:T(8,128)(2,1)S(1)}, bf16[192,1152]{1,0:T(8,128)(2,1)S(1)}, u32[]{:S(2)}, u32[]{:S(2)}) collective-permute-start(bf16[192,1152]{1,0:T(8,128)(2,1)S(1)} %pad_maximum_fusion.refs_0_), channel_id=1, source_target_pairs={{0,1},{1,0},{2,3},{3,2},{4,5},{5,4},{6,7},{7,6},{8,9},{9,8},{10,11... | collective-permute-start | bytes 1327112 | tf_op jit(solution)/shard_map/ppermute | solution.py:172
  48.3 12.2 %collective-permute-start.9 = (bf16[192,1152]{1,0:T(8,128)(2,1)S(1)}, bf16[192,1152]{1,0:T(8,128)(2,1)S(1)}, u32[]{:S(2)}, u32[]{:S(2)}) collective-permute-start(bf16[192,1152]{1,0:T(8,128)(2,1)S(1)} %pad_maximum_fusion.refs_0_), channel_id=1, source_target_pairs={{0,8},{1,9},{2,10},{3,11},{4,12},{5,13},{6,14},{7,15},{8,0},{9,1},... | collective-permute-start | bytes 1327112 | tf_op jit(solution)/shard_map/ppermute | solution.py:172
  50.1 2.4 %collective-permute-start.18 = (bf16[192,1152]{1,0:T(8,128)(2,1)S(1)}, bf16[192,1152]{1,0:T(8,128)(2,1)S(1)}, u32[]{:S(2)}, u32[]{:S(2)}) collective-permute-start(bf16[192,1152]{1,0:T(8,128)(2,1)S(1)} %pad_maximum_fusion.1.refs_1_), channel_id=1, source_target_pairs={{0,1},{1,0},{2,3},{3,2},{4,5},{5,4},{6,7},{7,6},{8,9},{9,8},{10,11... | collective-permute-start | bytes 1327112 | tf_op jit(solution)/shard_map/ppermute | solution.py:172
  50.6 10.6 %collective-permute-start.13 = (bf16[192,1152]{1,0:T(8,128)(2,1)S(1)}, bf16[192,1152]{1,0:T(8,128)(2,1)S(1)}, u32[]{:S(2)}, u32[]{:S(2)}) collective-permute-start(bf16[192,1152]{1,0:T(8,128)(2,1)S(1)} %pad_maximum_fusion.1.refs_1_), channel_id=1, source_target_pairs={{0,2},{1,3},{2,0},{3,1},{4,6},{5,7},{6,4},{7,5},{8,10},{9,11},{10,... | collective-permute-start | bytes 1327112 | tf_op jit(solution)/shard_map/ppermute | solution.py:172
  51.9 11.3 %collective-permute-start.4 = (bf16[192,1152]{1,0:T(8,128)(2,1)S(1)}, bf16[192,1152]{1,0:T(8,128)(2,1)S(1)}, u32[]{:S(2)}, u32[]{:S(2)}) collective-permute-start(bf16[192,1152]{1,0:T(8,128)(2,1)S(1)} %constant_dynamic-update-slice_fusion.refs_2_), channel_id=1, source_target_pairs={{0,6},{1,7},{2,4},{3,5},{4,2},{5,3},{6,0},{7,1},{8,14},{9,15},{10,... | collective-permute-start | bytes 1327112 | tf_op jit(solution)/shard_map/ppermute | solution.py:172
  52.6 13.2 %collective-permute-start.19 = (bf16[192,1152]{1,0:T(8,128)(2,1)S(1)}, bf16[192,1152]{1,0:T(8,128)(2,1)S(1)}, u32[]{:S(2)}, u32[]{:S(2)}) collective-permute-start(bf16[192,1152]{1,0:T(8,128)(2,1)S(1)} %constant_dynamic-update-slice_fusion.refs_2_), channel_id=1, source_target_pairs={{0,1},{1,0},{2,3},{3,2},{4,5},{5,4},{6,7},{7,6},{8,9},{9,8},{10,11... | collective-permute-start | bytes 1327112 | tf_op jit(solution)/shard_map/ppermute | solution.py:172
  60.5 8.2 %collective-permute-start.14 = (bf16[192,1152]{1,0:T(8,128)(2,1)S(1)}, bf16[192,1152]{1,0:T(8,128)(2,1)S(1)}, u32[]{:S(2)}, u32[]{:S(2)}) collective-permute-start(bf16[192,1152]{1,0:T(8,128)(2,1)S(1)} %collective-permute-done.9.refs_0_), channel_id=1, source_target_pairs={{0,1},{1,0},{2,3},{3,2},{4,5},{5,4},{6,7},{7,6},{8,9},{9,8},{10,11... | collective-permute-start | bytes 1327112 | tf_op jit(solution)/shard_map/ppermute | solution.py:172
  61.2 7.5 %collective-permute-start.15 = (bf16[192,1152]{1,0:T(8,128)(2,1)S(1)}, bf16[192,1152]{1,0:T(8,128)(2,1)S(1)}, u32[]{:S(2)}, u32[]{:S(2)}) collective-permute-start(bf16[192,1152]{1,0:T(8,128)(2,1)S(1)} %collective-permute-done.13.refs_1_), channel_id=1, source_target_pairs={{0,1},{1,0},{2,3},{3,2},{4,5},{5,4},{6,7},{7,6},{8,9},{9,8},{10,11... | collective-permute-start | bytes 1327112 | tf_op jit(solution)/shard_map/ppermute | solution.py:172
  63.2 7.1 %collective-permute-start.5 = (bf16[192,1152]{1,0:T(8,128)(2,1)S(1)}, bf16[192,1152]{1,0:T(8,128)(2,1)S(1)}, u32[]{:S(2)}, u32[]{:S(2)}) collective-permute-start(bf16[192,1152]{1,0:T(8,128)(2,1)S(1)} %collective-permute-done.4.refs_2_), channel_id=1, source_target_pairs={{0,1},{1,0},{2,3},{3,2},{4,5},{5,4},{6,7},{7,6},{8,9},{9,8},{10,11... | collective-permute-start | bytes 1327112 | tf_op jit(solution)/shard_map/ppermute | solution.py:172

commit v6 on v5

--- a/solution.py
+++ b/solution.py
@@ -28,11 +28,11 @@
 
 
 def first_kernel(
-    spec_ref, a_ref, h_ref, g_ref, w_ref, out_ref, grad_ref, mine_ref, a_in, h_in, g_in, w_in, out_buf, grad_buf, in_sem, out_sem
+    early_ref, core_ref, a_ref, h_ref, g_ref, w_ref, out_ref, grad_ref, mine_ref, a_in, h_in, g_in, w_in, out_buf, grad_buf, in_sem, out_sem
 ):
-    early = spec_ref[0] == 1
+    early = early_ref[0] == 1
     height, width = a_in.shape
-    start = pl.multiple_of(spec_ref[1] * height, height)
+    start = pl.multiple_of(core_ref[0] * height, height)
     part = width // 4
     rows = pl.ds(start, height)
     come = [
@@ -52,24 +52,29 @@
             pltpu.make_async_copy(buf, mine_ref.at[n], out_sem.at[2 + n]),
         ]
 
-    for copy in turn[:2] + come + turn[2:]:
+    take_h, take_g, take_a = come
+    for copy in [take_a, take_g] + turn + [take_h]:
         copy.start()
-    for copy in turn + come:
-        copy.wait()
 
     @pl.when(early)
     def _():
+        take_a.wait()
         for copy in go(a_in, out_ref, 0):
             copy.start()
+        for copy in turn + [take_h, take_g]:
+            copy.wait()
         product = times_t(h_in[...], w_in[...])
         grad_buf[...] = (g_in[...].astype(F32) + product).astype(BF16)
 
     @pl.when(jnp.logical_not(early))
     def _():
+        for copy in turn + [take_a, take_h]:
+            copy.wait()
         product = times(a_in[...], w_in[...])
         out_buf[...] = (product + h_in[...].astype(F32)).astype(BF16)
         for copy in go(out_buf, out_ref, 0):
             copy.start()
+        take_g.wait()
         grad_buf[...] = times_t(g_in[...], w_in[...]).astype(BF16)
 
     for copy in go(grad_buf, grad_ref, 1):
@@ -83,9 +88,9 @@
     half = height // 2
     anywhere = pl.BlockSpec(memory_space=pl.ANY)
     both = jax.ShapeDtypeStruct((1, 2, height, width), BF16)
-    return pl.pallas_call(
+    call = pl.pallas_call(
         first_kernel,
-        in_specs=[pl.BlockSpec(memory_space=pltpu.SMEM)] + [anywhere] * 4,
+        in_specs=[pl.BlockSpec(memory_space=pltpu.SMEM)] * 2 + [anywhere] * 4,
         out_specs=[anywhere] * 3,
         out_shape=[both, both, jax.ShapeDtypeStruct((2, half, width), BF16)],
         scratch_shapes=[pltpu.VMEM((half, width), BF16)] * 3
@@ -97,7 +102,9 @@
         ),
         compiler_params=pltpu.CompilerParams(vmem_limit_bytes=60 << 20),
         name="first_tick",
-    )(jnp.stack([early.astype(jnp.int32), core]), a, held, cot, weights)
+    )
+    scalars = (jnp.reshape(x.astype(jnp.int32), (1,)) for x in (early, core))
+    return call(*scalars, a, held, cot, weights)
 
 
 def place_kernel(plan, rows, halves, replica_ref, *refs):

time: 71.4 us -> 71.2 us (level)
  starting transfers between devices: 39.6 us -> 41.7 us
  waiting for transfers between devices: 11.8 us -> 10.3 us
    ppermute x20, starting transfers between devices: 39.6 us -> 41.7 us  [send(): return lax.ppermute(value, AXES, chosen)]
    ppermute x20, waiting for transfers between devices: 11.8 us -> 10.3 us  [send(): return lax.ppermute(value, AXES, chosen)]
  transfers between devices with their start and end apart: 20 -> 20, of which waited for: 3 -> 3; matrix products, arithmetic and copies ran while one was open for 7% -> 6% of each run, Pallas kernels for 15% -> 15%
where the time goes in v6:
time: 71.2 us; the launch traced here: 71.1 us
  starting transfers between devices  41.7 us (59%)
  Pallas kernels  11.3 us (16%)
  waiting for transfers between devices  10.3 us (14%)
  matrix products  6.6 us (9%)
  between operations  0.98 us (1%)
    ppermute x20, starting transfers between devices, send(): return lax.ppermute(value, AXES, chosen)  41.7 us
    ppermute x20, waiting for transfers between devices, send(): return lax.ppermute(value, AXES, chosen)  10.3 us
    pallas_call x1, Pallas kernels, first_tick(): return call(*scalars, a, held, cot, weights)  6.08 us
    pallas_call x4, Pallas kernels, place(): pl.pallas_call(functools.partial(place_kernel, plan, rows, len(halves) >...  5.24 us
    dot_general x3, matrix products, times(): return jnp.dot(left, weights, preferred_element_type=F32)  3.73 us
    dot_general x2, matrix products, times_t(): lax.dot_general(left, weights, (((1,), (1,)), ((), ())), preferred_elemen...  2.87 us
  transfers between devices with their start and end apart: 20, of which 3 were waited for; matrix products, arithmetic and copies ran while one was open for 6% of the time, Pallas kernels for 15%

profile of v6, /device:TPU:1, one launch (start us, length us, event | category | flops | bytes accessed | tf_op | source)
XLA Modules:
  0.0 71.1 jit_solution(17085634384842204171)
XLA Ops:
  0.6 0.0 copy-start
  0.7 2.6 %bitcast_select_fusion = (bf16[48,1152]{1,0:T(8,128)(2,1)S(1)}, bf16[48,1152]{1,0:T(8,128)(2,1)S(1)}) fusion(pred[]{:T(512)S(6)} %eq.15, bf16[1,768,1152]{2,1,0:T(8,128)(2,1)} %g_ref.1, s32[]{:T(128)S(6)} %select_n.81, bf16[1,768,1152]{2,1,0:T(8,128)(2,1)} %h_ref.1, bf16[768,1152]{1,0:T(8,128)(2,1)} %param.9, pred[]{:T(512)S(6)} %eq.16, ...), kind=kOutput, calls=%fused_computation.29 | convolution fusion | flops 127789056 | bytes 3430400 | tf_op jit(solution)/shard_map/dot_general | solution.py:23
  3.2 5.3 %collective-permute-start.6 = (bf16[48,1152]{1,0:T(8,128)(2,1)S(1)}, bf16[48,1152]{1,0:T(8,128)(2,1)S(1)}, u32[]{:S(2)}, u32[]{:S(2)}) collective-permute-start(bf16[48,1152]{1,0:T(8,128)(2,1)S(1)} %get-tuple-element.33), channel_id=1, source_target_pairs={{0,24},{1,25},{2,26},{3,27},{4,28},{5,29},{6,30},{7,31},{8,16},{9,... | collective-permute-start | bytes 331784 | tf_op jit(solution)/shard_map/ppermute | solution.py:179
  8.5 2.9 %collective-permute-start = (bf16[48,1152]{1,0:T(8,128)(2,1)S(1)}, bf16[48,1152]{1,0:T(8,128)(2,1)S(1)}, u32[]{:S(2)}, u32[]{:S(2)}) collective-permute-start(bf16[48,1152]{1,0:T(8,128)(2,1)S(1)} %get-tuple-element.34), channel_id=1, source_target_pairs={{0,40},{1,41},{2,42},{3,43},{4,44},{5,45},{6,46},{7,47},{8,32},{9,... | collective-permute-start | bytes 331784 | tf_op jit(solution)/shard_map/ppermute | solution.py:179
  11.4 0.0 copy-done
  11.4 2.0 %broadcast_select_fusion = (bf16[48,1152]{1,0:T(8,128)(2,1)S(1)}, bf16[48,1152]{1,0:T(8,128)(2,1)S(1)}) fusion(pred[]{:T(512)S(6)} %eq.18, bf16[768,1152]{1,0:T(8,128)(2,1)} %param.10, s32[]{:T(128)S(6)} %select_n.81, pred[]{:T(512)S(6)} %eq.17, bf16[1,1152,1152]{2,1,0:T(8,128)(2,1)S(1)} %copy-done, pred[]{:T(512)S(6)} %eq.15, ...), kind=kOutput, calls=%fused_computation.33 | convolution fusion | flops 127789056 | bytes 3320832 | tf_op jit(solution)/shard_map/dot_general | solution.py:27
  13.3 0.5 collective-permute-start.10
  13.8 0.0 copy-start.1
  13.8 6.1 %first_tick.1 = (bf16[1,2,768,1152]{3,2,1,0:T(8,128)(2,1)}, bf16[1,2,768,1152]{3,2,1,0:T(8,128)(2,1)}, bf16[2,384,1152]{2,1,0:T(8,128)(2,1)}) custom-call(s32[1]{0:T(128)} %bitcast.6.early_ref, s32[1]{0:T(128)} %bitcast.7.core_ref, bf16[1,768,1152]{2,1,0:T(8,128)(2,1)} %a_ref.1, bf16[1,768,1152]{2,1,0:T(8,128)(2,1)} %h_ref.1, bf16[1,768,1152]{2,1,0:T(8,128)(2,1)} %g_ref.1, ...), custom_call_target="tpu_custom_call" | custom-call | flops 2038431744 | bytes 7077888 | tf_op jit(solution)/shard_map/first_tick/pallas_call | solution.py:107
  19.9 1.6 %collective-permute-start.16 = (bf16[2,384,1152]{2,1,0:T(8,128)(2,1)}, bf16[2,384,1152]{2,1,0:T(8,128)(2,1)S(1)}, u32[]{:S(2)}, u32[]{:S(2)}) collective-permute-start(bf16[2,384,1152]{2,1,0:T(8,128)(2,1)} %get-tuple-element.19), channel_id=1, source_target_pairs={{0,1},{1,0},{2,3},{3,2},{4,5},{5,4},{6,7},{7,6},{8,9},{9,8},{10,11... | collective-permute-start | bytes 5308424 | tf_op jit(solution)/shard_map/ppermute | solution.py:179
  21.5 0.0 collective-permute-done
  21.5 0.0 collective-permute-done.6
  21.5 0.0 copy-done.1
  21.5 0.6 fusion.16
  22.1 1.4 %collective-permute-start.7 = (bf16[48,1152]{1,0:T(8,128)(2,1)S(1)}, bf16[48,1152]{1,0:T(8,128)(2,1)S(1)}, u32[]{:S(2)}, u32[]{:S(2)}) collective-permute-start(bf16[48,1152]{1,0:T(8,128)(2,1)S(1)} %fusion.16), channel_id=1, source_target_pairs={{0,2},{1,3},{2,0},{3,1},{4,6},{5,7},{6,4},{7,5},{8,10},{9,11},{10,... | collective-permute-start | bytes 331784 | tf_op jit(solution)/shard_map/ppermute | solution.py:179
  23.5 0.0 collective-permute-done.10
  23.5 0.9 %fusion.27 = bf16[48,1152]{1,0:T(8,128)(2,1)S(1)} fusion(bf16[1,1152,1152]{2,1,0:T(8,128)(2,1)S(1)} %copy-done.1, bf16[48,1152]{1,0:T(8,128)(2,1)S(1)} %collective-permute-done.10, bf16[48,1152]{1,0:T(8,128)(2,1)S(1)} %collective-permute-done.6, pred[]{:T(512)S(6)} %eq.15), kind=kOutput, calls=%fused_computation.18 | convolution fusion | flops 127678464 | bytes 2985985 | tf_op jit(solution)/shard_map/dot_general | solution.py:27
  24.4 2.8 %collective-permute-start.11 = (bf16[48,1152]{1,0:T(8,128)(2,1)S(1)}, bf16[48,1152]{1,0:T(8,128)(2,1)S(1)}, u32[]{:S(2)}, u32[]{:S(2)}) collective-permute-start(bf16[48,1152]{1,0:T(8,128)(2,1)S(1)} %fusion.27), channel_id=1, source_target_pairs={{0,6},{1,7},{2,4},{3,5},{4,2},{5,3},{6,0},{7,1},{8,14},{9,15},{10,... | collective-permute-start | bytes 331784 | tf_op jit(solution)/shard_map/ppermute | solution.py:179
  27.2 0.6 fusion.22
  27.8 2.0 %collective-permute-start.1 = (bf16[48,1152]{1,0:T(8,128)(2,1)S(1)}, bf16[48,1152]{1,0:T(8,128)(2,1)S(1)}, u32[]{:S(2)}, u32[]{:S(2)}) collective-permute-start(bf16[48,1152]{1,0:T(8,128)(2,1)S(1)} %fusion.22), channel_id=1, source_target_pairs={{0,16},{1,17},{2,18},{3,19},{4,20},{5,21},{6,22},{7,23},{8,24},{9,... | collective-permute-start | bytes 331784 | tf_op jit(solution)/shard_map/ppermute | solution.py:179
  29.8 0.0 collective-permute-done.7
  29.8 0.6 collective-permute-start.8
  30.4 0.0 collective-permute-done.11
  30.5 2.2 %collective-permute-start.12 = (bf16[96,1152]{1,0:T(8,128)(2,1)S(1)}, bf16[96,1152]{1,0:T(8,128)(2,1)S(1)}, u32[]{:S(2)}, u32[]{:S(2)}) collective-permute-start(bf16[96,1152]{1,0:T(8,128)(2,1)S(1)} %pad_maximum_fusion.4), channel_id=1, source_target_pairs={{0,8},{1,9},{2,10},{3,11},{4,12},{5,13},{6,14},{7,15},{8,0},{9,1},... | collective-permute-start | bytes 663560 | tf_op jit(solution)/shard_map/ppermute | solution.py:179
  32.7 2.6 %collective-permute-done.1 = bf16[48,1152]{1,0:T(8,128)(2,1)S(1)} collective-permute-done((bf16[48,1152]{1,0:T(8,128)(2,1)S(1)}, bf16[48,1152]{1,0:T(8,128)(2,1)S(1)}, u32[]{:S(2)}, u32[]{:S(2)}) %collective-permute-start.1) | collective-permute-done | bytes 110624 | tf_op jit(solution)/shard_map/ppermute | solution.py:179
  35.4 7.7 %collective-permute-start.2 = (bf16[48,1152]{1,0:T(8,128)(2,1)S(1)}, bf16[48,1152]{1,0:T(8,128)(2,1)S(1)}, u32[]{:S(2)}, u32[]{:S(2)}) collective-permute-start(bf16[48,1152]{1,0:T(8,128)(2,1)S(1)} %collective-permute-done.1), channel_id=1, source_target_pairs={{0,8},{1,9},{2,10},{3,11},{4,12},{5,13},{6,14},{7,15},{8,0},{9,1},... | collective-permute-start | bytes 331784 | tf_op jit(solution)/shard_map/ppermute | solution.py:179
  43.1 2.1 %collective-permute-done.2 = bf16[48,1152]{1,0:T(8,128)(2,1)S(1)} collective-permute-done((bf16[48,1152]{1,0:T(8,128)(2,1)S(1)}, bf16[48,1152]{1,0:T(8,128)(2,1)S(1)}, u32[]{:S(2)}, u32[]{:S(2)}) %collective-permute-start.2) | collective-permute-done | bytes 110624 | tf_op jit(solution)/shard_map/ppermute | solution.py:179
  45.2 0.2 collective-permute-start.3
  45.4 0.0 collective-permute-done.8
  45.4 2.5 %collective-permute-start.17 = (bf16[192,1152]{1,0:T(8,128)(2,1)S(1)}, bf16[192,1152]{1,0:T(8,128)(2,1)S(1)}, u32[]{:S(2)}, u32[]{:S(2)}) collective-permute-start(bf16[192,1152]{1,0:T(8,128)(2,1)S(1)} %pad_maximum_fusion.refs_0_), channel_id=1, source_target_pairs={{0,1},{1,0},{2,3},{3,2},{4,5},{5,4},{6,7},{7,6},{8,9},{9,8},{10,11... | collective-permute-start | bytes 1327112 | tf_op jit(solution)/shard_map/ppermute | solution.py:179
  48.0 1.7 %collective-permute-start.9 = (bf16[192,1152]{1,0:T(8,128)(2,1)S(1)}, bf16[192,1152]{1,0:T(8,128)(2,1)S(1)}, u32[]{:S(2)}, u32[]{:S(2)}) collective-permute-start(bf16[192,1152]{1,0:T(8,128)(2,1)S(1)} %pad_maximum_fusion.refs_0_), channel_id=1, source_target_pairs={{0,8},{1,9},{2,10},{3,11},{4,12},{5,13},{6,14},{7,15},{8,0},{9,1},... | collective-permute-start | bytes 1327112 | tf_op jit(solution)/shard_map/ppermute | solution.py:179
  49.7 0.0 collective-permute-done.12
  49.7 0.5 collective-permute-start.18
  50.2 0.0 collective-permute-done.3
  50.2 1.5 %collective-permute-start.13 = (bf16[192,1152]{1,0:T(8,128)(2,1)S(1)}, bf16[192,1152]{1,0:T(8,128)(2,1)S(1)}, u32[]{:S(2)}, u32[]{:S(2)}) collective-permute-start(bf16[192,1152]{1,0:T(8,128)(2,1)S(1)} %pad_maximum_fusion.1.refs_1_), channel_id=1, source_target_pairs={{0,2},{1,3},{2,0},{3,1},{4,6},{5,7},{6,4},{7,5},{8,10},{9,11},{10,... | collective-permute-start | bytes 1327112 | tf_op jit(solution)/shard_map/ppermute | solution.py:179
  51.7 0.0 collective-permute-done.17.refs_3_
  51.7 0.3 collective-permute-start.4
  52.0 0.0 collective-permute-done.18.refs_4_
  52.0 2.8 %collective-permute-start.19 = (bf16[192,1152]{1,0:T(8,128)(2,1)S(1)}, bf16[192,1152]{1,0:T(8,128)(2,1)S(1)}, u32[]{:S(2)}, u32[]{:S(2)}) collective-permute-start(bf16[192,1152]{1,0:T(8,128)(2,1)S(1)} %constant_dynamic-update-slice_fusion.refs_2_), channel_id=1, source_target_pairs={{0,1},{1,0},{2,3},{3,2},{4,5},{5,4},{6,7},{7,6},{8,9},{9,8},{10,11... | collective-permute-start | bytes 1327112 | tf_op jit(solution)/shard_map/ppermute | solution.py:179
  54.7 5.4 %collective-permute-done.9.refs_0_ = bf16[192,1152]{1,0:T(8,128)(2,1)S(1)} collective-permute-done((bf16[192,1152]{1,0:T(8,128)(2,1)S(1)}, bf16[192,1152]{1,0:T(8,128)(2,1)S(1)}, u32[]{:S(2)}, u32[]{:S(2)}) %collective-permute-start.9) | collective-permute-done | bytes 442400 | tf_op jit(solution)/shard_map/ppermute | solution.py:179
  60.1 0.7 collective-permute-start.14
  60.8 0.0 collective-permute-done.13.refs_1_
  60.8 2.0 %collective-permute-start.15 = (bf16[192,1152]{1,0:T(8,128)(2,1)S(1)}, bf16[192,1152]{1,0:T(8,128)(2,1)S(1)}, u32[]{:S(2)}, u32[]{:S(2)}) collective-permute-start(bf16[192,1152]{1,0:T(8,128)(2,1)S(1)} %collective-permute-done.13.refs_1_), channel_id=1, source_target_pairs={{0,1},{1,0},{2,3},{3,2},{4,5},{5,4},{6,7},{7,6},{8,9},{9,8},{10,11... | collective-permute-start | bytes 1327112 | tf_op jit(solution)/shard_map/ppermute | solution.py:179
  62.8 0.0 collective-permute-done.4.refs_2_
  62.8 2.7 %collective-permute-start.5 = (bf16[192,1152]{1,0:T(8,128)(2,1)S(1)}, bf16[192,1152]{1,0:T(8,128)(2,1)S(1)}, u32[]{:S(2)}, u32[]{:S(2)}) collective-permute-start(bf16[192,1152]{1,0:T(8,128)(2,1)S(1)} %collective-permute-done.4.refs_2_), channel_id=1, source_target_pairs={{0,1},{1,0},{2,3},{3,2},{4,5},{5,4},{6,7},{7,6},{8,9},{9,8},{10,11... | collective-permute-start | bytes 1327112 | tf_op jit(solution)/shard_map/ppermute | solution.py:179
  65.6 0.0 collective-permute-done.19.refs_5_
  65.6 1.7 %shard_map.85 = (bf16[1,2,768,1152]{3,2,1,0:T(8,128)(2,1)}, bf16[1,2,768,1152]{3,2,1,0:T(8,128)(2,1)}, bf16[1,768,1152]{2,1,0:T(8,128)(2,1)}) custom-call(s32[1]{0:T(128)} %bitcast.replica_ref, bf16[192,1152]{1,0:T(8,128)(2,1)S(1)} %pad_maximum_fusion.refs_0_, ...), custom_call_target="tpu_custom_call", output_to_operand_aliasing={{0}: (7, {}), {1}: (8, {})} | custom-call | bytes 5308416 | tf_op jit(solution)/shard_map/pallas_call | solution.py:143
  67.3 0.0 collective-permute-done.16.refs_0_
  67.3 1.2 %shard_map.86 = (bf16[1,2,768,1152]{3,2,1,0:T(8,128)(2,1)}, bf16[1,2,768,1152]{3,2,1,0:T(8,128)(2,1)}, bf16[1,768,1152]{2,1,0:T(8,128)(2,1)}) custom-call(s32[1]{0:T(128)} %bitcast.replica_ref, bf16[2,384,1152]{2,1,0:T(8,128)(2,1)S(1)} %collective-permute-done.16.refs_0_, ...), custom_call_target="tpu_custom_call", output_to_operand_aliasing={{0}: (2, {}), {1}: (3, {}), {2}: (4, {})} | custom-call | tf_op jit(solution)/shard_map/pallas_call | solution.py:143
  68.5 0.0 collective-permute-done.14.refs_3_
  68.6 0.0 collective-permute-done.15.refs_4_
  68.6 1.5 %shard_map.87 = (bf16[1,2,768,1152]{3,2,1,0:T(8,128)(2,1)}, bf16[1,2,768,1152]{3,2,1,0:T(8,128)(2,1)}, bf16[1,768,1152]{2,1,0:T(8,128)(2,1)}) custom-call(s32[1]{0:T(128)} %bitcast.replica_ref, bf16[192,1152]{1,0:T(8,128)(2,1)S(1)} %collective-permute-done.9.refs_0_, ...), custom_call_target="tpu_custom_call", output_to_operand_aliasing={{0}: (6, {}), {1}: (7, {}), {2}: (8, {})} | custom-call | bytes 4423680 | tf_op jit(solution)/shard_map/pallas_call | solution.py:143
  70.1 0.0 collective-permute-done.5.refs_0_
  70.1 0.8 %shard_map.88 = (bf16[1,2,768,1152]{3,2,1,0:T(8,128)(2,1)}, bf16[1,2,768,1152]{3,2,1,0:T(8,128)(2,1)}, bf16[1,768,1152]{2,1,0:T(8,128)(2,1)}) custom-call(s32[1]{0:T(128)} %bitcast.replica_ref, bf16[192,1152]{1,0:T(8,128)(2,1)S(1)} %collective-permute-done.5.refs_0_, ...), custom_call_target="tpu_custom_call", output_to_operand_aliasing={{0}: (2, {}), {1}: (3, {}), {2}: (4, {})} | custom-call | bytes 884736 | tf_op jit(solution)/shard_map/pallas_call | solution.py:143
  (8 shorter events, 0.2 us)
Async XLA Ops:
  0.6 10.7 %copy-start = (bf16[1,1152,1152]{2,1,0:T(8,128)(2,1)S(1)}, bf16[1,1152,1152]{2,1,0:T(8,128)(2,1)}, u32[]{:S(2)}) copy-start(bf16[1,1152,1152]{2,1,0:T(8,128)(2,1)} %w_ref.1) | copy-start | bytes 7962628
  3.2 18.3 %collective-permute-start.6 = (bf16[48,1152]{1,0:T(8,128)(2,1)S(1)}, bf16[48,1152]{1,0:T(8,128)(2,1)S(1)}, u32[]{:S(2)}, u32[]{:S(2)}) collective-permute-start(bf16[48,1152]{1,0:T(8,128)(2,1)S(1)} %get-tuple-element.33), channel_id=1, source_target_pairs={{0,24},{1,25},{2,26},{3,27},{4,28},{5,29},{6,30},{7,31},{8,16},{9,... | collective-permute-start | bytes 331784 | tf_op jit(solution)/shard_map/ppermute | solution.py:179
  8.5 13.0 %collective-permute-start = (bf16[48,1152]{1,0:T(8,128)(2,1)S(1)}, bf16[48,1152]{1,0:T(8,128)(2,1)S(1)}, u32[]{:S(2)}, u32[]{:S(2)}) collective-permute-start(bf16[48,1152]{1,0:T(8,128)(2,1)S(1)} %get-tuple-element.34), channel_id=1, source_target_pairs={{0,40},{1,41},{2,42},{3,43},{4,44},{5,45},{6,46},{7,47},{8,32},{9,... | collective-permute-start | bytes 331784 | tf_op jit(solution)/shard_map/ppermute | solution.py:179
  13.3 10.2 %collective-permute-start.10 = (bf16[48,1152]{1,0:T(8,128)(2,1)S(1)}, bf16[48,1152]{1,0:T(8,128)(2,1)S(1)}, u32[]{:S(2)}, u32[]{:S(2)}) collective-permute-start(bf16[48,1152]{1,0:T(8,128)(2,1)S(1)} %get-tuple-element.18), channel_id=1, source_target_pairs={{32,8},{33,9},{34,10},{35,11},{36,12},{37,13},{38,14},{39,15},{40,... | collective-permute-start | bytes 331784 | tf_op jit(solution)/shard_map/ppermute | solution.py:179
  13.8 7.7 %copy-start.1 = (bf16[1,1152,1152]{2,1,0:T(8,128)(2,1)S(1)}, bf16[1,1152,1152]{2,1,0:T(8,128)(2,1)}, u32[]{:S(2)}) copy-start(bf16[1,1152,1152]{2,1,0:T(8,128)(2,1)} %w_ref.1) | copy-start | bytes 7962628
  19.9 47.4 %collective-permute-start.16 = (bf16[2,384,1152]{2,1,0:T(8,128)(2,1)}, bf16[2,384,1152]{2,1,0:T(8,128)(2,1)S(1)}, u32[]{:S(2)}, u32[]{:S(2)}) collective-permute-start(bf16[2,384,1152]{2,1,0:T(8,128)(2,1)} %get-tuple-element.19), channel_id=1, source_target_pairs={{0,1},{1,0},{2,3},{3,2},{4,5},{5,4},{6,7},{7,6},{8,9},{9,8},{10,11... | collective-permute-start | bytes 5308424 | tf_op jit(solution)/shard_map/ppermute | solution.py:179
  22.1 7.7 %collective-permute-start.7 = (bf16[48,1152]{1,0:T(8,128)(2,1)S(1)}, bf16[48,1152]{1,0:T(8,128)(2,1)S(1)}, u32[]{:S(2)}, u32[]{:S(2)}) collective-permute-start(bf16[48,1152]{1,0:T(8,128)(2,1)S(1)} %fusion.16), channel_id=1, source_target_pairs={{0,2},{1,3},{2,0},{3,1},{4,6},{5,7},{6,4},{7,5},{8,10},{9,11},{10,... | collective-permute-start | bytes 331784 | tf_op jit(solution)/shard_map/ppermute | solution.py:179
  24.4 6.0 %collective-permute-start.11 = (bf16[48,1152]{1,0:T(8,128)(2,1)S(1)}, bf16[48,1152]{1,0:T(8,128)(2,1)S(1)}, u32[]{:S(2)}, u32[]{:S(2)}) collective-permute-start(bf16[48,1152]{1,0:T(8,128)(2,1)S(1)} %fusion.27), channel_id=1, source_target_pairs={{0,6},{1,7},{2,4},{3,5},{4,2},{5,3},{6,0},{7,1},{8,14},{9,15},{10,... | collective-permute-start | bytes 331784 | tf_op jit(solution)/shard_map/ppermute | solution.py:179
  27.8 7.5 %collective-permute-start.1 = (bf16[48,1152]{1,0:T(8,128)(2,1)S(1)}, bf16[48,1152]{1,0:T(8,128)(2,1)S(1)}, u32[]{:S(2)}, u32[]{:S(2)}) collective-permute-start(bf16[48,1152]{1,0:T(8,128)(2,1)S(1)} %fusion.22), channel_id=1, source_target_pairs={{0,16},{1,17},{2,18},{3,19},{4,20},{5,21},{6,22},{7,23},{8,24},{9,... | collective-permute-start | bytes 331784 | tf_op jit(solution)/shard_map/ppermute | solution.py:179
  29.8 15.6 %collective-permute-start.8 = (bf16[96,1152]{1,0:T(8,128)(2,1)S(1)}, bf16[96,1152]{1,0:T(8,128)(2,1)S(1)}, u32[]{:S(2)}, u32[]{:S(2)}) collective-permute-start(bf16[96,1152]{1,0:T(8,128)(2,1)S(1)} %pad_maximum_fusion.3), channel_id=1, source_target_pairs={{0,6},{1,7},{2,4},{3,5},{4,2},{5,3},{6,0},{7,1},{8,14},{9,15},{10,... | collective-permute-start | bytes 663560 | tf_op jit(solution)/shard_map/ppermute | solution.py:179
  30.5 19.2 %collective-permute-start.12 = (bf16[96,1152]{1,0:T(8,128)(2,1)S(1)}, bf16[96,1152]{1,0:T(8,128)(2,1)S(1)}, u32[]{:S(2)}, u32[]{:S(2)}) collective-permute-start(bf16[96,1152]{1,0:T(8,128)(2,1)S(1)} %pad_maximum_fusion.4), channel_id=1, source_target_pairs={{0,8},{1,9},{2,10},{3,11},{4,12},{5,13},{6,14},{7,15},{8,0},{9,1},... | collective-permute-start | bytes 663560 | tf_op jit(solution)/shard_map/ppermute | solution.py:179
  35.4 9.8 %collective-permute-start.2 = (bf16[48,1152]{1,0:T(8,128)(2,1)S(1)}, bf16[48,1152]{1,0:T(8,128)(2,1)S(1)}, u32[]{:S(2)}, u32[]{:S(2)}) collective-permute-start(bf16[48,1152]{1,0:T(8,128)(2,1)S(1)} %collective-permute-done.1), channel_id=1, source_target_pairs={{0,8},{1,9},{2,10},{3,11},{4,12},{5,13},{6,14},{7,15},{8,0},{9,1},... | collective-permute-start | bytes 331784 | tf_op jit(solution)/shard_map/ppermute | solution.py:179
  45.2 5.0 %collective-permute-start.3 = (bf16[96,1152]{1,0:T(8,128)(2,1)S(1)}, bf16[96,1152]{1,0:T(8,128)(2,1)S(1)}, u32[]{:S(2)}, u32[]{:S(2)}) collective-permute-start(bf16[96,1152]{1,0:T(8,128)(2,1)S(1)} %pad_maximum_fusion.2), channel_id=1, source_target_pairs={{0,2},{1,3},{2,0},{3,1},{4,6},{5,7},{6,4},{7,5},{8,10},{9,11},{10,... | collective-permute-start | bytes 663560 | tf_op jit(solution)/shard_map/ppermute | solution.py:179
  45.4 6.2 %collective-permute-start.17 = (bf16[192,1152]{1,0:T(8,128)(2,1)S(1)}, bf16[192,1152]{1,0:T(8,128)(2,1)S(1)}, u32[]{:S(2)}, u32[]{:S(2)}) collective-permute-start(bf16[192,1152]{1,0:T(8,128)(2,1)S(1)} %pad_maximum_fusion.refs_0_), channel_id=1, source_target_pairs={{0,1},{1,0},{2,3},{3,2},{4,5},{5,4},{6,7},{7,6},{8,9},{9,8},{10,11... | collective-permute-start | bytes 1327112 | tf_op jit(solution)/shard_map/ppermute | solution.py:179
  48.0 12.2 %collective-permute-start.9 = (bf16[192,1152]{1,0:T(8,128)(2,1)S(1)}, bf16[192,1152]{1,0:T(8,128)(2,1)S(1)}, u32[]{:S(2)}, u32[]{:S(2)}) collective-permute-start(bf16[192,1152]{1,0:T(8,128)(2,1)S(1)} %pad_maximum_fusion.refs_0_), channel_id=1, source_target_pairs={{0,8},{1,9},{2,10},{3,11},{4,12},{5,13},{6,14},{7,15},{8,0},{9,1},... | collective-permute-start | bytes 1327112 | tf_op jit(solution)/shard_map/ppermute | solution.py:179
  49.7 2.2 %collective-permute-start.18 = (bf16[192,1152]{1,0:T(8,128)(2,1)S(1)}, bf16[192,1152]{1,0:T(8,128)(2,1)S(1)}, u32[]{:S(2)}, u32[]{:S(2)}) collective-permute-start(bf16[192,1152]{1,0:T(8,128)(2,1)S(1)} %pad_maximum_fusion.1.refs_1_), channel_id=1, source_target_pairs={{0,1},{1,0},{2,3},{3,2},{4,5},{5,4},{6,7},{7,6},{8,9},{9,8},{10,11... | collective-permute-start | bytes 1327112 | tf_op jit(solution)/shard_map/ppermute | solution.py:179
  50.2 10.6 %collective-permute-start.13 = (bf16[192,1152]{1,0:T(8,128)(2,1)S(1)}, bf16[192,1152]{1,0:T(8,128)(2,1)S(1)}, u32[]{:S(2)}, u32[]{:S(2)}) collective-permute-start(bf16[192,1152]{1,0:T(8,128)(2,1)S(1)} %pad_maximum_fusion.1.refs_1_), channel_id=1, source_target_pairs={{0,2},{1,3},{2,0},{3,1},{4,6},{5,7},{6,4},{7,5},{8,10},{9,11},{10,... | collective-permute-start | bytes 1327112 | tf_op jit(solution)/shard_map/ppermute | solution.py:179
  51.7 11.1 %collective-permute-start.4 = (bf16[192,1152]{1,0:T(8,128)(2,1)S(1)}, bf16[192,1152]{1,0:T(8,128)(2,1)S(1)}, u32[]{:S(2)}, u32[]{:S(2)}) collective-permute-start(bf16[192,1152]{1,0:T(8,128)(2,1)S(1)} %constant_dynamic-update-slice_fusion.refs_2_), channel_id=1, source_target_pairs={{0,6},{1,7},{2,4},{3,5},{4,2},{5,3},{6,0},{7,1},{8,14},{9,15},{10,... | collective-permute-start | bytes 1327112 | tf_op jit(solution)/shard_map/ppermute | solution.py:179
  52.0 13.6 %collective-permute-start.19 = (bf16[192,1152]{1,0:T(8,128)(2,1)S(1)}, bf16[192,1152]{1,0:T(8,128)(2,1)S(1)}, u32[]{:S(2)}, u32[]{:S(2)}) collective-permute-start(bf16[192,1152]{1,0:T(8,128)(2,1)S(1)} %constant_dynamic-update-slice_fusion.refs_2_), channel_id=1, source_target_pairs={{0,1},{1,0},{2,3},{3,2},{4,5},{5,4},{6,7},{7,6},{8,9},{9,8},{10,11... | collective-permute-start | bytes 1327112 | tf_op jit(solution)/shard_map/ppermute | solution.py:179
  60.1 8.4 %collective-permute-start.14 = (bf16[192,1152]{1,0:T(8,128)(2,1)S(1)}, bf16[192,1152]{1,0:T(8,128)(2,1)S(1)}, u32[]{:S(2)}, u32[]{:S(2)}) collective-permute-start(bf16[192,1152]{1,0:T(8,128)(2,1)S(1)} %collective-permute-done.9.refs_0_), channel_id=1, source_target_pairs={{0,1},{1,0},{2,3},{3,2},{4,5},{5,4},{6,7},{7,6},{8,9},{9,8},{10,11... | collective-permute-start | bytes 1327112 | tf_op jit(solution)/shard_map/ppermute | solution.py:179
  60.8 7.7 %collective-permute-start.15 = (bf16[192,1152]{1,0:T(8,128)(2,1)S(1)}, bf16[192,1152]{1,0:T(8,128)(2,1)S(1)}, u32[]{:S(2)}, u32[]{:S(2)}) collective-permute-start(bf16[192,1152]{1,0:T(8,128)(2,1)S(1)} %collective-permute-done.13.refs_1_), channel_id=1, source_target_pairs={{0,1},{1,0},{2,3},{3,2},{4,5},{5,4},{6,7},{7,6},{8,9},{9,8},{10,11... | collective-permute-start | bytes 1327112 | tf_op jit(solution)/shard_map/ppermute | solution.py:179
  62.8 7.3 %collective-permute-start.5 = (bf16[192,1152]{1,0:T(8,128)(2,1)S(1)}, bf16[192,1152]{1,0:T(8,128)(2,1)S(1)}, u32[]{:S(2)}, u32[]{:S(2)}) collective-permute-start(bf16[192,1152]{1,0:T(8,128)(2,1)S(1)} %collective-permute-done.4.refs_2_), channel_id=1, source_target_pairs={{0,1},{1,0},{2,3},{3,2},{4,5},{5,4},{6,7},{7,6},{8,9},{9,8},{10,11... | collective-permute-start | bytes 1327112 | tf_op jit(solution)/shard_map/ppermute | solution.py:179
